TPU v7x, 32 devices: a whole 2x2x4 slice. The times are simulated.
32 devices in a mesh: seq: 8 (over z, y), mp: 4 (over x, core).
Axes of the slice: x: 2, y: 2, z: 4, core: 2. Of those that a mesh axis runs over, the one named last changes fastest.
Arguments:
- hidden_entry_states: bfloat16 [1024, 512], P('seq'), may hold values from -6 to 6
- base_ids: int32 [1024], P('seq'), may hold values from 0 to 4
- mask_index: int32 [128], P('seq'), may hold values from 0 to 1023, as said below
- first_kernel: bfloat16 [9, 512, 512], P(None, None, 'mp'), may hold values from -0.09375 to 0.09375
- second_kernel: bfloat16 [9, 512, 512], P(None, None, 'mp'), may hold values from -0.09375 to 0.09375
- head_weight: bfloat16 [512, 5], replicated, may hold values from -0.5 to 0.5
Outputs:
- input_grad: bfloat16 [1024, 512], P('seq')
- first_kernel_gradient: float32 [9, 512, 512], P(None, 'seq', 'mp')
- second_kernel_gradient: float32 [9, 512, 512], P(None, 'seq', 'mp')
Inputs may be any that keep to these rules, and one draw needn't show every extreme that they name: `mask_index`: each device's 16 entries are distinct positions within its own block of 128 bases, in no particular order.
All inputs are finite; a program needn't handle non-finite values.
Results may differ from a plain program's by a relative error of at most 0.014.
Values may be sent and summed in bfloat16 or wider, within the bound.
No kernel may reach another device: no remote copies, remote signals or barrier semaphores. Data moves between devices by JAX's collectives and lax.ppermute only.
A program may use at most 64 MiB of HBM per device.

v0:
```python
import functools

import jax
import jax.numpy as jnp
from jax import lax
from jax.experimental import pallas as pl
from jax.experimental.pallas import tpu as pltpu
from jax.sharding import PartitionSpec as P

DILATION_FIRST1 = 2048
DILATION_SECOND2 = 4096


epsilon = 1e-05
root_half = 0.7071067811865476
inv_root_two_pi = 0.3989422804014327
ROW_CHUNK = 32
SIDE_ROWS = 16
VMEM_LIMIT = 24 * 1024 * 1024


def gelu_parts(conv_out):
    normal_cdf = 0.5 * (1.0 + lax.erf(conv_out * root_half))
    gelu_slope = normal_cdf + conv_out * inv_root_two_pi * jnp.exp(-0.5 * conv_out * conv_out)
    return (conv_out * normal_cdf, gelu_slope)


def norm_parts(activation):
    values = activation.astype(jnp.float32)
    centre = jnp.mean(values, axis=-1, keepdims=True)
    centred = values - centre
    spread = jnp.mean(centred * centred, axis=-1, keepdims=True)
    inverse = lax.rsqrt(spread + epsilon)
    return (centred * inverse, inverse)


def active_hops(tap_count, dilation_blocks, seq_count):
    centre_tap = tap_count // 2
    hops = [(tap, dilation_blocks * (tap - centre_tap)) for tap in range(tap_count)]
    return [(tap, hop) for tap, hop in hops if abs(hop) < seq_count]


def shifted(x, axis, by):
    if by == 0:
        return x
    peers = lax.axis_size(axis)
    pairs = [(i, i + by) for i in range(peers) if 0 <= i + by < peers]
    return lax.ppermute(x, axis, pairs)


def loss_grad(hidden_top, targets, head_weight):
    logits = lax.dot_general(
        head_weight, hidden_top, (((0,), (1,)), ((), ())), preferred_element_type=jnp.float32
    )
    exponent = jnp.exp(logits)
    probability = exponent / jnp.sum(exponent, axis=0, keepdims=True)
    vocab_rows = lax.broadcasted_iota(jnp.int32, logits.shape, 0)
    onehot = (vocab_rows == targets[None, :]).astype(jnp.float32)
    weight = (targets >= 0).astype(jnp.float32)[None, :]
    dlogits = weight * (probability - onehot)
    return lax.dot_general(
        dlogits,
        head_weight.astype(jnp.float32),
        (((0,), (1,)), ((), ())),
        precision=lax.Precision.HIGHEST,
    )


def general_plan(hidden_entry_states, base_ids, mask_index, first_kernel, second_kernel, head_weight, first_hops, second_hops):
    seq_count = lax.axis_size("seq")
    rows_per_block, channels = hidden_entry_states.shape
    tap_count, _, own_width = first_kernel.shape
    mask_count = mask_index.shape[0]
    offsets = mask_index - lax.axis_index("seq") * rows_per_block
    positions = lax.broadcasted_iota(jnp.int32, (rows_per_block, mask_count), 0)
    masked = jnp.any(positions == offsets[None, :], axis=1)
    targets = jnp.where(masked, base_ids, -1)

    def used(kernel, hops):
        first_tap, last_tap = hops[0][0], hops[-1][0]
        return kernel[first_tap : last_tap + 1]

    def block_forward_pass(source, kernel, hops):
        stacked = jnp.concatenate([shifted(source, "seq", -hop) for _, hop in hops], axis=1)
        conv_out = jnp.dot(
            stacked,
            used(kernel, hops).reshape(len(hops) * channels, own_width),
            preferred_element_type=jnp.float32,
        )
        activation, gelu_slope = gelu_parts(conv_out)
        mixed_all = lax.all_gather(activation.astype(jnp.bfloat16), "mp", axis=1, tiled=True)
        normed, inverse = norm_parts(mixed_all)
        result = (source.astype(jnp.float32) + normed).astype(jnp.bfloat16)
        return (result, (source, normed, inverse, gelu_slope))

    def block_backward_pass(grad_out, saved, kernel, hops):
        source, normed, inverse, gelu_slope = saved
        mean_grad = jnp.mean(grad_out, axis=-1, keepdims=True)
        mean_cross = jnp.mean(grad_out * normed, axis=-1, keepdims=True)
        grad_act = inverse * (grad_out - mean_grad - normed * mean_cross)
        own_cols = lax.dynamic_slice_in_dim(
            grad_act, lax.axis_index("mp") * own_width, own_width, 1
        )
        grad_conv = (own_cols * gelu_slope).astype(jnp.bfloat16)
        tap_stack = jnp.stack([shifted(grad_conv, "seq", hop) for _, hop in hops], axis=0)
        input_part = jnp.einsum(
            "kro,kdo->rd", tap_stack, used(kernel, hops), preferred_element_type=jnp.float32
        )
        grad_in = grad_out + lax.psum(input_part.astype(jnp.bfloat16), "mp").astype(jnp.float32)
        kernel_part = jnp.einsum(
            "rd,kro->kdo", source, tap_stack, preferred_element_type=jnp.float32
        )
        by_owner = kernel_part.reshape(len(hops), seq_count, channels // seq_count, own_width)
        received = lax.all_to_all(
            by_owner.astype(jnp.bfloat16), "seq", split_axis=1, concat_axis=1, tiled=True
        ).astype(by_owner.dtype)
        first_tap, last_tap = hops[0][0], hops[-1][0]
        kernel_grad = jnp.pad(
            jnp.sum(received, axis=1),
            ((first_tap, tap_count - 1 - last_tap), (0, 0), (0, 0)),
        )
        return (grad_in, kernel_grad)

    hidden_one, saved_one = block_forward_pass(hidden_entry_states, first_kernel, first_hops)
    hidden_two, saved_two = block_forward_pass(hidden_one, second_kernel, second_hops)
    grad_two = loss_grad(hidden_two, targets, head_weight)
    grad_one, second_grad = block_backward_pass(grad_two, saved_two, second_kernel, second_hops)
    grad_zero, first_grad = block_backward_pass(grad_one, saved_one, first_kernel, first_hops)
    return (grad_zero.astype(jnp.bfloat16), first_grad, second_grad)


NN = (((1,), (0,)), ((), ()))
NT = (((1,), (1,)), ((), ()))
TN = (((0,), (0,)), ((), ()))


def dot(a, b, dims=NN):
    return lax.dot_general(a, b, dims, preferred_element_type=jnp.float32)


def swap(block, axis, offset):
    return lax.ppermute(block, axis, [(i, i ^ offset) for i in range(lax.axis_size(axis))])


def block_at(me, offset, width):
    return pl.ds(pl.multiple_of((me ^ offset) * width, width), width)


def own_order(me, ref, rows, count):
    width = ref.shape[1] // count
    return jnp.concatenate([ref[rows, block_at(me, o, width)] for o in range(count)], axis=1)


def matrices_body(centre_tap, first_ref, second_ref, both_ref, sems):
    copies = [
        pltpu.make_async_copy(ref.at[centre_tap], both_ref.at[slot], sems.at[slot])
        for slot, ref in enumerate((first_ref, second_ref))
    ]
    for copy in copies:
        copy.start()
    for copy in copies:
        copy.wait()


def rows_body(where_ref, mask_ref, ids_ref, source_ref, rows_ref, mask_at, ids_at, sems):
    rows = source_ref.shape[0]
    copies = [
        pltpu.make_async_copy(mask_ref, mask_at, sems.at[0]),
        pltpu.make_async_copy(ids_ref, ids_at, sems.at[1]),
        pltpu.make_async_copy(source_ref, rows_ref.at[pl.ds(0, rows)], sems.at[2]),
    ]
    for copy in copies:
        copy.start()
    copies[0].wait()
    copies[1].wait()
    positions = lax.broadcasted_iota(jnp.int32, ids_at.shape, 1) + where_ref[1] * rows
    masked = jnp.zeros(ids_at.shape, jnp.int32)
    for entry in range(mask_at.shape[0]):
        masked = jnp.where(positions == mask_at[entry], 1, masked)
    targets = jnp.where(masked == 1, ids_at[...], -1).astype(jnp.float32)
    extra = rows_ref.shape[0] - rows
    rows_ref[rows:, :] = jnp.zeros((extra, rows_ref.shape[1]), jnp.bfloat16)
    rows_ref[rows:, 0:rows] = jnp.broadcast_to(targets, (extra, rows)).astype(jnp.bfloat16)
    copies[2].wait()


def blank_body(first_ref, second_ref):
    first_ref[...] = jnp.zeros_like(first_ref)
    second_ref[...] = jnp.zeros_like(second_ref)


def stacked(blocks, axis):
    return blocks[0] if len(blocks) == 1 else jnp.concatenate(blocks, axis=axis)


def columns_of(me, matrix_refs, slot, count):
    width = matrix_refs[0].shape[2]
    return stacked(
        [
            stacked([ref[slot, block_at(me, o, width), :] for o in range(count)], 0)
            for ref in matrix_refs
        ],
        1,
    )


def early_body(count, where_ref, own_ref, peer_ref, head_ref, *refs):
    matrix_refs = refs[:-4]
    activation_ref, slope_ref, flip_ref, head_out_ref = refs[-4:]
    me = where_ref[0]
    half = activation_ref.shape[0] // 2
    weights = columns_of(me, matrix_refs, 0, count)
    for part, ref in enumerate((own_ref, peer_ref)):
        conv_out = dot(own_order(me, ref, pl.ds(0, half), count), weights)
        for start in range(0, half, ROW_CHUNK):
            rows = pl.ds(part * half + start, ROW_CHUNK)
            activation, gelu_slope = gelu_parts(conv_out[start : start + ROW_CHUNK])
            activation_ref[rows, :] = activation.astype(jnp.bfloat16)
            slope_ref[rows, :] = gelu_slope
        flip_ref[:, pl.ds(part * half, half)] = ref[pl.ds(0, half), :].T
    head_out_ref[...] = jnp.zeros_like(head_out_ref)
    classes = head_ref.shape[0]
    head_out_ref[0:classes, :] = own_order(me, head_ref, pl.ds(0, classes), count)


def main_body(count, sent_count, classes, where_ref, own_ref, peer_ref, activation_ref, slope_ref, source_flip_ref, head_ref, *refs):
    matrix_refs, refs = refs[:count], refs[count:]
    self_ref, sent_refs, refs = refs[0], refs[1 : 1 + sent_count], refs[1 + sent_count :]
    grad_out_ref, grad_conv_out_ref = refs[:2]
    hidden_one_ref, normed_one_ref, scale_one_ref, hidden_flip_ref, normed_two_ref, scale_two_ref, hidden_two_ref, grad_ref, grad_conv_ref = refs[2:]
    me, block = where_ref[0], where_ref[1]
    total_rows = grad_ref.shape[0]
    half = total_rows // 2
    width = self_ref.shape[2]
    depth = self_ref.shape[1]
    halves = (0, half)

    late = columns_of(me, matrix_refs[-1:], 0, count)
    for start, ref in zip(halves, (own_ref, peer_ref)):
        conv_out = dot(own_order(me, ref, pl.ds(0, half), count), late)
        for inner in range(0, half, ROW_CHUNK):
            rows = pl.ds(start + inner, ROW_CHUNK)
            activation, gelu_slope = gelu_parts(conv_out[inner : inner + ROW_CHUNK])
            normed, inverse = norm_parts(
                jnp.concatenate([activation_ref[rows, :], activation.astype(jnp.bfloat16)], axis=1)
            )
            scale_one_ref[rows, :] = jnp.concatenate([slope_ref[rows, :], gelu_slope], axis=1) * inverse
            normed_one_ref[rows, :] = normed
            source = own_order(me, ref, pl.ds(inner, ROW_CHUNK), count)
            hidden_one_ref[rows, :] = (source.astype(jnp.float32) + normed).astype(jnp.bfloat16)

    weights = columns_of(me, matrix_refs, 1, count)
    for start in halves:
        conv_out = dot(hidden_one_ref[pl.ds(start, half), :], weights)
        for inner in range(0, half, ROW_CHUNK):
            rows = pl.ds(start + inner, ROW_CHUNK)
            activation, gelu_slope = gelu_parts(conv_out[inner : inner + ROW_CHUNK])
            normed, inverse = norm_parts(activation.astype(jnp.bfloat16))
            scale_two_ref[rows, :] = gelu_slope * inverse
            normed_two_ref[rows, :] = normed
            hidden_two_ref[rows, :] = (hidden_one_ref[rows, :].astype(jnp.float32) + normed).astype(jnp.bfloat16)

    for offset in range(count):
        flipped = hidden_one_ref[:, pl.ds(offset * width, width)].T
        hidden_flip_ref[block_at(me, offset, width), :] = flipped

    head = head_ref[...]
    logits = dot(head, hidden_two_ref[...], NT)
    class_rows = lax.broadcasted_iota(jnp.int32, logits.shape, 0)
    exponent = jnp.where(class_rows < classes, jnp.exp(logits), 0.0)
    probability = exponent / jnp.sum(exponent, axis=0, keepdims=True)
    targets = jnp.concatenate(
        [ref[half : half + head.shape[0], 0:half] for ref in (own_ref, peer_ref)], axis=1
    ).astype(jnp.float32)
    onehot = (class_rows.astype(jnp.float32) == targets).astype(jnp.float32)
    weight = (targets >= 0.0).astype(jnp.float32)
    rest = jnp.where(class_rows < classes, weight * (probability - onehot), 0.0)
    terms = []
    for _ in range(3):
        term = rest.astype(jnp.bfloat16)
        terms.append(term)
        rest = rest - term.astype(jnp.float32)
    grad_ref[...] = dot(jnp.concatenate(terms, axis=0), jnp.concatenate([head] * 3, axis=0), TN)

    def norm_backward(normed_ref, scale_ref):
        for start in range(0, total_rows, ROW_CHUNK):
            rows = pl.ds(start, ROW_CHUNK)
            grad_out, normed = grad_ref[rows, :], normed_ref[rows, :]
            mean_grad = jnp.mean(grad_out, axis=-1, keepdims=True)
            mean_cross = jnp.mean(grad_out * normed, axis=-1, keepdims=True)
            grad_conv_ref[rows, :] = (
                (grad_out - mean_grad - normed * mean_cross) * scale_ref[rows, :]
            ).astype(jnp.bfloat16)

    def kernel_parts(flip_ref, slot):
        sources = [
            flip_ref[pl.ds(pl.multiple_of((block ^ (2 * j)) * depth, depth), depth), :]
            for j in range(1 + sent_count)
        ]
        part = dot(stacked(sources, 0), grad_conv_ref[:, 0:width])
        self_ref[slot] = part[0:depth]
        for j, ref in enumerate(sent_refs):
            ref[slot] = part[(j + 1) * depth : (j + 2) * depth].astype(jnp.bfloat16)

    norm_backward(normed_two_ref, scale_two_ref)
    for start in halves:
        rows = pl.ds(start, half)
        grad_ref[rows, :] += dot(grad_conv_ref[rows, :], weights, NT)
    kernel_parts(hidden_flip_ref, 1)
    norm_backward(normed_one_ref, scale_one_ref)
    kernel_parts(source_flip_ref, 0)
    grad_out_ref[...] = grad_ref[pl.ds(0, half), :]
    grad_conv_out_ref[...] = grad_conv_ref[pl.ds(0, half), :]


def input_grad_body(count, where_ref, grad_ref, grad_conv_ref, *refs):
    matrix_refs, input_grad_ref = refs[:count], refs[count]
    me = where_ref[0]
    width = matrix_refs[0].shape[2]
    total = grad_ref[...] + dot(grad_conv_ref[...], columns_of(me, matrix_refs, 0, count), NT)
    for offset in range(count):
        input_grad_ref[:, block_at(me, offset, width)] = total[
            :, offset * width : (offset + 1) * width
        ].astype(jnp.bfloat16)


def total_body(centre_tap, first_in_ref, second_in_ref, self_ref, *refs):
    received = refs[:-4]
    first_ref, second_ref, sum_ref, sems = refs[-4:]
    sum_ref[...] = self_ref[...] + sum(ref[...].astype(jnp.float32) for ref in received)
    copies = [
        pltpu.make_async_copy(sum_ref.at[slot], ref.at[centre_tap], sems.at[slot])
        for slot, ref in enumerate((first_ref, second_ref))
    ]
    for copy in copies:
        copy.start()
    for copy in copies:
        copy.wait()


def local_plan(hidden_entry_states, base_ids, mask_index, first_kernel, second_kernel, head_weight):
    seq_count = lax.axis_size("seq")
    mp_count = lax.axis_size("mp")
    rows, channels = hidden_entry_states.shape
    tap_count, _, width = first_kernel.shape
    classes = head_weight.shape[1]
    centre_tap = tap_count // 2
    depth = channels // seq_count
    where = jnp.stack([lax.axis_index("mp"), lax.axis_index("seq")]).astype(jnp.int32)

    vmem = pl.BlockSpec(memory_space=pltpu.VMEM)
    smem = pl.BlockSpec(memory_space=pltpu.SMEM)
    hbm = pl.BlockSpec(memory_space=pltpu.HBM)

    def shape(dims, dtype=jnp.bfloat16):
        return jax.ShapeDtypeStruct(dims, dtype)

    def in_hbm(array):
        return pltpu.with_memory_space_constraint(array, pltpu.HBM)

    def call(body, in_specs, out_shape, out_specs=None, scratch=(), aliases={}, flops=0, moved=0):
        return pl.pallas_call(
            body,
            out_shape=out_shape,
            in_specs=in_specs,
            out_specs=(vmem,) * len(out_shape) if out_specs is None else out_specs,
            scratch_shapes=list(scratch),
            input_output_aliases=aliases,
            compiler_params=pltpu.CompilerParams(vmem_limit_bytes=VMEM_LIMIT),
            cost_estimate=pl.CostEstimate(flops=flops, bytes_accessed=moved, transcendentals=0),
        )

    (own,) = call(
        functools.partial(matrices_body, centre_tap),
        [hbm] * 2,
        (shape((2, channels, width)),),
        scratch=[pltpu.SemaphoreType.DMA((2,))],
    )(in_hbm(first_kernel), in_hbm(second_kernel))
    blocks = {0: own}
    bit = mp_count // 2
    while bit:
        for offset in list(blocks):
            blocks[offset ^ bit] = swap(blocks[offset], "mp", bit)
        bit //= 2
    blocks = [blocks[offset] for offset in range(mp_count)]

    (own_rows,) = call(
        rows_body,
        [smem] + [hbm] * 3,
        (shape((rows + SIDE_ROWS, channels)),),
        scratch=[
            pltpu.SMEM(mask_index.shape, jnp.int32),
            pltpu.VMEM((1, rows), jnp.int32),
            pltpu.SemaphoreType.DMA((3,)),
        ],
    )(where, in_hbm(mask_index), in_hbm(base_ids[None, :]), in_hbm(hidden_entry_states))
    peer_rows = swap(own_rows, "seq", 1)
    whole = shape((tap_count, depth, width), jnp.float32)
    first_grad, second_grad = call(blank_body, [], (whole, whole))()

    pair_rows = 2 * rows
    early = channels - width
    product = 2 * pair_rows * channels * channels
    activation, slope, source_flip, head = call(
        functools.partial(early_body, mp_count),
        [smem] + [vmem] * (2 + mp_count),
        (
            shape((pair_rows, early)),
            shape((pair_rows, early), jnp.float32),
            shape((channels, pair_rows)),
            shape((SIDE_ROWS, channels)),
        ),
        flops=product,
        moved=8 * pair_rows * channels,
    )(where, own_rows, peer_rows, head_weight.T, *blocks[:-1])

    sent_count = seq_count // 2 - 1
    part = (2, depth, width)
    outs = call(
        functools.partial(main_body, mp_count, sent_count, classes),
        [smem] + [vmem] * (6 + mp_count),
        (shape(part, jnp.float32),)
        + (shape(part),) * sent_count
        + (shape((rows, channels), jnp.float32), shape((rows, channels))),
        scratch=[
            pltpu.VMEM((pair_rows, channels), jnp.bfloat16),
            pltpu.VMEM((pair_rows, channels), jnp.float32),
            pltpu.VMEM((pair_rows, channels), jnp.float32),
            pltpu.VMEM((channels, pair_rows), jnp.bfloat16),
            pltpu.VMEM((pair_rows, channels), jnp.float32),
            pltpu.VMEM((pair_rows, channels), jnp.float32),
            pltpu.VMEM((pair_rows, channels), jnp.bfloat16),
            pltpu.VMEM((pair_rows, channels), jnp.float32),
            pltpu.VMEM((pair_rows, channels), jnp.bfloat16),
        ],
        flops=3 * product,
        moved=16 * pair_rows * channels,
    )(where, own_rows, peer_rows, activation, slope, source_flip, head, *blocks)
    own_part, sent, (grad_one, grad_conv) = outs[0], outs[1:-2], outs[-2:]

    received = [swap(piece, "seq", 2 * (j + 1)) for j, piece in enumerate(sent)]
    (input_grad,) = call(
        functools.partial(input_grad_body, mp_count),
        [smem] + [vmem] * (2 + mp_count),
        (shape((rows, channels)),),
        flops=product // 2,
        moved=8 * rows * channels,
    )(where, grad_one, grad_conv, *blocks)
    first_grad, second_grad = call(
        functools.partial(total_body, centre_tap),
        [hbm, hbm] + [vmem] * (1 + sent_count),
        (whole, whole),
        out_specs=(hbm, hbm),
        scratch=[pltpu.VMEM(part, jnp.float32), pltpu.SemaphoreType.DMA((2,))],
        aliases={0: 0, 1: 1},
    )(first_grad, second_grad, own_part, *received)
    return (input_grad, first_grad, second_grad)


def power_of_two(count):
    return count & (count - 1) == 0


def local(hidden_entry_states, base_ids, mask_index, first_kernel, second_kernel, head_weight):
    rows, channels = hidden_entry_states.shape
    tap_count, _, width = first_kernel.shape
    seq_count = lax.axis_size("seq")
    mp_count = lax.axis_size("mp")
    first_hops = active_hops(tap_count, DILATION_FIRST1 // rows, seq_count)
    second_hops = active_hops(tap_count, DILATION_SECOND2 // rows, seq_count)
    args = (hidden_entry_states, base_ids, mask_index, first_kernel, second_kernel, head_weight)
    fits = (
        power_of_two(mp_count)
        and power_of_two(seq_count)
        and mp_count > 1
        and seq_count > 1
        and width % 128 == 0
        and rows % 128 == 0
        and rows <= channels
        and (channels // seq_count) % 16 == 0
        and head_weight.shape[1] <= SIDE_ROWS
    )
    if len(first_hops) == 1 and len(second_hops) == 1 and fits:
        return local_plan(*args)
    return general_plan(*args, first_hops, second_hops)


def solution(mesh):
    placed = (P("seq", None), P("seq"), P("seq"), P(None, None, "mp"), P(None, None, "mp"), P())
    return jax.shard_map(
        local,
        mesh=mesh,
        in_specs=placed,
        out_specs=(P("seq", None), P(None, "seq", "mp"), P(None, "seq", "mp")),
        check_vma=False,
    )
```

profile of v0, /device:TPU:0, one launch (start us, length us, event | category | flops | bytes accessed | tf_op | source)
XLA Modules:
  0.0 33.6 jit_solution(4770494211340923493)
XLA Ops:
  0.6 0.0 copy-start
  0.6 1.0 %shard_map.86.refs_0_ = bf16[2,512,128]{2,1,0:T(8,128)(2,1)S(1)} custom-call(bf16[9,512,128]{2,1,0:T(8,128)(2,1)} %first_ref.1, bf16[9,512,128]{2,1,0:T(8,128)(2,1)} %second_ref.1), custom_call_target="tpu_custom_call" | custom-call | tf_op jit(solution)/shard_map/pallas_call | solution.py:373
  1.6 3.0 %collective-permute-start.2 = (bf16[2,512,128]{2,1,0:T(8,128)(2,1)S(1)}, bf16[2,512,128]{2,1,0:T(8,128)(2,1)S(1)}, u32[]{:S(2)}, u32[]{:S(2)}) collective-permute-start(bf16[2,512,128]{2,1,0:T(8,128)(2,1)S(1)} %shard_map.86.refs_0_), channel_id=1, source_target_pairs={{0,2},{1,3},{2,0},{3,1},{4,6},{5,7},{6,4},{7,5},{8,10},{9,11},{10,... | collective-permute-start | bytes 786440 | tf_op jit(solution)/shard_map/ppermute | solution.py:142
  4.7 0.0 collective-permute-start.1
  4.7 6.3 %collective-permute-done.2.refs_2_ = bf16[2,512,128]{2,1,0:T(8,128)(2,1)S(1)} collective-permute-done((bf16[2,512,128]{2,1,0:T(8,128)(2,1)S(1)}, bf16[2,512,128]{2,1,0:T(8,128)(2,1)S(1)}, u32[]{:S(2)}, u32[]{:S(2)}) %collective-permute-start.2) | collective-permute-done | bytes 262176 | tf_op jit(solution)/shard_map/ppermute | solution.py:142
  11.0 0.0 collective-permute-start.3
  11.0 0.1 pad_add_fusion.where_ref
  11.1 1.5 %shard_map.85.own_ref = bf16[144,512]{1,0:T(8,128)(2,1)S(1)} custom-call(s32[2]{0:T(128)S(1)} %pad_add_fusion.where_ref, s32[16]{0:T(128)} %mask_ref.1, s32[1,128]{1,0:T(1,128)} %bitcast.5, bf16[128,512]{1,0:T(8,128)(2,1)} %source_ref.1), custom_call_target="tpu_custom_call" | custom-call | tf_op jit(solution)/shard_map/pallas_call | solution.py:387
  12.6 1.8 %collective-permute-start = (bf16[144,512]{1,0:T(8,128)(2,1)S(1)}, bf16[144,512]{1,0:T(8,128)(2,1)S(1)}, u32[]{:S(2)}, u32[]{:S(2)}) collective-permute-start(bf16[144,512]{1,0:T(8,128)(2,1)S(1)} %shard_map.85.own_ref), channel_id=1, source_target_pairs={{0,4},{4,0},{8,12},{12,8},{16,20},{20,16},{24,28},{28,24},{1,5},{5... | collective-permute-start | bytes 442376 | tf_op jit(solution)/shard_map/ppermute | solution.py:142
  14.4 4.5 %collective-permute-done.peer_ref = bf16[144,512]{1,0:T(8,128)(2,1)S(1)} collective-permute-done((bf16[144,512]{1,0:T(8,128)(2,1)S(1)}, bf16[144,512]{1,0:T(8,128)(2,1)S(1)}, u32[]{:S(2)}, u32[]{:S(2)}) %collective-permute-start) | collective-permute-done | bytes 147488 | tf_op jit(solution)/shard_map/ppermute | solution.py:142
  18.9 0.0 collective-permute-done.1.refs_1_
  18.9 0.0 copy-done
  18.9 0.9 %shard_map.87 = (bf16[256,384]{1,0:T(8,128)(2,1)S(1)}, f32[256,384]{1,0:T(8,128)S(1)}, bf16[512,256]{1,0:T(8,128)(2,1)S(1)}, bf16[16,512]{1,0:T(8,128)(2,1)S(1)}) custom-call(s32[2]{0:T(128)S(1)} %pad_add_fusion.where_ref, bf16[144,512]{1,0:T(8,128)(2,1)S(1)} %shard_map.85.own_ref, bf16[144,512]{1,0:T(8,128)(2,1)S(1)} %collective-permute-done.peer_ref, ...), custom_call_target="tpu_custom_call" | custom-call | flops 134217728 | bytes 1048576 | tf_op jit(solution)/shard_map/pallas_call | solution.py:404
  19.9 0.0 collective-permute-done.3.refs_3_
  19.9 2.9 %shard_map.88 = (f32[2,64,128]{2,1,0:T(8,128)S(1)}, bf16[2,64,128]{2,1,0:T(8,128)(2,1)S(1)}, bf16[2,64,128]{2,1,0:T(8,128)(2,1)S(1)}, bf16[2,64,128]{2,1,0:T(8,1...) custom-call(s32[2]{0:T(128)S(1)} %pad_add_fusion.where_ref, bf16[144,512]{1,0:T(8,128)(2,1)S(1)} %shard_map.85.own_ref, ...), custom_call_target="tpu_custom_call" | custom-call | flops 402653184 | bytes 2097152 | tf_op jit(solution)/shard_map/pallas_call | solution.py:419
  22.8 1.9 %collective-permute-start.4 = (bf16[2,64,128]{2,1,0:T(8,128)(2,1)S(1)}, bf16[2,64,128]{2,1,0:T(8,128)(2,1)S(1)}, u32[]{:S(2)}, u32[]{:S(2)}) collective-permute-start(bf16[2,64,128]{2,1,0:T(8,128)(2,1)S(1)} %get-tuple-element.26), channel_id=1, source_target_pairs={{0,8},{4,12},{8,0},{12,4},{16,24},{20,28},{24,16},{28,20},{1,9},{5... | collective-permute-start | bytes 98312 | tf_op jit(solution)/shard_map/ppermute | solution.py:142
  24.6 2.6 %collective-permute-start.5 = (bf16[2,64,128]{2,1,0:T(8,128)(2,1)S(1)}, bf16[2,64,128]{2,1,0:T(8,128)(2,1)S(1)}, u32[]{:S(2)}, u32[]{:S(2)}) collective-permute-start(bf16[2,64,128]{2,1,0:T(8,128)(2,1)S(1)} %get-tuple-element.27), channel_id=1, source_target_pairs={{0,16},{4,20},{8,24},{12,28},{16,0},{20,4},{24,8},{28,12},{1,17},{... | collective-permute-start | bytes 98312 | tf_op jit(solution)/shard_map/ppermute | solution.py:142
  27.2 0.0 collective-permute-start.6
  27.2 0.8 %shard_map.90 = (f32[9,64,128]{2,1,0:T(8,128)}, f32[9,64,128]{2,1,0:T(8,128)}) custom-call(), custom_call_target="tpu_custom_call" | custom-call | tf_op jit(solution)/shard_map/pallas_call | solution.py:399
  28.1 1.5 %shard_map.89 = bf16[128,512]{1,0:T(8,128)(2,1)} custom-call(s32[2]{0:T(128)S(1)} %pad_add_fusion.where_ref, f32[128,512]{1,0:T(8,128)S(1)} %get-tuple-element.21.grad_ref, bf16[128,512]{1,0:T(8,128)(2,1)S(1)} %get-tuple-element.22.grad_conv_ref, bf16[2,512,128]{2,1,0:T(8,128)(2,1)S(1)} %shard_map.86.refs_0_, ...), custom_call_target="tpu_custom_call" | custom-call | flops 67108864 | bytes 524288 | tf_op jit(solution)/shard_map/pallas_call | solution.py:442
  29.6 0.0 collective-permute-done.4.refs_0_
  29.6 0.3 collective-permute-done.5.refs_1_
  29.9 3.1 %collective-permute-done.6.refs_2_ = bf16[2,64,128]{2,1,0:T(8,128)(2,1)S(1)} collective-permute-done((bf16[2,64,128]{2,1,0:T(8,128)(2,1)S(1)}, bf16[2,64,128]{2,1,0:T(8,128)(2,1)S(1)}, u32[]{:S(2)}, u32[]{:S(2)}) %collective-permute-start.6) | collective-permute-done | bytes 32800 | tf_op jit(solution)/shard_map/ppermute | solution.py:142
  32.9 0.7 %shard_map.91 = (f32[9,64,128]{2,1,0:T(8,128)}, f32[9,64,128]{2,1,0:T(8,128)}) custom-call(f32[9,64,128]{2,1,0:T(8,128)} %get-tuple-element.23.first_in_ref, f32[9,64,128]{2,1,0:T(8,128)} %get-tuple-element.24.second_in_ref, f32[2,64,128]{2,1,0:T(8,128)S(1)} %get-tuple-element.25.self_ref, ...), custom_call_target="tpu_custom_call", output_to_operand_aliasing={{0}: (0, {}), {1}: (1, {})} | custom-call | tf_op jit(solution)/shard_map/pallas_call | solution.py:449
Async XLA Ops:
  0.6 18.3 %copy-start = (bf16[512,5]{0,1:T(8,128)(2,1)S(1)}, bf16[512,5]{0,1:T(8,128)(2,1)}, u32[]{:S(2)}) copy-start(bf16[512,5]{0,1:T(8,128)(2,1)} %param.11) | copy-start | bytes 15364
  1.6 9.3 %collective-permute-start.2 = (bf16[2,512,128]{2,1,0:T(8,128)(2,1)S(1)}, bf16[2,512,128]{2,1,0:T(8,128)(2,1)S(1)}, u32[]{:S(2)}, u32[]{:S(2)}) collective-permute-start(bf16[2,512,128]{2,1,0:T(8,128)(2,1)S(1)} %shard_map.86.refs_0_), channel_id=1, source_target_pairs={{0,2},{1,3},{2,0},{3,1},{4,6},{5,7},{6,4},{7,5},{8,10},{9,11},{10,... | collective-permute-start | bytes 786440 | tf_op jit(solution)/shard_map/ppermute | solution.py:142
  4.7 14.2 %collective-permute-start.1 = (bf16[2,512,128]{2,1,0:T(8,128)(2,1)S(1)}, bf16[2,512,128]{2,1,0:T(8,128)(2,1)S(1)}, u32[]{:S(2)}, u32[]{:S(2)}) collective-permute-start(bf16[2,512,128]{2,1,0:T(8,128)(2,1)S(1)} %shard_map.86.refs_0_), channel_id=1, source_target_pairs={{0,1},{1,0},{2,3},{3,2},{4,5},{5,4},{6,7},{7,6},{8,9},{9,8},{10,11... | collective-permute-start | bytes 786440 | tf_op jit(solution)/shard_map/ppermute | solution.py:142
  11.0 8.9 %collective-permute-start.3 = (bf16[2,512,128]{2,1,0:T(8,128)(2,1)S(1)}, bf16[2,512,128]{2,1,0:T(8,128)(2,1)S(1)}, u32[]{:S(2)}, u32[]{:S(2)}) collective-permute-start(bf16[2,512,128]{2,1,0:T(8,128)(2,1)S(1)} %collective-permute-done.2.refs_2_), channel_id=1, source_target_pairs={{0,1},{1,0},{2,3},{3,2},{4,5},{5,4},{6,7},{7,6},{8,9},{9,8},{10,11... | collective-permute-start | bytes 786440 | tf_op jit(solution)/shard_map/ppermute | solution.py:142
  12.6 6.4 %collective-permute-start = (bf16[144,512]{1,0:T(8,128)(2,1)S(1)}, bf16[144,512]{1,0:T(8,128)(2,1)S(1)}, u32[]{:S(2)}, u32[]{:S(2)}) collective-permute-start(bf16[144,512]{1,0:T(8,128)(2,1)S(1)} %shard_map.85.own_ref), channel_id=1, source_target_pairs={{0,4},{4,0},{8,12},{12,8},{16,20},{20,16},{24,28},{28,24},{1,5},{5... | collective-permute-start | bytes 442376 | tf_op jit(solution)/shard_map/ppermute | solution.py:142
  22.8 6.8 %collective-permute-start.4 = (bf16[2,64,128]{2,1,0:T(8,128)(2,1)S(1)}, bf16[2,64,128]{2,1,0:T(8,128)(2,1)S(1)}, u32[]{:S(2)}, u32[]{:S(2)}) collective-permute-start(bf16[2,64,128]{2,1,0:T(8,128)(2,1)S(1)} %get-tuple-element.26), channel_id=1, source_target_pairs={{0,8},{4,12},{8,0},{12,4},{16,24},{20,28},{24,16},{28,20},{1,9},{5... | collective-permute-start | bytes 98312 | tf_op jit(solution)/shard_map/ppermute | solution.py:142
  24.6 5.2 %collective-permute-start.5 = (bf16[2,64,128]{2,1,0:T(8,128)(2,1)S(1)}, bf16[2,64,128]{2,1,0:T(8,128)(2,1)S(1)}, u32[]{:S(2)}, u32[]{:S(2)}) collective-permute-start(bf16[2,64,128]{2,1,0:T(8,128)(2,1)S(1)} %get-tuple-element.27), channel_id=1, source_target_pairs={{0,16},{4,20},{8,24},{12,28},{16,0},{20,4},{24,8},{28,12},{1,17},{... | collective-permute-start | bytes 98312 | tf_op jit(solution)/shard_map/ppermute | solution.py:142
  27.2 5.7 %collective-permute-start.6 = (bf16[2,64,128]{2,1,0:T(8,128)(2,1)S(1)}, bf16[2,64,128]{2,1,0:T(8,128)(2,1)S(1)}, u32[]{:S(2)}, u32[]{:S(2)}) collective-permute-start(bf16[2,64,128]{2,1,0:T(8,128)(2,1)S(1)} %get-tuple-element.28), channel_id=1, source_target_pairs={{0,24},{4,28},{8,16},{12,20},{16,8},{20,12},{24,0},{28,4},{1,25},{... | collective-permute-start | bytes 98312 | tf_op jit(solution)/shard_map/ppermute | solution.py:142
where the time goes:
time: 33.8 us; the launch traced here: 33.6 us
  waiting for transfers between devices  14.2 us (42%)
  Pallas kernels  9.33 us (28%)
  starting transfers between devices  9.33 us (28%)
  between operations  0.69 us (2%)
    ppermute x7, waiting for transfers between devices, swap(): lax.ppermute(block, axis, [(i, i ^ offset) for i in range(lax.axis_size(a...  14.2 us
    ppermute x7, starting transfers between devices, swap(): lax.ppermute(block, axis, [(i, i ^ offset) for i in range(lax.axis_size(a...  9.33 us
    pallas_call x1, Pallas kernels, local_plan(): call(functools.partial(main_body, mp_count, sent_count, classes), [smem]...  2.91 us
    pallas_call x1, Pallas kernels, local_plan(): call(functools.partial(input_grad_body, mp_count), [smem] + [vmem] * (2 +...  1.52 us
    pallas_call x1, Pallas kernels, local_plan(): call(rows_body, [smem] + [hbm] * 3, (shape((rows + SIDE_ROWS, channels)),...  1.49 us
    pallas_call x1, Pallas kernels, local_plan(): call(functools.partial(matrices_body, centre_tap), [hbm] * 2, (shape((2,...  0.99 us
    pallas_call x1, Pallas kernels, local_plan(): call(functools.partial(early_body, mp_count), [smem] + [vmem] * (2 + mp_c...  0.93 us
    pallas_call x1, Pallas kernels, local_plan(): first_grad, second_grad = call(blank_body, [], (whole, whole))()  0.83 us
  transfers between devices with their start and end apart: 7, of which 4 were waited for; matrix products, arithmetic and copies ran while one was open for 0% of the time, Pallas kernels for 14%

commit v1 on v0

--- a/solution.py
+++ b/solution.py
@@ -14,7 +14,8 @@
 epsilon = 1e-05
 root_half = 0.7071067811865476
 inv_root_two_pi = 0.3989422804014327
-ROW_CHUNK = 32
+half_log2_e = -0.7213475204444817
+log2_inv_root_two_pi = -1.3257480647361593
 SIDE_ROWS = 16
 VMEM_LIMIT = 24 * 1024 * 1024
 
@@ -32,6 +33,12 @@
     spread = jnp.mean(centred * centred, axis=-1, keepdims=True)
     inverse = lax.rsqrt(spread + epsilon)
     return (centred * inverse, inverse)
+
+
+def gelu_and_slope(conv_out):
+    normal_cdf = 0.5 + 0.5 * lax.erf(conv_out * root_half)
+    density = jnp.exp2(conv_out * conv_out * half_log2_e + log2_inv_root_two_pi)
+    return (conv_out * normal_cdf, normal_cdf + conv_out * density)
 
 
 def active_hops(tap_count, dilation_blocks, seq_count):
@@ -142,6 +149,11 @@
     return lax.ppermute(block, axis, [(i, i ^ offset) for i in range(lax.axis_size(axis))])
 
 
+def turn_pairs(block, axis, turn):
+    count = lax.axis_size(axis)
+    return lax.ppermute(block, axis, [(i, (i + 2 * turn) % count) for i in range(count)])
+
+
 def block_at(me, offset, width):
     return pl.ds(pl.multiple_of((me ^ offset) * width, width), width)
 
@@ -162,26 +174,21 @@
         copy.wait()
 
 
-def rows_body(where_ref, mask_ref, ids_ref, source_ref, rows_ref, mask_at, ids_at, sems):
-    rows = source_ref.shape[0]
+def targets_body(where_ref, mask_ref, ids_ref, targets_ref, mask_at, ids_at, sems):
     copies = [
         pltpu.make_async_copy(mask_ref, mask_at, sems.at[0]),
         pltpu.make_async_copy(ids_ref, ids_at, sems.at[1]),
-        pltpu.make_async_copy(source_ref, rows_ref.at[pl.ds(0, rows)], sems.at[2]),
     ]
     for copy in copies:
         copy.start()
-    copies[0].wait()
-    copies[1].wait()
-    positions = lax.broadcasted_iota(jnp.int32, ids_at.shape, 1) + where_ref[1] * rows
+    for copy in copies:
+        copy.wait()
+    positions = lax.broadcasted_iota(jnp.int32, ids_at.shape, 1) + where_ref[1] * ids_at.shape[1]
     masked = jnp.zeros(ids_at.shape, jnp.int32)
     for entry in range(mask_at.shape[0]):
         masked = jnp.where(positions == mask_at[entry], 1, masked)
     targets = jnp.where(masked == 1, ids_at[...], -1).astype(jnp.float32)
-    extra = rows_ref.shape[0] - rows
-    rows_ref[rows:, :] = jnp.zeros((extra, rows_ref.shape[1]), jnp.bfloat16)
-    rows_ref[rows:, 0:rows] = jnp.broadcast_to(targets, (extra, rows)).astype(jnp.bfloat16)
-    copies[2].wait()
+    targets_ref[...] = jnp.broadcast_to(targets, targets_ref.shape).astype(jnp.bfloat16)
 
 
 def blank_body(first_ref, second_ref):
@@ -208,106 +215,116 @@
     matrix_refs = refs[:-4]
     activation_ref, slope_ref, flip_ref, head_out_ref = refs[-4:]
     me = where_ref[0]
-    half = activation_ref.shape[0] // 2
+    half = own_ref.shape[0]
     weights = columns_of(me, matrix_refs, 0, count)
     for part, ref in enumerate((own_ref, peer_ref)):
+        rows = pl.ds(part * half, half)
         conv_out = dot(own_order(me, ref, pl.ds(0, half), count), weights)
-        for start in range(0, half, ROW_CHUNK):
-            rows = pl.ds(part * half + start, ROW_CHUNK)
-            activation, gelu_slope = gelu_parts(conv_out[start : start + ROW_CHUNK])
-            activation_ref[rows, :] = activation.astype(jnp.bfloat16)
-            slope_ref[rows, :] = gelu_slope
-        flip_ref[:, pl.ds(part * half, half)] = ref[pl.ds(0, half), :].T
+        activation_ref[rows, :], slope_ref[rows, :] = gelu_and_slope(conv_out)
+        flip_ref[:, rows] = ref[...].T
     head_out_ref[...] = jnp.zeros_like(head_out_ref)
     classes = head_ref.shape[0]
     head_out_ref[0:classes, :] = own_order(me, head_ref, pl.ds(0, classes), count)
 
 
-def main_body(count, sent_count, classes, where_ref, own_ref, peer_ref, activation_ref, slope_ref, source_flip_ref, head_ref, *refs):
+def owner_of(block, blocks, turn):
+    return lax.rem(lax.div(block, 2) + turn, blocks // 2) * 2 + lax.rem(block, 2)
+
+
+def main_body(count, blocks, classes, where_ref, own_ref, peer_ref, own_targets_ref, peer_targets_ref, activation_ref, slope_ref, source_flip_ref, head_ref, *refs):
+    turns = blocks // 2
     matrix_refs, refs = refs[:count], refs[count:]
-    self_ref, sent_refs, refs = refs[0], refs[1 : 1 + sent_count], refs[1 + sent_count :]
+    self_ref, sent_refs, refs = refs[0], refs[1:turns], refs[turns:]
     grad_out_ref, grad_conv_out_ref = refs[:2]
     hidden_one_ref, normed_one_ref, scale_one_ref, hidden_flip_ref, normed_two_ref, scale_two_ref, hidden_two_ref, grad_ref, grad_conv_ref = refs[2:]
     me, block = where_ref[0], where_ref[1]
-    total_rows = grad_ref.shape[0]
-    half = total_rows // 2
-    width = self_ref.shape[2]
-    depth = self_ref.shape[1]
-    halves = (0, half)
-
+    half = own_ref.shape[0]
+    _, depth, width = self_ref.shape
+    source_refs = (own_ref, peer_ref)
+    target_refs = (own_targets_ref, peer_targets_ref)
     late = columns_of(me, matrix_refs[-1:], 0, count)
-    for start, ref in zip(halves, (own_ref, peer_ref)):
-        conv_out = dot(own_order(me, ref, pl.ds(0, half), count), late)
-        for inner in range(0, half, ROW_CHUNK):
-            rows = pl.ds(start + inner, ROW_CHUNK)
-            activation, gelu_slope = gelu_parts(conv_out[inner : inner + ROW_CHUNK])
-            normed, inverse = norm_parts(
-                jnp.concatenate([activation_ref[rows, :], activation.astype(jnp.bfloat16)], axis=1)
-            )
-            scale_one_ref[rows, :] = jnp.concatenate([slope_ref[rows, :], gelu_slope], axis=1) * inverse
-            normed_one_ref[rows, :] = normed
-            source = own_order(me, ref, pl.ds(inner, ROW_CHUNK), count)
-            hidden_one_ref[rows, :] = (source.astype(jnp.float32) + normed).astype(jnp.bfloat16)
-
     weights = columns_of(me, matrix_refs, 1, count)
-    for start in halves:
-        conv_out = dot(hidden_one_ref[pl.ds(start, half), :], weights)
-        for inner in range(0, half, ROW_CHUNK):
-            rows = pl.ds(start + inner, ROW_CHUNK)
-            activation, gelu_slope = gelu_parts(conv_out[inner : inner + ROW_CHUNK])
-            normed, inverse = norm_parts(activation.astype(jnp.bfloat16))
-            scale_two_ref[rows, :] = gelu_slope * inverse
-            normed_two_ref[rows, :] = normed
-            hidden_two_ref[rows, :] = (hidden_one_ref[rows, :].astype(jnp.float32) + normed).astype(jnp.bfloat16)
-
-    for offset in range(count):
-        flipped = hidden_one_ref[:, pl.ds(offset * width, width)].T
-        hidden_flip_ref[block_at(me, offset, width), :] = flipped
-
     head = head_ref[...]
-    logits = dot(head, hidden_two_ref[...], NT)
-    class_rows = lax.broadcasted_iota(jnp.int32, logits.shape, 0)
-    exponent = jnp.where(class_rows < classes, jnp.exp(logits), 0.0)
-    probability = exponent / jnp.sum(exponent, axis=0, keepdims=True)
-    targets = jnp.concatenate(
-        [ref[half : half + head.shape[0], 0:half] for ref in (own_ref, peer_ref)], axis=1
-    ).astype(jnp.float32)
-    onehot = (class_rows.astype(jnp.float32) == targets).astype(jnp.float32)
-    weight = (targets >= 0.0).astype(jnp.float32)
-    rest = jnp.where(class_rows < classes, weight * (probability - onehot), 0.0)
-    terms = []
-    for _ in range(3):
-        term = rest.astype(jnp.bfloat16)
-        terms.append(term)
-        rest = rest - term.astype(jnp.float32)
-    grad_ref[...] = dot(jnp.concatenate(terms, axis=0), jnp.concatenate([head] * 3, axis=0), TN)
-
-    def norm_backward(normed_ref, scale_ref):
-        for start in range(0, total_rows, ROW_CHUNK):
-            rows = pl.ds(start, ROW_CHUNK)
-            grad_out, normed = grad_ref[rows, :], normed_ref[rows, :]
-            mean_grad = jnp.mean(grad_out, axis=-1, keepdims=True)
-            mean_cross = jnp.mean(grad_out * normed, axis=-1, keepdims=True)
-            grad_conv_ref[rows, :] = (
-                (grad_out - mean_grad - normed * mean_cross) * scale_ref[rows, :]
-            ).astype(jnp.bfloat16)
+
+    def first_block(part):
+        rows = pl.ds(part * half, half)
+        source = own_order(me, source_refs[part], pl.ds(0, half), count)
+        activation, gelu_slope = gelu_and_slope(dot(source, late))
+        normed, inverse = norm_parts(jnp.concatenate([activation_ref[rows, :], activation], axis=1))
+        scale_one_ref[rows, :] = jnp.concatenate([slope_ref[rows, :], gelu_slope], axis=1) * inverse
+        normed_one_ref[rows, :] = normed
+        hidden_one_ref[rows, :] = (source.astype(jnp.float32) + normed).astype(jnp.bfloat16)
+
+    def second_block(part):
+        rows = pl.ds(part * half, half)
+        source = hidden_one_ref[rows, :]
+        activation, gelu_slope = gelu_and_slope(dot(source, weights))
+        normed, inverse = norm_parts(activation)
+        scale_two_ref[rows, :] = gelu_slope * inverse
+        normed_two_ref[rows, :] = normed
+        hidden_two_ref[rows, :] = (source.astype(jnp.float32) + normed).astype(jnp.bfloat16)
+
+    def flip_hidden(part):
+        rows = pl.ds(part * half, half)
+        for offset in range(count):
+            flipped = hidden_one_ref[rows, pl.ds(offset * width, width)].T
+            hidden_flip_ref[block_at(me, offset, width), rows] = flipped
+
+    def loss_backward(part):
+        rows = pl.ds(part * half, half)
+        logits = dot(head, hidden_two_ref[rows, :], NT)
+        class_rows = lax.broadcasted_iota(jnp.int32, logits.shape, 0)
+        exponent = jnp.where(class_rows < classes, jnp.exp(logits), 0.0)
+        probability = exponent / jnp.sum(exponent, axis=0, keepdims=True)
+        targets = target_refs[part][...].astype(jnp.float32)
+        onehot = (class_rows.astype(jnp.float32) == targets).astype(jnp.float32)
+        weight = (targets >= 0.0).astype(jnp.float32)
+        rest = jnp.where(class_rows < classes, weight * (probability - onehot), 0.0)
+        terms = []
+        for _ in range(3):
+            term = rest.astype(jnp.bfloat16)
+            terms.append(term)
+            rest = rest - term.astype(jnp.float32)
+        grad_ref[rows, :] = dot(jnp.concatenate(terms, axis=0), jnp.concatenate([head] * 3, axis=0), TN)
+
+    def norm_backward(part, normed_ref, scale_ref):
+        rows = pl.ds(part * half, half)
+        grad_out, normed = grad_ref[rows, :], normed_ref[rows, :]
+        mean_grad = jnp.mean(grad_out, axis=-1, keepdims=True)
+        mean_cross = jnp.mean(grad_out * normed, axis=-1, keepdims=True)
+        grad_conv_ref[rows, :] = (
+            (grad_out - mean_grad - normed * mean_cross) * scale_ref[rows, :]
+        ).astype(jnp.bfloat16)
+
+    def input_backward(part):
+        rows = pl.ds(part * half, half)
+        grad_ref[rows, :] += dot(grad_conv_ref[rows, :], weights, NT)
 
     def kernel_parts(flip_ref, slot):
         sources = [
-            flip_ref[pl.ds(pl.multiple_of((block ^ (2 * j)) * depth, depth), depth), :]
-            for j in range(1 + sent_count)
+            flip_ref[pl.ds(pl.multiple_of(owner_of(block, blocks, turn) * depth, depth), depth), :]
+            for turn in range(turns)
         ]
         part = dot(stacked(sources, 0), grad_conv_ref[:, 0:width])
         self_ref[slot] = part[0:depth]
-        for j, ref in enumerate(sent_refs):
-            ref[slot] = part[(j + 1) * depth : (j + 2) * depth].astype(jnp.bfloat16)
-
-    norm_backward(normed_two_ref, scale_two_ref)
-    for start in halves:
-        rows = pl.ds(start, half)
-        grad_ref[rows, :] += dot(grad_conv_ref[rows, :], weights, NT)
+        for turn, ref in enumerate(sent_refs, 1):
+            ref[slot] = part[turn * depth : (turn + 1) * depth].astype(jnp.bfloat16)
+
+    first_block(0)
+    first_block(1)
+    second_block(0)
+    second_block(1)
+    loss_backward(0)
+    norm_backward(0, normed_two_ref, scale_two_ref)
+    loss_backward(1)
+    norm_backward(1, normed_two_ref, scale_two_ref)
+    input_backward(0)
+    input_backward(1)
+    flip_hidden(0)
+    flip_hidden(1)
     kernel_parts(hidden_flip_ref, 1)
-    norm_backward(normed_one_ref, scale_one_ref)
+    norm_backward(0, normed_one_ref, scale_one_ref)
+    norm_backward(1, normed_one_ref, scale_one_ref)
     kernel_parts(source_flip_ref, 0)
     grad_out_ref[...] = grad_ref[pl.ds(0, half), :]
     grad_conv_out_ref[...] = grad_conv_ref[pl.ds(0, half), :]
@@ -324,16 +341,15 @@
         ].astype(jnp.bfloat16)
 
 
-def total_body(centre_tap, first_in_ref, second_in_ref, self_ref, *refs):
-    received = refs[:-4]
-    first_ref, second_ref, sum_ref, sems = refs[-4:]
+def total_body(centre_tap, first_in_ref, second_in_ref, input_grad_ref, self_ref, *refs):
+    received = refs[:-5]
+    first_ref, second_ref, grad_out_ref, sum_ref, sems = refs[-5:]
+    copies = [pltpu.make_async_copy(input_grad_ref, grad_out_ref, sems.at[2])]
+    copies[0].start()
     sum_ref[...] = self_ref[...] + sum(ref[...].astype(jnp.float32) for ref in received)
-    copies = [
-        pltpu.make_async_copy(sum_ref.at[slot], ref.at[centre_tap], sems.at[slot])
-        for slot, ref in enumerate((first_ref, second_ref))
-    ]
-    for copy in copies:
-        copy.start()
+    for slot, ref in enumerate((first_ref, second_ref)):
+        copies.append(pltpu.make_async_copy(sum_ref.at[slot], ref.at[centre_tap], sems.at[slot]))
+        copies[-1].start()
     for copy in copies:
         copy.wait()
 
@@ -384,17 +400,18 @@
         bit //= 2
     blocks = [blocks[offset] for offset in range(mp_count)]
 
-    (own_rows,) = call(
-        rows_body,
-        [smem] + [hbm] * 3,
-        (shape((rows + SIDE_ROWS, channels)),),
+    peer_rows = swap(hidden_entry_states, "seq", 1)
+    (own_targets,) = call(
+        targets_body,
+        [smem] + [hbm] * 2,
+        (shape((SIDE_ROWS, rows)),),
         scratch=[
             pltpu.SMEM(mask_index.shape, jnp.int32),
             pltpu.VMEM((1, rows), jnp.int32),
-            pltpu.SemaphoreType.DMA((3,)),
+            pltpu.SemaphoreType.DMA((2,)),
         ],
-    )(where, in_hbm(mask_index), in_hbm(base_ids[None, :]), in_hbm(hidden_entry_states))
-    peer_rows = swap(own_rows, "seq", 1)
+    )(where, in_hbm(mask_index), in_hbm(base_ids[None, :]))
+    peer_targets = swap(own_targets, "seq", 1)
     whole = shape((tap_count, depth, width), jnp.float32)
     first_grad, second_grad = call(blank_body, [], (whole, whole))()
 
@@ -405,22 +422,22 @@
         functools.partial(early_body, mp_count),
         [smem] + [vmem] * (2 + mp_count),
         (
-            shape((pair_rows, early)),
+            shape((pair_rows, early), jnp.float32),
             shape((pair_rows, early), jnp.float32),
             shape((channels, pair_rows)),
             shape((SIDE_ROWS, channels)),
         ),
         flops=product,
         moved=8 * pair_rows * channels,
-    )(where, own_rows, peer_rows, head_weight.T, *blocks[:-1])
-
-    sent_count = seq_count // 2 - 1
+    )(where, hidden_entry_states, peer_rows, head_weight.T, *blocks[:-1])
+
+    turns = seq_count // 2
     part = (2, depth, width)
     outs = call(
-        functools.partial(main_body, mp_count, sent_count, classes),
-        [smem] + [vmem] * (6 + mp_count),
+        functools.partial(main_body, mp_count, seq_count, classes),
+        [smem] + [vmem] * (8 + mp_count),
         (shape(part, jnp.float32),)
-        + (shape(part),) * sent_count
+        + (shape(part),) * (turns - 1)
         + (shape((rows, channels), jnp.float32), shape((rows, channels))),
         scratch=[
             pltpu.VMEM((pair_rows, channels), jnp.bfloat16),
@@ -435,10 +452,10 @@
         ],
         flops=3 * product,
         moved=16 * pair_rows * channels,
-    )(where, own_rows, peer_rows, activation, slope, source_flip, head, *blocks)
+    )(where, hidden_entry_states, peer_rows, own_targets, peer_targets, activation, slope, source_flip, head, *blocks)
     own_part, sent, (grad_one, grad_conv) = outs[0], outs[1:-2], outs[-2:]
 
-    received = [swap(piece, "seq", 2 * (j + 1)) for j, piece in enumerate(sent)]
+    received = [turn_pairs(piece, "seq", turn) for turn, piece in enumerate(sent, 1)]
     (input_grad,) = call(
         functools.partial(input_grad_body, mp_count),
         [smem] + [vmem] * (2 + mp_count),
@@ -446,14 +463,14 @@
         flops=product // 2,
         moved=8 * rows * channels,
     )(where, grad_one, grad_conv, *blocks)
-    first_grad, second_grad = call(
+    first_grad, second_grad, input_grad = call(
         functools.partial(total_body, centre_tap),
-        [hbm, hbm] + [vmem] * (1 + sent_count),
-        (whole, whole),
-        out_specs=(hbm, hbm),
-        scratch=[pltpu.VMEM(part, jnp.float32), pltpu.SemaphoreType.DMA((2,))],
+        [hbm, hbm] + [vmem] * (1 + turns),
+        (whole, whole, shape((rows, channels))),
+        out_specs=(hbm,) * 3,
+        scratch=[pltpu.VMEM(part, jnp.float32), pltpu.SemaphoreType.DMA((3,))],
         aliases={0: 0, 1: 1},
-    )(first_grad, second_grad, own_part, *received)
+    )(first_grad, second_grad, input_grad, own_part, *received)
     return (input_grad, first_grad, second_grad)
 
 

time: 33.8 us -> 29.8 us (0.88)
  waiting for transfers between devices: 14.2 us -> 9.69 us
  starting transfers between devices: 9.33 us -> 11 us
  Pallas kernels: 9.33 us -> 8.21 us
    ppermute x0 -> x3, starting transfers between devices: none -> 5.83 us  [turn_pairs(): lax.ppermute(block, axis, [(i, (i + 2 * turn) % count) for i in range(cou...]
    ppermute x7 -> x5, waiting for transfers between devices: 14.2 us -> 8.83 us  [swap(): lax.ppermute(block, axis, [(i, i ^ offset) for i in range(lax.axis_size(a...]
    ppermute x7 -> x5, starting transfers between devices: 9.33 us -> 5.13 us  [swap(): lax.ppermute(block, axis, [(i, i ^ offset) for i in range(lax.axis_size(a...]
    ppermute x0 -> x3, waiting for transfers between devices: none -> 0.86 us  [turn_pairs(): lax.ppermute(block, axis, [(i, (i + 2 * turn) % count) for i in range(cou...]
    pallas_call x1, Pallas kernels: 1.52 us -> 0.86 us  [local_plan(): call(functools.partial(input_grad_body, mp_count), [smem] + [vmem] * (2 +...]
    pallas_call x2, Pallas kernels: 4.4 us -> 3.9 us  [the longest x1 2.66 us: local_plan(): call(functools.partial(main_body, mp_count, seq_count, classes), [smem] +...]
  transfers between devices with their start and end apart: 7 -> 8, of which waited for: 4 -> 3; matrix products, arithmetic and copies ran while one was open for 0% -> 0% of each run, Pallas kernels for 14% -> 13%
where the time goes in v1:
time: 29.8 us; the launch traced here: 29.7 us
  starting transfers between devices  11 us (37%)
  waiting for transfers between devices  9.69 us (33%)
  Pallas kernels  8.21 us (28%)
  between operations  0.72 us (2%)
    ppermute x5, waiting for transfers between devices, swap(): lax.ppermute(block, axis, [(i, i ^ offset) for i in range(lax.axis_size(a...  8.83 us
    ppermute x3, starting transfers between devices, turn_pairs(): lax.ppermute(block, axis, [(i, (i + 2 * turn) % count) for i in range(cou...  5.83 us
    ppermute x5, starting transfers between devices, swap(): lax.ppermute(block, axis, [(i, i ^ offset) for i in range(lax.axis_size(a...  5.13 us
    pallas_call x1, Pallas kernels, local_plan(): call(functools.partial(main_body, mp_count, seq_count, classes), [smem] +...  2.66 us
    pallas_call x1, Pallas kernels, local_plan(): call(targets_body, [smem] + [hbm] * 2, (shape((SIDE_ROWS, rows)),), scrat...  1.24 us
    pallas_call x1, Pallas kernels, local_plan(): call(functools.partial(matrices_body, centre_tap), [hbm] * 2, (shape((2,...  1.02 us
    pallas_call x1, Pallas kernels, local_plan(): call(functools.partial(early_body, mp_count), [smem] + [vmem] * (2 + mp_c...  0.91 us
    pallas_call x1, Pallas kernels, local_plan(): call(functools.partial(input_grad_body, mp_count), [smem] + [vmem] * (2 +...  0.86 us
  transfers between devices with their start and end apart: 8, of which 3 were waited for; matrix products, arithmetic and copies ran while one was open for 0% of the time, Pallas kernels for 13%

profile of v1, /device:TPU:0, one launch (start us, length us, event | category | flops | bytes accessed | tf_op | source)
XLA Modules:
  0.0 29.7 jit_solution(14316671797999396594)
XLA Ops:
  0.7 1.0 %shard_map.87.refs_0_ = bf16[2,512,128]{2,1,0:T(8,128)(2,1)S(1)} custom-call(bf16[9,512,128]{2,1,0:T(8,128)(2,1)} %first_ref.1, bf16[9,512,128]{2,1,0:T(8,128)(2,1)} %second_ref.1), custom_call_target="tpu_custom_call" | custom-call | tf_op jit(solution)/shard_map/pallas_call | solution.py:389
  1.7 3.0 %collective-permute-start.3 = (bf16[2,512,128]{2,1,0:T(8,128)(2,1)S(1)}, bf16[2,512,128]{2,1,0:T(8,128)(2,1)S(1)}, u32[]{:S(2)}, u32[]{:S(2)}) collective-permute-start(bf16[2,512,128]{2,1,0:T(8,128)(2,1)S(1)} %shard_map.87.refs_0_), channel_id=1, source_target_pairs={{0,2},{1,3},{2,0},{3,1},{4,6},{5,7},{6,4},{7,5},{8,10},{9,11},{10,... | collective-permute-start | bytes 786440 | tf_op jit(solution)/shard_map/ppermute | solution.py:149
  4.7 0.0 collective-permute-start.2
  4.7 6.3 %collective-permute-done.3.refs_2_ = bf16[2,512,128]{2,1,0:T(8,128)(2,1)S(1)} collective-permute-done((bf16[2,512,128]{2,1,0:T(8,128)(2,1)S(1)}, bf16[2,512,128]{2,1,0:T(8,128)(2,1)S(1)}, u32[]{:S(2)}, u32[]{:S(2)}) %collective-permute-start.3) | collective-permute-done | bytes 262176 | tf_op jit(solution)/shard_map/ppermute | solution.py:149
  11.0 0.0 collective-permute-start.4
  11.0 1.8 %collective-permute-start = (bf16[128,512]{1,0:T(8,128)(2,1)S(1)}, bf16[128,512]{1,0:T(8,128)(2,1)S(1)}, u32[]{:S(2)}, u32[]{:S(2)}) collective-permute-start(bf16[128,512]{1,0:T(8,128)(2,1)S(1)} %copy-done), channel_id=1, source_target_pairs={{0,4},{4,0},{8,12},{12,8},{16,20},{20,16},{24,28},{28,24},{1,5},{5... | collective-permute-start | bytes 393224 | tf_op jit(solution)/shard_map/ppermute | solution.py:149
  12.8 0.1 pad_add_fusion.where_ref
  12.9 1.2 %shard_map.86.own_targets_ref = bf16[16,128]{1,0:T(8,128)(2,1)S(1)} custom-call(s32[2]{0:T(128)S(1)} %pad_add_fusion.where_ref, s32[16]{0:T(128)} %mask_ref.1, s32[1,128]{1,0:T(1,128)} %bitcast.5), custom_call_target="tpu_custom_call" | custom-call | tf_op jit(solution)/shard_map/pallas_call | solution.py:404
  14.1 0.3 %collective-permute-start.1 = (bf16[16,128]{1,0:T(8,128)(2,1)S(1)}, bf16[16,128]{1,0:T(8,128)(2,1)S(1)}, u32[]{:S(2)}, u32[]{:S(2)}) collective-permute-start(bf16[16,128]{1,0:T(8,128)(2,1)S(1)} %shard_map.86.own_targets_ref), channel_id=1, source_target_pairs={{0,4},{4,0},{8,12},{12,8},{16,20},{20,16},{24,28},{28,24},{1,5},{5... | collective-permute-start | bytes 12296 | tf_op jit(solution)/shard_map/ppermute | solution.py:149
  14.4 2.5 %collective-permute-done.peer_ref = bf16[128,512]{1,0:T(8,128)(2,1)S(1)} collective-permute-done((bf16[128,512]{1,0:T(8,128)(2,1)S(1)}, bf16[128,512]{1,0:T(8,128)(2,1)S(1)}, u32[]{:S(2)}, u32[]{:S(2)}) %collective-permute-start) | collective-permute-done | bytes 131104 | tf_op jit(solution)/shard_map/ppermute | solution.py:149
  17.0 0.0 collective-permute-done.2.refs_1_
  17.0 0.9 %shard_map.88 = (f32[256,384]{1,0:T(8,128)S(1)}, f32[256,384]{1,0:T(8,128)S(1)}, bf16[512,256]{1,0:T(8,128)(2,1)S(1)}, bf16[16,512]{1,0:T(8,128)(2,1)S(1)}) custom-call(s32[2]{0:T(128)S(1)} %pad_add_fusion.where_ref, bf16[128,512]{1,0:T(8,128)(2,1)S(1)} %copy-done, bf16[128,512]{1,0:T(8,128)(2,1)S(1)} %collective-permute-done.peer_ref, ...), custom_call_target="tpu_custom_call" | custom-call | flops 134217728 | bytes 1048576 | tf_op jit(solution)/shard_map/pallas_call | solution.py:421
  17.9 0.0 collective-permute-done.1.peer_targets_ref
  17.9 0.0 collective-permute-done.4.refs_3_
  17.9 2.7 %shard_map.89 = (f32[2,64,128]{2,1,0:T(8,128)S(1)}, bf16[2,64,128]{2,1,0:T(8,128)(2,1)S(1)}, bf16[2,64,128]{2,1,0:T(8,128)(2,1)S(1)}, bf16[2,64,128]{2,1,0:T(8,1...) custom-call(s32[2]{0:T(128)S(1)} %pad_add_fusion.where_ref, bf16[128,512]{1,0:T(8,128)(2,1)S(1)} %copy-done, ...), custom_call_target="tpu_custom_call" | custom-call | flops 402653184 | bytes 2097152 | tf_op jit(solution)/shard_map/pallas_call | solution.py:436
  20.6 1.9 %collective-permute-start.5 = (bf16[2,64,128]{2,1,0:T(8,128)(2,1)S(1)}, bf16[2,64,128]{2,1,0:T(8,128)(2,1)S(1)}, u32[]{:S(2)}, u32[]{:S(2)}) collective-permute-start(bf16[2,64,128]{2,1,0:T(8,128)(2,1)S(1)} %get-tuple-element.27), channel_id=1, source_target_pairs={{0,8},{4,12},{8,16},{12,20},{16,24},{20,28},{24,0},{28,4},{1,9},{5... | collective-permute-start | bytes 98312 | tf_op jit(solution)/shard_map/ppermute | solution.py:154
  22.5 2.6 %collective-permute-start.6 = (bf16[2,64,128]{2,1,0:T(8,128)(2,1)S(1)}, bf16[2,64,128]{2,1,0:T(8,128)(2,1)S(1)}, u32[]{:S(2)}, u32[]{:S(2)}) collective-permute-start(bf16[2,64,128]{2,1,0:T(8,128)(2,1)S(1)} %get-tuple-element.28), channel_id=1, source_target_pairs={{0,16},{4,20},{8,24},{12,28},{16,0},{20,4},{24,8},{28,12},{1,17},{... | collective-permute-start | bytes 98312 | tf_op jit(solution)/shard_map/ppermute | solution.py:154
  25.1 1.3 %collective-permute-start.7 = (bf16[2,64,128]{2,1,0:T(8,128)(2,1)S(1)}, bf16[2,64,128]{2,1,0:T(8,128)(2,1)S(1)}, u32[]{:S(2)}, u32[]{:S(2)}) collective-permute-start(bf16[2,64,128]{2,1,0:T(8,128)(2,1)S(1)} %get-tuple-element.29), channel_id=1, source_target_pairs={{0,24},{4,28},{8,0},{12,4},{16,8},{20,12},{24,16},{28,20},{1,25},{... | collective-permute-start | bytes 98312 | tf_op jit(solution)/shard_map/ppermute | solution.py:154
  26.4 0.8 %shard_map.85 = (f32[9,64,128]{2,1,0:T(8,128)}, f32[9,64,128]{2,1,0:T(8,128)}) custom-call(), custom_call_target="tpu_custom_call" | custom-call | tf_op jit(solution)/shard_map/pallas_call | solution.py:416
  27.2 0.9 %shard_map.90.input_grad_ref = bf16[128,512]{1,0:T(8,128)(2,1)S(1)} custom-call(s32[2]{0:T(128)S(1)} %pad_add_fusion.where_ref, f32[128,512]{1,0:T(8,128)S(1)} %get-tuple-element.24.grad_ref, bf16[128,512]{1,0:T(8,128)(2,1)S(1)} %get-tuple-element.25.grad_conv_ref, bf16[2,512,128]{2,1,0:T(8,128)(2,1)S(1)} %shard_map.87.refs_0_, ...), custom_call_target="tpu_custom_call" | custom-call | flops 67108864 | bytes 524288 | tf_op jit(solution)/shard_map/pallas_call | solution.py:459
  28.1 0.0 collective-permute-done.5.refs_0_
  28.1 0.0 collective-permute-done.6.refs_1_
  28.1 0.9 %collective-permute-done.7.refs_2_ = bf16[2,64,128]{2,1,0:T(8,128)(2,1)S(1)} collective-permute-done((bf16[2,64,128]{2,1,0:T(8,128)(2,1)S(1)}, bf16[2,64,128]{2,1,0:T(8,128)(2,1)S(1)}, u32[]{:S(2)}, u32[]{:S(2)}) %collective-permute-start.7) | collective-permute-done | bytes 32800 | tf_op jit(solution)/shard_map/ppermute | solution.py:154
  29.0 0.7 %shard_map.91 = (f32[9,64,128]{2,1,0:T(8,128)}, f32[9,64,128]{2,1,0:T(8,128)}, bf16[128,512]{1,0:T(8,128)(2,1)}) custom-call(f32[9,64,128]{2,1,0:T(8,128)} %get-tuple-element.18.first_in_ref, f32[9,64,128]{2,1,0:T(8,128)} %get-tuple-element.19.second_in_ref, ...), custom_call_target="tpu_custom_call", output_to_operand_aliasing={{0}: (0, {}), {1}: (1, {})} | custom-call | tf_op jit(solution)/shard_map/pallas_call | solution.py:466
  (4 shorter events, 0.0 us)
Async XLA Ops:
  0.6 10.4 %copy-start = (bf16[128,512]{1,0:T(8,128)(2,1)S(1)}, bf16[128,512]{1,0:T(8,128)(2,1)}, u32[]{:S(2)}) copy-start(bf16[128,512]{1,0:T(8,128)(2,1)} %own_ref.3) | copy-start | bytes 393220
  0.6 16.3 %copy-start.1 = (bf16[512,5]{0,1:T(8,128)(2,1)S(1)}, bf16[512,5]{0,1:T(8,128)(2,1)}, u32[]{:S(2)}) copy-start(bf16[512,5]{0,1:T(8,128)(2,1)} %param.11) | copy-start | bytes 15364
  1.7 9.3 %collective-permute-start.3 = (bf16[2,512,128]{2,1,0:T(8,128)(2,1)S(1)}, bf16[2,512,128]{2,1,0:T(8,128)(2,1)S(1)}, u32[]{:S(2)}, u32[]{:S(2)}) collective-permute-start(bf16[2,512,128]{2,1,0:T(8,128)(2,1)S(1)} %shard_map.87.refs_0_), channel_id=1, source_target_pairs={{0,2},{1,3},{2,0},{3,1},{4,6},{5,7},{6,4},{7,5},{8,10},{9,11},{10,... | collective-permute-start | bytes 786440 | tf_op jit(solution)/shard_map/ppermute | solution.py:149
  4.7 12.2 %collective-permute-start.2 = (bf16[2,512,128]{2,1,0:T(8,128)(2,1)S(1)}, bf16[2,512,128]{2,1,0:T(8,128)(2,1)S(1)}, u32[]{:S(2)}, u32[]{:S(2)}) collective-permute-start(bf16[2,512,128]{2,1,0:T(8,128)(2,1)S(1)} %shard_map.87.refs_0_), channel_id=1, source_target_pairs={{0,1},{1,0},{2,3},{3,2},{4,5},{5,4},{6,7},{7,6},{8,9},{9,8},{10,11... | collective-permute-start | bytes 786440 | tf_op jit(solution)/shard_map/ppermute | solution.py:149
  11.0 6.9 %collective-permute-start.4 = (bf16[2,512,128]{2,1,0:T(8,128)(2,1)S(1)}, bf16[2,512,128]{2,1,0:T(8,128)(2,1)S(1)}, u32[]{:S(2)}, u32[]{:S(2)}) collective-permute-start(bf16[2,512,128]{2,1,0:T(8,128)(2,1)S(1)} %collective-permute-done.3.refs_2_), channel_id=1, source_target_pairs={{0,1},{1,0},{2,3},{3,2},{4,5},{5,4},{6,7},{7,6},{8,9},{9,8},{10,11... | collective-permute-start | bytes 786440 | tf_op jit(solution)/shard_map/ppermute | solution.py:149
  11.0 5.9 %collective-permute-start = (bf16[128,512]{1,0:T(8,128)(2,1)S(1)}, bf16[128,512]{1,0:T(8,128)(2,1)S(1)}, u32[]{:S(2)}, u32[]{:S(2)}) collective-permute-start(bf16[128,512]{1,0:T(8,128)(2,1)S(1)} %copy-done), channel_id=1, source_target_pairs={{0,4},{4,0},{8,12},{12,8},{16,20},{20,16},{24,28},{28,24},{1,5},{5... | collective-permute-start | bytes 393224 | tf_op jit(solution)/shard_map/ppermute | solution.py:149
  14.1 3.8 %collective-permute-start.1 = (bf16[16,128]{1,0:T(8,128)(2,1)S(1)}, bf16[16,128]{1,0:T(8,128)(2,1)S(1)}, u32[]{:S(2)}, u32[]{:S(2)}) collective-permute-start(bf16[16,128]{1,0:T(8,128)(2,1)S(1)} %shard_map.86.own_targets_ref), channel_id=1, source_target_pairs={{0,4},{4,0},{8,12},{12,8},{16,20},{20,16},{24,28},{28,24},{1,5},{5... | collective-permute-start | bytes 12296 | tf_op jit(solution)/shard_map/ppermute | solution.py:149
  20.6 7.5 %collective-permute-start.5 = (bf16[2,64,128]{2,1,0:T(8,128)(2,1)S(1)}, bf16[2,64,128]{2,1,0:T(8,128)(2,1)S(1)}, u32[]{:S(2)}, u32[]{:S(2)}) collective-permute-start(bf16[2,64,128]{2,1,0:T(8,128)(2,1)S(1)} %get-tuple-element.27), channel_id=1, source_target_pairs={{0,8},{4,12},{8,16},{12,20},{16,24},{20,28},{24,0},{28,4},{1,9},{5... | collective-permute-start | bytes 98312 | tf_op jit(solution)/shard_map/ppermute | solution.py:154
  22.5 5.7 %collective-permute-start.6 = (bf16[2,64,128]{2,1,0:T(8,128)(2,1)S(1)}, bf16[2,64,128]{2,1,0:T(8,128)(2,1)S(1)}, u32[]{:S(2)}, u32[]{:S(2)}) collective-permute-start(bf16[2,64,128]{2,1,0:T(8,128)(2,1)S(1)} %get-tuple-element.28), channel_id=1, source_target_pairs={{0,16},{4,20},{8,24},{12,28},{16,0},{20,4},{24,8},{28,12},{1,17},{... | collective-permute-start | bytes 98312 | tf_op jit(solution)/shard_map/ppermute | solution.py:154
  25.1 3.9 %collective-permute-start.7 = (bf16[2,64,128]{2,1,0:T(8,128)(2,1)S(1)}, bf16[2,64,128]{2,1,0:T(8,128)(2,1)S(1)}, u32[]{:S(2)}, u32[]{:S(2)}) collective-permute-start(bf16[2,64,128]{2,1,0:T(8,128)(2,1)S(1)} %get-tuple-element.29), channel_id=1, source_target_pairs={{0,24},{4,28},{8,0},{12,4},{16,8},{20,12},{24,16},{28,20},{1,25},{... | collective-permute-start | bytes 98312 | tf_op jit(solution)/shard_map/ppermute | solution.py:154

commit v2 on v1

--- a/solution.py
+++ b/solution.py
@@ -149,24 +149,28 @@
     return lax.ppermute(block, axis, [(i, i ^ offset) for i in range(lax.axis_size(axis))])
 
 
-def turn_pairs(block, axis, turn):
-    count = lax.axis_size(axis)
-    return lax.ppermute(block, axis, [(i, (i + 2 * turn) % count) for i in range(count)])
-
-
 def block_at(me, offset, width):
     return pl.ds(pl.multiple_of((me ^ offset) * width, width), width)
 
 
-def own_order(me, ref, rows, count):
-    width = ref.shape[1] // count
-    return jnp.concatenate([ref[rows, block_at(me, o, width)] for o in range(count)], axis=1)
-
-
-def matrices_body(centre_tap, first_ref, second_ref, both_ref, sems):
+def stacked(blocks, axis):
+    return blocks[0] if len(blocks) == 1 else jnp.concatenate(blocks, axis=axis)
+
+
+def own_order(me, refs, count):
+    width = refs[0].shape[1] // count
+    return stacked(
+        [stacked([ref[:, block_at(me, o, width)] for o in range(count)], 1) for ref in refs], 0
+    )
+
+
+def first_copies_body(centre_tap, where_ref, first_ref, second_ref, source_ref, both_ref, share_ref, sems):
+    share = share_ref.shape[0]
+    start = pl.multiple_of(lax.rem(where_ref[0], 2) * share, share)
     copies = [
-        pltpu.make_async_copy(ref.at[centre_tap], both_ref.at[slot], sems.at[slot])
-        for slot, ref in enumerate((first_ref, second_ref))
+        pltpu.make_async_copy(first_ref.at[centre_tap], both_ref.at[0], sems.at[0]),
+        pltpu.make_async_copy(second_ref.at[centre_tap], both_ref.at[1], sems.at[1]),
+        pltpu.make_async_copy(source_ref.at[pl.ds(start, share)], share_ref, sems.at[2]),
     ]
     for copy in copies:
         copy.start()
@@ -174,7 +178,7 @@
         copy.wait()
 
 
-def targets_body(where_ref, mask_ref, ids_ref, targets_ref, mask_at, ids_at, sems):
+def targets_body(where_ref, mask_ref, ids_ref, own_ref, sent_ref, mask_at, ids_at, sems):
     copies = [
         pltpu.make_async_copy(mask_ref, mask_at, sems.at[0]),
         pltpu.make_async_copy(ids_ref, ids_at, sems.at[1]),
@@ -183,21 +187,21 @@
         copy.start()
     for copy in copies:
         copy.wait()
-    positions = lax.broadcasted_iota(jnp.int32, ids_at.shape, 1) + where_ref[1] * ids_at.shape[1]
+    rows = ids_at.shape[1]
+    positions = lax.broadcasted_iota(jnp.int32, ids_at.shape, 1) + where_ref[1] * rows
     masked = jnp.zeros(ids_at.shape, jnp.int32)
     for entry in range(mask_at.shape[0]):
         masked = jnp.where(positions == mask_at[entry], 1, masked)
     targets = jnp.where(masked == 1, ids_at[...], -1).astype(jnp.float32)
-    targets_ref[...] = jnp.broadcast_to(targets, targets_ref.shape).astype(jnp.bfloat16)
+    targets = jnp.broadcast_to(targets, own_ref.shape)
+    turned = pltpu.roll(targets, rows // 2, 1)
+    own_ref[...] = targets.astype(jnp.bfloat16)
+    sent_ref[...] = jnp.where(lax.rem(where_ref[0], 2) == 1, turned, targets).astype(jnp.bfloat16)
 
 
 def blank_body(first_ref, second_ref):
     first_ref[...] = jnp.zeros_like(first_ref)
     second_ref[...] = jnp.zeros_like(second_ref)
-
-
-def stacked(blocks, axis):
-    return blocks[0] if len(blocks) == 1 else jnp.concatenate(blocks, axis=axis)
 
 
 def columns_of(me, matrix_refs, slot, count):
@@ -211,27 +215,23 @@
     )
 
 
-def early_body(count, where_ref, own_ref, peer_ref, head_ref, *refs):
+def early_body(count, where_ref, own_ref, far_ref, near_ref, head_ref, *refs):
     matrix_refs = refs[:-4]
     activation_ref, slope_ref, flip_ref, head_out_ref = refs[-4:]
     me = where_ref[0]
     half = own_ref.shape[0]
     weights = columns_of(me, matrix_refs, 0, count)
-    for part, ref in enumerate((own_ref, peer_ref)):
-        rows = pl.ds(part * half, half)
-        conv_out = dot(own_order(me, ref, pl.ds(0, half), count), weights)
+    for part, source_refs in enumerate(((own_ref,), (far_ref, near_ref))):
+        rows = pl.ds(part * half, half)
+        conv_out = dot(own_order(me, source_refs, count), weights)
         activation_ref[rows, :], slope_ref[rows, :] = gelu_and_slope(conv_out)
-        flip_ref[:, rows] = ref[...].T
+        flip_ref[:, rows] = stacked([ref[...] for ref in source_refs], 0).T
     head_out_ref[...] = jnp.zeros_like(head_out_ref)
     classes = head_ref.shape[0]
-    head_out_ref[0:classes, :] = own_order(me, head_ref, pl.ds(0, classes), count)
-
-
-def owner_of(block, blocks, turn):
-    return lax.rem(lax.div(block, 2) + turn, blocks // 2) * 2 + lax.rem(block, 2)
-
-
-def main_body(count, blocks, classes, where_ref, own_ref, peer_ref, own_targets_ref, peer_targets_ref, activation_ref, slope_ref, source_flip_ref, head_ref, *refs):
+    head_out_ref[0:classes, :] = own_order(me, (head_ref,), count)
+
+
+def main_body(count, blocks, classes, where_ref, own_ref, far_ref, near_ref, own_targets_ref, peer_targets_ref, activation_ref, slope_ref, source_flip_ref, head_ref, *refs):
     turns = blocks // 2
     matrix_refs, refs = refs[:count], refs[count:]
     self_ref, sent_refs, refs = refs[0], refs[1:turns], refs[turns:]
@@ -240,7 +240,7 @@
     me, block = where_ref[0], where_ref[1]
     half = own_ref.shape[0]
     _, depth, width = self_ref.shape
-    source_refs = (own_ref, peer_ref)
+    source_refs = ((own_ref,), (far_ref, near_ref))
     target_refs = (own_targets_ref, peer_targets_ref)
     late = columns_of(me, matrix_refs[-1:], 0, count)
     weights = columns_of(me, matrix_refs, 1, count)
@@ -248,7 +248,7 @@
 
     def first_block(part):
         rows = pl.ds(part * half, half)
-        source = own_order(me, source_refs[part], pl.ds(0, half), count)
+        source = own_order(me, source_refs[part], count)
         activation, gelu_slope = gelu_and_slope(dot(source, late))
         normed, inverse = norm_parts(jnp.concatenate([activation_ref[rows, :], activation], axis=1))
         scale_one_ref[rows, :] = jnp.concatenate([slope_ref[rows, :], gelu_slope], axis=1) * inverse
@@ -302,7 +302,7 @@
 
     def kernel_parts(flip_ref, slot):
         sources = [
-            flip_ref[pl.ds(pl.multiple_of(owner_of(block, blocks, turn) * depth, depth), depth), :]
+            flip_ref[pl.ds(pl.multiple_of((block ^ turn) * depth, depth), depth), :]
             for turn in range(turns)
         ]
         part = dot(stacked(sources, 0), grad_conv_ref[:, 0:width])
@@ -386,12 +386,12 @@
             cost_estimate=pl.CostEstimate(flops=flops, bytes_accessed=moved, transcendentals=0),
         )
 
-    (own,) = call(
-        functools.partial(matrices_body, centre_tap),
-        [hbm] * 2,
-        (shape((2, channels, width)),),
-        scratch=[pltpu.SemaphoreType.DMA((2,))],
-    )(in_hbm(first_kernel), in_hbm(second_kernel))
+    own, own_share = call(
+        functools.partial(first_copies_body, centre_tap),
+        [smem] + [hbm] * 3,
+        (shape((2, channels, width)), shape((rows // 2, channels))),
+        scratch=[pltpu.SemaphoreType.DMA((3,))],
+    )(where, in_hbm(first_kernel), in_hbm(second_kernel), in_hbm(hidden_entry_states))
     blocks = {0: own}
     bit = mp_count // 2
     while bit:
@@ -400,18 +400,20 @@
         bit //= 2
     blocks = [blocks[offset] for offset in range(mp_count)]
 
-    peer_rows = swap(hidden_entry_states, "seq", 1)
-    (own_targets,) = call(
+    apart = seq_count // 2
+    far_rows = swap(own_share, "seq", apart)
+    near_rows = swap(far_rows, "mp", 1)
+    own_targets, sent_targets = call(
         targets_body,
         [smem] + [hbm] * 2,
-        (shape((SIDE_ROWS, rows)),),
+        (shape((SIDE_ROWS, rows)),) * 2,
         scratch=[
             pltpu.SMEM(mask_index.shape, jnp.int32),
             pltpu.VMEM((1, rows), jnp.int32),
             pltpu.SemaphoreType.DMA((2,)),
         ],
     )(where, in_hbm(mask_index), in_hbm(base_ids[None, :]))
-    peer_targets = swap(own_targets, "seq", 1)
+    peer_targets = swap(sent_targets, "seq", apart)
     whole = shape((tap_count, depth, width), jnp.float32)
     first_grad, second_grad = call(blank_body, [], (whole, whole))()
 
@@ -420,7 +422,7 @@
     product = 2 * pair_rows * channels * channels
     activation, slope, source_flip, head = call(
         functools.partial(early_body, mp_count),
-        [smem] + [vmem] * (2 + mp_count),
+        [smem] + [vmem] * (3 + mp_count),
         (
             shape((pair_rows, early), jnp.float32),
             shape((pair_rows, early), jnp.float32),
@@ -429,13 +431,13 @@
         ),
         flops=product,
         moved=8 * pair_rows * channels,
-    )(where, hidden_entry_states, peer_rows, head_weight.T, *blocks[:-1])
+    )(where, hidden_entry_states, far_rows, near_rows, head_weight.T, *blocks[:-1])
 
     turns = seq_count // 2
     part = (2, depth, width)
     outs = call(
         functools.partial(main_body, mp_count, seq_count, classes),
-        [smem] + [vmem] * (8 + mp_count),
+        [smem] + [vmem] * (9 + mp_count),
         (shape(part, jnp.float32),)
         + (shape(part),) * (turns - 1)
         + (shape((rows, channels), jnp.float32), shape((rows, channels))),
@@ -452,10 +454,10 @@
         ],
         flops=3 * product,
         moved=16 * pair_rows * channels,
-    )(where, hidden_entry_states, peer_rows, own_targets, peer_targets, activation, slope, source_flip, head, *blocks)
+    )(where, hidden_entry_states, far_rows, near_rows, own_targets, peer_targets, activation, slope, source_flip, head, *blocks)
     own_part, sent, (grad_one, grad_conv) = outs[0], outs[1:-2], outs[-2:]
 
-    received = [turn_pairs(piece, "seq", turn) for turn, piece in enumerate(sent, 1)]
+    received = [swap(piece, "seq", turn) for turn, piece in enumerate(sent, 1)]
     (input_grad,) = call(
         functools.partial(input_grad_body, mp_count),
         [smem] + [vmem] * (2 + mp_count),

time: 29.8 us -> 35.7 us (1.20)
  waiting for transfers between devices: 9.69 us -> 15.1 us
  Pallas kernels: 8.21 us -> 8.82 us
    ppermute x5 -> x9, waiting for transfers between devices: 8.83 us -> 15.1 us  [swap(): lax.ppermute(block, axis, [(i, i ^ offset) for i in range(lax.axis_size(a...]
    ppermute x3 -> x0, starting transfers between devices: 5.83 us -> none  [turn_pairs(): lax.ppermute(block, axis, [(i, (i + 2 * turn) % count) for i in range(cou...]
    ppermute x5 -> x9, starting transfers between devices: 5.13 us -> 10.8 us  [swap(): lax.ppermute(block, axis, [(i, i ^ offset) for i in range(lax.axis_size(a...]
    ppermute x3 -> x0, waiting for transfers between devices: 0.86 us -> none  [turn_pairs(): lax.ppermute(block, axis, [(i, (i + 2 * turn) % count) for i in range(cou...]
    pallas_call x3, Pallas kernels: 3.16 us -> 3.75 us  [the longest x1 1.53 us: local_plan(): call(functools.partial(first_copies_body, centre_tap), [smem] + [hbm] * 3...]
  transfers between devices with their start and end apart: 8 -> 9, of which waited for: 3 -> 5; matrix products, arithmetic and copies ran while one was open for 0% -> 0% of each run, Pallas kernels for 13% -> 11%
where the time goes in v2:
time: 35.7 us; the launch traced here: 35.5 us
  waiting for transfers between devices  15.1 us (42%)
  starting transfers between devices  10.8 us (30%)
  Pallas kernels  8.82 us (25%)
  between operations  0.7 us (2%)
    ppermute x9, waiting for transfers between devices, swap(): lax.ppermute(block, axis, [(i, i ^ offset) for i in range(lax.axis_size(a...  15.1 us
    ppermute x9, starting transfers between devices, swap(): lax.ppermute(block, axis, [(i, i ^ offset) for i in range(lax.axis_size(a...  10.8 us
    pallas_call x1, Pallas kernels, local_plan(): call(functools.partial(main_body, mp_count, seq_count, classes), [smem] +...  2.67 us
    pallas_call x1, Pallas kernels, local_plan(): call(functools.partial(first_copies_body, centre_tap), [smem] + [hbm] * 3...  1.53 us
    pallas_call x1, Pallas kernels, local_plan(): call(targets_body, [smem] + [hbm] * 2, (shape((SIDE_ROWS, rows)),) * 2, s...  1.31 us
    pallas_call x1, Pallas kernels, local_plan(): call(functools.partial(early_body, mp_count), [smem] + [vmem] * (3 + mp_c...  0.91 us
    pallas_call x1, Pallas kernels, local_plan(): call(functools.partial(input_grad_body, mp_count), [smem] + [vmem] * (2 +...  0.87 us
    pallas_call x1, Pallas kernels, local_plan(): first_grad, second_grad = call(blank_body, [], (whole, whole))()  0.83 us
  transfers between devices with their start and end apart: 9, of which 5 were waited for; matrix products, arithmetic and copies ran while one was open for 0% of the time, Pallas kernels for 11%

profile of v2, /device:TPU:0, one launch (start us, length us, event | category | flops | bytes accessed | tf_op | source)
XLA Modules:
  0.0 35.5 jit_solution(14592564991390553851)
XLA Ops:
  0.6 0.1 pad_add_fusion.where_ref
  0.7 1.5 %shard_map.86 = (bf16[2,512,128]{2,1,0:T(8,128)(2,1)S(1)}, bf16[64,512]{1,0:T(8,128)(2,1)S(1)}) custom-call(s32[2]{0:T(128)S(1)} %pad_add_fusion.where_ref, bf16[9,512,128]{2,1,0:T(8,128)(2,1)} %first_ref.1, bf16[9,512,128]{2,1,0:T(8,128)(2,1)} %second_ref.1, bf16[128,512]{1,0:T(8,128)(2,1)} %own_ref.3), custom_call_target="tpu_custom_call" | custom-call | tf_op jit(solution)/shard_map/pallas_call | solution.py:389
  2.3 3.0 %collective-permute-start.4 = (bf16[2,512,128]{2,1,0:T(8,128)(2,1)S(1)}, bf16[2,512,128]{2,1,0:T(8,128)(2,1)S(1)}, u32[]{:S(2)}, u32[]{:S(2)}) collective-permute-start(bf16[2,512,128]{2,1,0:T(8,128)(2,1)S(1)} %get-tuple-element.27.refs_0_), channel_id=1, source_target_pairs={{0,2},{1,3},{2,0},{3,1},{4,6},{5,7},{6,4},{7,5},{8,10},{9,11},{10,... | collective-permute-start | bytes 786440 | tf_op jit(solution)/shard_map/ppermute | solution.py:149
  5.3 0.0 collective-permute-start.3
  5.3 6.3 %collective-permute-done.4.refs_2_ = bf16[2,512,128]{2,1,0:T(8,128)(2,1)S(1)} collective-permute-done((bf16[2,512,128]{2,1,0:T(8,128)(2,1)S(1)}, bf16[2,512,128]{2,1,0:T(8,128)(2,1)S(1)}, u32[]{:S(2)}, u32[]{:S(2)}) %collective-permute-start.4) | collective-permute-done | bytes 262176 | tf_op jit(solution)/shard_map/ppermute | solution.py:149
  11.6 0.0 collective-permute-start.5
  11.6 2.8 %collective-permute-start = (bf16[64,512]{1,0:T(8,128)(2,1)S(1)}, bf16[64,512]{1,0:T(8,128)(2,1)S(1)}, u32[]{:S(2)}, u32[]{:S(2)}) collective-permute-start(bf16[64,512]{1,0:T(8,128)(2,1)S(1)} %get-tuple-element.24), channel_id=1, source_target_pairs={{0,16},{4,20},{8,24},{12,28},{16,0},{20,4},{24,8},{28,12},{1,17},{... | collective-permute-start | bytes 196616 | tf_op jit(solution)/shard_map/ppermute | solution.py:149
  14.4 4.2 %collective-permute-done.far_ref = bf16[64,512]{1,0:T(8,128)(2,1)S(1)} collective-permute-done((bf16[64,512]{1,0:T(8,128)(2,1)S(1)}, bf16[64,512]{1,0:T(8,128)(2,1)S(1)}, u32[]{:S(2)}, u32[]{:S(2)}) %collective-permute-start) | collective-permute-done | bytes 65568 | tf_op jit(solution)/shard_map/ppermute | solution.py:149
  18.6 1.3 %shard_map.87 = (bf16[16,128]{1,0:T(8,128)(2,1)S(1)}, bf16[16,128]{1,0:T(8,128)(2,1)S(1)}) custom-call(s32[2]{0:T(128)S(1)} %pad_add_fusion.where_ref, s32[16]{0:T(128)} %mask_ref.1, s32[1,128]{1,0:T(1,128)} %bitcast.5), custom_call_target="tpu_custom_call" | custom-call | tf_op jit(solution)/shard_map/pallas_call | solution.py:406
  19.9 1.4 %collective-permute-start.2 = (bf16[16,128]{1,0:T(8,128)(2,1)S(1)}, bf16[16,128]{1,0:T(8,128)(2,1)S(1)}, u32[]{:S(2)}, u32[]{:S(2)}) collective-permute-start(bf16[16,128]{1,0:T(8,128)(2,1)S(1)} %get-tuple-element.26), channel_id=1, source_target_pairs={{0,16},{4,20},{8,24},{12,28},{16,0},{20,4},{24,8},{28,12},{1,17},{... | collective-permute-start | bytes 12296 | tf_op jit(solution)/shard_map/ppermute | solution.py:149
  21.3 0.0 collective-permute-done.1.near_ref
  21.3 0.0 collective-permute-done.3.refs_1_
  21.3 0.9 %shard_map.88 = (f32[256,384]{1,0:T(8,128)S(1)}, f32[256,384]{1,0:T(8,128)S(1)}, bf16[512,256]{1,0:T(8,128)(2,1)S(1)}, bf16[16,512]{1,0:T(8,128)(2,1)S(1)}) custom-call(s32[2]{0:T(128)S(1)} %pad_add_fusion.where_ref, bf16[128,512]{1,0:T(8,128)(2,1)S(1)} %copy-done, bf16[64,512]{1,0:T(8,128)(2,1)S(1)} %collective-permute-done.far_ref, ...), custom_call_target="tpu_custom_call" | custom-call | flops 134217728 | bytes 1048576 | tf_op jit(solution)/shard_map/pallas_call | solution.py:423
  22.3 2.2 %collective-permute-done.2.peer_targets_ref = bf16[16,128]{1,0:T(8,128)(2,1)S(1)} collective-permute-done((bf16[16,128]{1,0:T(8,128)(2,1)S(1)}, bf16[16,128]{1,0:T(8,128)(2,1)S(1)}, u32[]{:S(2)}, u32[]{:S(2)}) %collective-permute-start.2) | collective-permute-done | bytes 4128 | tf_op jit(solution)/shard_map/ppermute | solution.py:149
  24.5 2.7 %shard_map.89 = (f32[2,64,128]{2,1,0:T(8,128)S(1)}, bf16[2,64,128]{2,1,0:T(8,128)(2,1)S(1)}, bf16[2,64,128]{2,1,0:T(8,128)(2,1)S(1)}, bf16[2,64,128]{2,1,0:T(8,1...) custom-call(s32[2]{0:T(128)S(1)} %pad_add_fusion.where_ref, bf16[128,512]{1,0:T(8,128)(2,1)S(1)} %copy-done, ...), custom_call_target="tpu_custom_call" | custom-call | flops 402653184 | bytes 2097152 | tf_op jit(solution)/shard_map/pallas_call | solution.py:438
  27.2 1.6 %collective-permute-start.6 = (bf16[2,64,128]{2,1,0:T(8,128)(2,1)S(1)}, bf16[2,64,128]{2,1,0:T(8,128)(2,1)S(1)}, u32[]{:S(2)}, u32[]{:S(2)}) collective-permute-start(bf16[2,64,128]{2,1,0:T(8,128)(2,1)S(1)} %get-tuple-element.35), channel_id=1, source_target_pairs={{0,4},{4,0},{8,12},{12,8},{16,20},{20,16},{24,28},{28,24},{1,5},{5... | collective-permute-start | bytes 98312 | tf_op jit(solution)/shard_map/ppermute | solution.py:149
  28.8 1.2 %collective-permute-start.7 = (bf16[2,64,128]{2,1,0:T(8,128)(2,1)S(1)}, bf16[2,64,128]{2,1,0:T(8,128)(2,1)S(1)}, u32[]{:S(2)}, u32[]{:S(2)}) collective-permute-start(bf16[2,64,128]{2,1,0:T(8,128)(2,1)S(1)} %get-tuple-element.36), channel_id=1, source_target_pairs={{0,8},{4,12},{8,0},{12,4},{16,24},{20,28},{24,16},{28,20},{1,9},{5... | collective-permute-start | bytes 98312 | tf_op jit(solution)/shard_map/ppermute | solution.py:149
  30.0 0.7 %collective-permute-start.8 = (bf16[2,64,128]{2,1,0:T(8,128)(2,1)S(1)}, bf16[2,64,128]{2,1,0:T(8,128)(2,1)S(1)}, u32[]{:S(2)}, u32[]{:S(2)}) collective-permute-start(bf16[2,64,128]{2,1,0:T(8,128)(2,1)S(1)} %get-tuple-element.37), channel_id=1, source_target_pairs={{0,12},{4,8},{8,4},{12,0},{16,28},{20,24},{24,20},{28,16},{1,13},{... | collective-permute-start | bytes 98312 | tf_op jit(solution)/shard_map/ppermute | solution.py:149
  30.7 0.8 %shard_map.85 = (f32[9,64,128]{2,1,0:T(8,128)}, f32[9,64,128]{2,1,0:T(8,128)}) custom-call(), custom_call_target="tpu_custom_call" | custom-call | tf_op jit(solution)/shard_map/pallas_call | solution.py:418
  31.6 0.9 %shard_map.90.input_grad_ref = bf16[128,512]{1,0:T(8,128)(2,1)S(1)} custom-call(s32[2]{0:T(128)S(1)} %pad_add_fusion.where_ref, f32[128,512]{1,0:T(8,128)S(1)} %get-tuple-element.32.grad_ref, bf16[128,512]{1,0:T(8,128)(2,1)S(1)} %get-tuple-element.33.grad_conv_ref, bf16[2,512,128]{2,1,0:T(8,128)(2,1)S(1)} %get-tuple-element.27.refs_0_, ...), custom_call_target="tpu_custom_call" | custom-call | flops 67108864 | bytes 524288 | tf_op jit(solution)/shard_map/pallas_call | solution.py:461
  32.4 0.0 collective-permute-done.6.refs_0_
  32.4 0.3 collective-permute-done.7.refs_1_
  32.7 2.1 %collective-permute-done.8.refs_2_ = bf16[2,64,128]{2,1,0:T(8,128)(2,1)S(1)} collective-permute-done((bf16[2,64,128]{2,1,0:T(8,128)(2,1)S(1)}, bf16[2,64,128]{2,1,0:T(8,128)(2,1)S(1)}, u32[]{:S(2)}, u32[]{:S(2)}) %collective-permute-start.8) | collective-permute-done | bytes 32800 | tf_op jit(solution)/shard_map/ppermute | solution.py:149
  34.8 0.7 %shard_map.91 = (f32[9,64,128]{2,1,0:T(8,128)}, f32[9,64,128]{2,1,0:T(8,128)}, bf16[128,512]{1,0:T(8,128)(2,1)}) custom-call(f32[9,64,128]{2,1,0:T(8,128)} %get-tuple-element.22.first_in_ref, f32[9,64,128]{2,1,0:T(8,128)} %get-tuple-element.23.second_in_ref, ...), custom_call_target="tpu_custom_call", output_to_operand_aliasing={{0}: (0, {}), {1}: (1, {})} | custom-call | tf_op jit(solution)/shard_map/pallas_call | solution.py:468
  (6 shorter events, 0.0 us)
Async XLA Ops:
  0.7 20.6 %copy-start = (bf16[128,512]{1,0:T(8,128)(2,1)S(1)}, bf16[128,512]{1,0:T(8,128)(2,1)}, u32[]{:S(2)}) copy-start(bf16[128,512]{1,0:T(8,128)(2,1)} %own_ref.3) | copy-start | bytes 393220
  0.7 20.6 %copy-start.1 = (bf16[512,5]{0,1:T(8,128)(2,1)S(1)}, bf16[512,5]{0,1:T(8,128)(2,1)}, u32[]{:S(2)}) copy-start(bf16[512,5]{0,1:T(8,128)(2,1)} %param.11) | copy-start | bytes 15364
  2.3 9.3 %collective-permute-start.4 = (bf16[2,512,128]{2,1,0:T(8,128)(2,1)S(1)}, bf16[2,512,128]{2,1,0:T(8,128)(2,1)S(1)}, u32[]{:S(2)}, u32[]{:S(2)}) collective-permute-start(bf16[2,512,128]{2,1,0:T(8,128)(2,1)S(1)} %get-tuple-element.27.refs_0_), channel_id=1, source_target_pairs={{0,2},{1,3},{2,0},{3,1},{4,6},{5,7},{6,4},{7,5},{8,10},{9,11},{10,... | collective-permute-start | bytes 786440 | tf_op jit(solution)/shard_map/ppermute | solution.py:149
  5.3 16.0 %collective-permute-start.3 = (bf16[2,512,128]{2,1,0:T(8,128)(2,1)S(1)}, bf16[2,512,128]{2,1,0:T(8,128)(2,1)S(1)}, u32[]{:S(2)}, u32[]{:S(2)}) collective-permute-start(bf16[2,512,128]{2,1,0:T(8,128)(2,1)S(1)} %get-tuple-element.27.refs_0_), channel_id=1, source_target_pairs={{0,1},{1,0},{2,3},{3,2},{4,5},{5,4},{6,7},{7,6},{8,9},{9,8},{10,11... | collective-permute-start | bytes 786440 | tf_op jit(solution)/shard_map/ppermute | solution.py:149
  11.6 12.9 %collective-permute-start.5 = (bf16[2,512,128]{2,1,0:T(8,128)(2,1)S(1)}, bf16[2,512,128]{2,1,0:T(8,128)(2,1)S(1)}, u32[]{:S(2)}, u32[]{:S(2)}) collective-permute-start(bf16[2,512,128]{2,1,0:T(8,128)(2,1)S(1)} %collective-permute-done.4.refs_2_), channel_id=1, source_target_pairs={{0,1},{1,0},{2,3},{3,2},{4,5},{5,4},{6,7},{7,6},{8,9},{9,8},{10,11... | collective-permute-start | bytes 786440 | tf_op jit(solution)/shard_map/ppermute | solution.py:149
  11.6 7.0 %collective-permute-start = (bf16[64,512]{1,0:T(8,128)(2,1)S(1)}, bf16[64,512]{1,0:T(8,128)(2,1)S(1)}, u32[]{:S(2)}, u32[]{:S(2)}) collective-permute-start(bf16[64,512]{1,0:T(8,128)(2,1)S(1)} %get-tuple-element.24), channel_id=1, source_target_pairs={{0,16},{4,20},{8,24},{12,28},{16,0},{20,4},{24,8},{28,12},{1,17},{... | collective-permute-start | bytes 196616 | tf_op jit(solution)/shard_map/ppermute | solution.py:149
  18.6 2.7 %collective-permute-start.1 = (bf16[64,512]{1,0:T(8,128)(2,1)S(1)}, bf16[64,512]{1,0:T(8,128)(2,1)S(1)}, u32[]{:S(2)}, u32[]{:S(2)}) collective-permute-start(bf16[64,512]{1,0:T(8,128)(2,1)S(1)} %collective-permute-done.far_ref), channel_id=1, source_target_pairs={{0,1},{1,0},{2,3},{3,2},{4,5},{5,4},{6,7},{7,6},{8,9},{9,8},{10,11... | collective-permute-start | bytes 196616 | tf_op jit(solution)/shard_map/ppermute | solution.py:149
  19.9 4.6 %collective-permute-start.2 = (bf16[16,128]{1,0:T(8,128)(2,1)S(1)}, bf16[16,128]{1,0:T(8,128)(2,1)S(1)}, u32[]{:S(2)}, u32[]{:S(2)}) collective-permute-start(bf16[16,128]{1,0:T(8,128)(2,1)S(1)} %get-tuple-element.26), channel_id=1, source_target_pairs={{0,16},{4,20},{8,24},{12,28},{16,0},{20,4},{24,8},{28,12},{1,17},{... | collective-permute-start | bytes 12296 | tf_op jit(solution)/shard_map/ppermute | solution.py:149
  27.2 5.3 %collective-permute-start.6 = (bf16[2,64,128]{2,1,0:T(8,128)(2,1)S(1)}, bf16[2,64,128]{2,1,0:T(8,128)(2,1)S(1)}, u32[]{:S(2)}, u32[]{:S(2)}) collective-permute-start(bf16[2,64,128]{2,1,0:T(8,128)(2,1)S(1)} %get-tuple-element.35), channel_id=1, source_target_pairs={{0,4},{4,0},{8,12},{12,8},{16,20},{20,16},{24,28},{28,24},{1,5},{5... | collective-permute-start | bytes 98312 | tf_op jit(solution)/shard_map/ppermute | solution.py:149
  28.8 3.9 %collective-permute-start.7 = (bf16[2,64,128]{2,1,0:T(8,128)(2,1)S(1)}, bf16[2,64,128]{2,1,0:T(8,128)(2,1)S(1)}, u32[]{:S(2)}, u32[]{:S(2)}) collective-permute-start(bf16[2,64,128]{2,1,0:T(8,128)(2,1)S(1)} %get-tuple-element.36), channel_id=1, source_target_pairs={{0,8},{4,12},{8,0},{12,4},{16,24},{20,28},{24,16},{28,20},{1,9},{5... | collective-permute-start | bytes 98312 | tf_op jit(solution)/shard_map/ppermute | solution.py:149
  30.0 4.8 %collective-permute-start.8 = (bf16[2,64,128]{2,1,0:T(8,128)(2,1)S(1)}, bf16[2,64,128]{2,1,0:T(8,128)(2,1)S(1)}, u32[]{:S(2)}, u32[]{:S(2)}) collective-permute-start(bf16[2,64,128]{2,1,0:T(8,128)(2,1)S(1)} %get-tuple-element.37), channel_id=1, source_target_pairs={{0,12},{4,8},{8,4},{12,0},{16,28},{20,24},{24,20},{28,16},{1,13},{... | collective-permute-start | bytes 98312 | tf_op jit(solution)/shard_map/ppermute | solution.py:149

commit v3 on v2

--- a/solution.py
+++ b/solution.py
@@ -164,13 +164,10 @@
     )
 
 
-def first_copies_body(centre_tap, where_ref, first_ref, second_ref, source_ref, both_ref, share_ref, sems):
-    share = share_ref.shape[0]
-    start = pl.multiple_of(lax.rem(where_ref[0], 2) * share, share)
+def matrices_body(centre_tap, first_ref, second_ref, both_ref, sems):
     copies = [
-        pltpu.make_async_copy(first_ref.at[centre_tap], both_ref.at[0], sems.at[0]),
-        pltpu.make_async_copy(second_ref.at[centre_tap], both_ref.at[1], sems.at[1]),
-        pltpu.make_async_copy(source_ref.at[pl.ds(start, share)], share_ref, sems.at[2]),
+        pltpu.make_async_copy(ref.at[centre_tap], both_ref.at[slot], sems.at[slot])
+        for slot, ref in enumerate((first_ref, second_ref))
     ]
     for copy in copies:
         copy.start()
@@ -178,25 +175,24 @@
         copy.wait()
 
 
-def targets_body(where_ref, mask_ref, ids_ref, own_ref, sent_ref, mask_at, ids_at, sems):
-    copies = [
-        pltpu.make_async_copy(mask_ref, mask_at, sems.at[0]),
-        pltpu.make_async_copy(ids_ref, ids_at, sems.at[1]),
-    ]
-    for copy in copies:
-        copy.start()
-    for copy in copies:
-        copy.wait()
-    rows = ids_at.shape[1]
-    positions = lax.broadcasted_iota(jnp.int32, ids_at.shape, 1) + where_ref[1] * rows
-    masked = jnp.zeros(ids_at.shape, jnp.int32)
-    for entry in range(mask_at.shape[0]):
-        masked = jnp.where(positions == mask_at[entry], 1, masked)
-    targets = jnp.where(masked == 1, ids_at[...], -1).astype(jnp.float32)
+def prepare_body(mask_ref, ids_ref, source_ref, own_ref, sent_ref):
+    rows = source_ref.shape[0]
+    share = rows // 2
+    entries = mask_ref.shape[1]
+    part = lax.rem(lax.axis_index("mp"), 2)
+    square = (entries, entries)
+    diagonal = lax.broadcasted_iota(jnp.int32, square, 0) == lax.broadcasted_iota(jnp.int32, square, 1)
+    offsets = (mask_ref[...] - lax.axis_index("seq") * rows).astype(jnp.float32)
+    column = jnp.sum(jnp.where(diagonal, offsets, 0.0), axis=1, keepdims=True)
+    positions = lax.broadcasted_iota(jnp.int32, (entries, rows), 1).astype(jnp.float32)
+    masked = jnp.max((positions == column).astype(jnp.float32), axis=0, keepdims=True)
+    targets = jnp.where(masked > 0.0, ids_ref[...].astype(jnp.float32), -1.0)
     targets = jnp.broadcast_to(targets, own_ref.shape)
-    turned = pltpu.roll(targets, rows // 2, 1)
+    turned = pltpu.roll(targets, share, 1)
     own_ref[...] = targets.astype(jnp.bfloat16)
-    sent_ref[...] = jnp.where(lax.rem(where_ref[0], 2) == 1, turned, targets).astype(jnp.bfloat16)
+    sent_ref[0:share, :] = source_ref[pl.ds(pl.multiple_of(part * share, share), share), :]
+    sent_ref[share:, :] = jnp.zeros((SIDE_ROWS, source_ref.shape[1]), jnp.bfloat16)
+    sent_ref[share:, 0:rows] = jnp.where(part == 1, turned, targets).astype(jnp.bfloat16)
 
 
 def blank_body(first_ref, second_ref):
@@ -215,13 +211,18 @@
     )
 
 
-def early_body(count, where_ref, own_ref, far_ref, near_ref, head_ref, *refs):
+def row_halves(own_ref, far_ref, near_ref):
+    share = own_ref.shape[0] // 2
+    return ((own_ref,), (far_ref.at[0:share], near_ref.at[0:share]))
+
+
+def early_body(count, own_ref, far_ref, near_ref, head_ref, *refs):
     matrix_refs = refs[:-4]
     activation_ref, slope_ref, flip_ref, head_out_ref = refs[-4:]
-    me = where_ref[0]
+    me = lax.axis_index("mp")
     half = own_ref.shape[0]
     weights = columns_of(me, matrix_refs, 0, count)
-    for part, source_refs in enumerate(((own_ref,), (far_ref, near_ref))):
+    for part, source_refs in enumerate(row_halves(own_ref, far_ref, near_ref)):
         rows = pl.ds(part * half, half)
         conv_out = dot(own_order(me, source_refs, count), weights)
         activation_ref[rows, :], slope_ref[rows, :] = gelu_and_slope(conv_out)
@@ -231,17 +232,17 @@
     head_out_ref[0:classes, :] = own_order(me, (head_ref,), count)
 
 
-def main_body(count, blocks, classes, where_ref, own_ref, far_ref, near_ref, own_targets_ref, peer_targets_ref, activation_ref, slope_ref, source_flip_ref, head_ref, *refs):
+def main_body(count, blocks, classes, own_ref, far_ref, near_ref, own_targets_ref, activation_ref, slope_ref, source_flip_ref, head_ref, *refs):
     turns = blocks // 2
     matrix_refs, refs = refs[:count], refs[count:]
     self_ref, sent_refs, refs = refs[0], refs[1:turns], refs[turns:]
     grad_out_ref, grad_conv_out_ref = refs[:2]
     hidden_one_ref, normed_one_ref, scale_one_ref, hidden_flip_ref, normed_two_ref, scale_two_ref, hidden_two_ref, grad_ref, grad_conv_ref = refs[2:]
-    me, block = where_ref[0], where_ref[1]
+    me, block = lax.axis_index("mp"), lax.axis_index("seq")
     half = own_ref.shape[0]
     _, depth, width = self_ref.shape
-    source_refs = ((own_ref,), (far_ref, near_ref))
-    target_refs = (own_targets_ref, peer_targets_ref)
+    source_refs = row_halves(own_ref, far_ref, near_ref)
+    target_refs = (own_targets_ref, far_ref.at[half // 2 :, 0:half])
     late = columns_of(me, matrix_refs[-1:], 0, count)
     weights = columns_of(me, matrix_refs, 1, count)
     head = head_ref[...]
@@ -330,9 +331,9 @@
     grad_conv_out_ref[...] = grad_conv_ref[pl.ds(0, half), :]
 
 
-def input_grad_body(count, where_ref, grad_ref, grad_conv_ref, *refs):
+def input_grad_body(count, grad_ref, grad_conv_ref, *refs):
     matrix_refs, input_grad_ref = refs[:count], refs[count]
-    me = where_ref[0]
+    me = lax.axis_index("mp")
     width = matrix_refs[0].shape[2]
     total = grad_ref[...] + dot(grad_conv_ref[...], columns_of(me, matrix_refs, 0, count), NT)
     for offset in range(count):
@@ -362,10 +363,8 @@
     classes = head_weight.shape[1]
     centre_tap = tap_count // 2
     depth = channels // seq_count
-    where = jnp.stack([lax.axis_index("mp"), lax.axis_index("seq")]).astype(jnp.int32)
 
     vmem = pl.BlockSpec(memory_space=pltpu.VMEM)
-    smem = pl.BlockSpec(memory_space=pltpu.SMEM)
     hbm = pl.BlockSpec(memory_space=pltpu.HBM)
 
     def shape(dims, dtype=jnp.bfloat16):
@@ -386,12 +385,12 @@
             cost_estimate=pl.CostEstimate(flops=flops, bytes_accessed=moved, transcendentals=0),
         )
 
-    own, own_share = call(
-        functools.partial(first_copies_body, centre_tap),
-        [smem] + [hbm] * 3,
-        (shape((2, channels, width)), shape((rows // 2, channels))),
-        scratch=[pltpu.SemaphoreType.DMA((3,))],
-    )(where, in_hbm(first_kernel), in_hbm(second_kernel), in_hbm(hidden_entry_states))
+    (own,) = call(
+        functools.partial(matrices_body, centre_tap),
+        [hbm] * 2,
+        (shape((2, channels, width)),),
+        scratch=[pltpu.SemaphoreType.DMA((2,))],
+    )(in_hbm(first_kernel), in_hbm(second_kernel))
     blocks = {0: own}
     bit = mp_count // 2
     while bit:
@@ -400,20 +399,13 @@
         bit //= 2
     blocks = [blocks[offset] for offset in range(mp_count)]
 
-    apart = seq_count // 2
-    far_rows = swap(own_share, "seq", apart)
+    own_targets, sent_rows = call(
+        prepare_body,
+        [vmem] * 3,
+        (shape((SIDE_ROWS, rows)), shape((rows // 2 + SIDE_ROWS, channels))),
+    )(mask_index[None, :], base_ids[None, :], hidden_entry_states)
+    far_rows = swap(sent_rows, "seq", seq_count // 2)
     near_rows = swap(far_rows, "mp", 1)
-    own_targets, sent_targets = call(
-        targets_body,
-        [smem] + [hbm] * 2,
-        (shape((SIDE_ROWS, rows)),) * 2,
-        scratch=[
-            pltpu.SMEM(mask_index.shape, jnp.int32),
-            pltpu.VMEM((1, rows), jnp.int32),
-            pltpu.SemaphoreType.DMA((2,)),
-        ],
-    )(where, in_hbm(mask_index), in_hbm(base_ids[None, :]))
-    peer_targets = swap(sent_targets, "seq", apart)
     whole = shape((tap_count, depth, width), jnp.float32)
     first_grad, second_grad = call(blank_body, [], (whole, whole))()
 
@@ -422,7 +414,7 @@
     product = 2 * pair_rows * channels * channels
     activation, slope, source_flip, head = call(
         functools.partial(early_body, mp_count),
-        [smem] + [vmem] * (3 + mp_count),
+        [vmem] * (3 + mp_count),
         (
             shape((pair_rows, early), jnp.float32),
             shape((pair_rows, early), jnp.float32),
@@ -431,13 +423,13 @@
         ),
         flops=product,
         moved=8 * pair_rows * channels,
-    )(where, hidden_entry_states, far_rows, near_rows, head_weight.T, *blocks[:-1])
+    )(hidden_entry_states, far_rows, near_rows, head_weight.T, *blocks[:-1])
 
     turns = seq_count // 2
     part = (2, depth, width)
     outs = call(
         functools.partial(main_body, mp_count, seq_count, classes),
-        [smem] + [vmem] * (9 + mp_count),
+        [vmem] * (8 + mp_count),
         (shape(part, jnp.float32),)
         + (shape(part),) * (turns - 1)
         + (shape((rows, channels), jnp.float32), shape((rows, channels))),
@@ -454,17 +446,17 @@
         ],
         flops=3 * product,
         moved=16 * pair_rows * channels,
-    )(where, hidden_entry_states, far_rows, near_rows, own_targets, peer_targets, activation, slope, source_flip, head, *blocks)
+    )(hidden_entry_states, far_rows, near_rows, own_targets, activation, slope, source_flip, head, *blocks)
     own_part, sent, (grad_one, grad_conv) = outs[0], outs[1:-2], outs[-2:]
 
     received = [swap(piece, "seq", turn) for turn, piece in enumerate(sent, 1)]
     (input_grad,) = call(
         functools.partial(input_grad_body, mp_count),
-        [smem] + [vmem] * (2 + mp_count),
+        [vmem] * (2 + mp_count),
         (shape((rows, channels)),),
         flops=product // 2,
         moved=8 * rows * channels,
-    )(where, grad_one, grad_conv, *blocks)
+    )(grad_one, grad_conv, *blocks)
     first_grad, second_grad, input_grad = call(
         functools.partial(total_body, centre_tap),
         [hbm, hbm] + [vmem] * (1 + turns),

time: 35.7 us -> 30.7 us (0.86)
  Pallas kernels: 8.82 us -> 5.55 us
  starting transfers between devices: 10.8 us -> 9.43 us
    pallas_call x5, Pallas kernels: 7.29 us -> 4.02 us  [the longest x1 2.14 us: local_plan(): call(functools.partial(main_body, mp_count, seq_count, classes), [vmem] *...]
    ppermute x9 -> x8, starting transfers between devices: 10.8 us -> 9.43 us  [swap(): lax.ppermute(block, axis, [(i, i ^ offset) for i in range(lax.axis_size(a...]
    ppermute x9 -> x8, waiting for transfers between devices: 15.1 us -> 14.9 us  [swap(): lax.ppermute(block, axis, [(i, i ^ offset) for i in range(lax.axis_size(a...]
  transfers between devices with their start and end apart: 9 -> 8, of which waited for: 5 -> 5; matrix products, arithmetic and copies ran while one was open for 0% -> 0% of each run, Pallas kernels for 11% -> 6%
where the time goes in v3:
time: 30.7 us; the launch traced here: 30.6 us
  waiting for transfers between devices  14.9 us (49%)
  starting transfers between devices  9.43 us (31%)
  Pallas kernels  5.55 us (18%)
  between operations  0.73 us (2%)
    ppermute x8, waiting for transfers between devices, swap(): lax.ppermute(block, axis, [(i, i ^ offset) for i in range(lax.axis_size(a...  14.9 us
    ppermute x8, starting transfers between devices, swap(): lax.ppermute(block, axis, [(i, i ^ offset) for i in range(lax.axis_size(a...  9.43 us
    pallas_call x1, Pallas kernels, local_plan(): call(functools.partial(main_body, mp_count, seq_count, classes), [vmem] *...  2.14 us
    pallas_call x1, Pallas kernels, local_plan(): call(functools.partial(matrices_body, centre_tap), [hbm] * 2, (shape((2,...  1.03 us
    pallas_call x1, Pallas kernels, local_plan(): first_grad, second_grad = call(blank_body, [], (whole, whole))()  0.83 us
    pallas_call x1, Pallas kernels, local_plan(): call(functools.partial(total_body, centre_tap), [hbm, hbm] + [vmem] * (1...  0.69 us
  transfers between devices with their start and end apart: 8, of which 5 were waited for; matrix products, arithmetic and copies ran while one was open for 0% of the time, Pallas kernels for 6%

profile of v3, /device:TPU:0, one launch (start us, length us, event | category | flops | bytes accessed | tf_op | source)
XLA Modules:
  0.0 30.6 jit_solution(11033903765709518162)
XLA Ops:
  0.7 1.0 %shard_map.87.refs_0_ = bf16[2,512,128]{2,1,0:T(8,128)(2,1)S(1)} custom-call(bf16[9,512,128]{2,1,0:T(8,128)(2,1)} %first_ref.1, bf16[9,512,128]{2,1,0:T(8,128)(2,1)} %second_ref.1), custom_call_target="tpu_custom_call" | custom-call | tf_op jit(solution)/shard_map/pallas_call | solution.py:388
  1.7 3.0 %collective-permute-start.3 = (bf16[2,512,128]{2,1,0:T(8,128)(2,1)S(1)}, bf16[2,512,128]{2,1,0:T(8,128)(2,1)S(1)}, u32[]{:S(2)}, u32[]{:S(2)}) collective-permute-start(bf16[2,512,128]{2,1,0:T(8,128)(2,1)S(1)} %shard_map.87.refs_0_), channel_id=1, source_target_pairs={{0,2},{1,3},{2,0},{3,1},{4,6},{5,7},{6,4},{7,5},{8,10},{9,11},{10,... | collective-permute-start | bytes 786440 | tf_op jit(solution)/shard_map/ppermute | solution.py:149
  4.7 0.0 collective-permute-start.2
  4.7 6.3 %collective-permute-done.3.refs_2_ = bf16[2,512,128]{2,1,0:T(8,128)(2,1)S(1)} collective-permute-done((bf16[2,512,128]{2,1,0:T(8,128)(2,1)S(1)}, bf16[2,512,128]{2,1,0:T(8,128)(2,1)S(1)}, u32[]{:S(2)}, u32[]{:S(2)}) %collective-permute-start.3) | collective-permute-done | bytes 262176 | tf_op jit(solution)/shard_map/ppermute | solution.py:149
  11.0 0.0 collective-permute-start.4
  11.1 0.0 copy-done
  11.1 0.2 shard_map.86
  11.2 2.8 %collective-permute-start = (bf16[80,512]{1,0:T(8,128)(2,1)S(1)}, bf16[80,512]{1,0:T(8,128)(2,1)S(1)}, u32[]{:S(2)}, u32[]{:S(2)}) collective-permute-start(bf16[80,512]{1,0:T(8,128)(2,1)S(1)} %get-tuple-element.22), channel_id=1, source_target_pairs={{0,16},{4,20},{8,24},{12,28},{16,0},{20,4},{24,8},{28,12},{1,17},{... | collective-permute-start | bytes 245768 | tf_op jit(solution)/shard_map/ppermute | solution.py:149
  14.1 4.9 %collective-permute-done.far_ref = bf16[80,512]{1,0:T(8,128)(2,1)S(1)} collective-permute-done((bf16[80,512]{1,0:T(8,128)(2,1)S(1)}, bf16[80,512]{1,0:T(8,128)(2,1)S(1)}, u32[]{:S(2)}, u32[]{:S(2)}) %collective-permute-start) | collective-permute-done | bytes 81952 | tf_op jit(solution)/shard_map/ppermute | solution.py:149
  18.9 0.0 collective-permute-start.1
  18.9 1.3 %collective-permute-done.1.near_ref = bf16[80,512]{1,0:T(8,128)(2,1)S(1)} collective-permute-done((bf16[80,512]{1,0:T(8,128)(2,1)S(1)}, bf16[80,512]{1,0:T(8,128)(2,1)S(1)}, u32[]{:S(2)}, u32[]{:S(2)}) %collective-permute-start.1) | collective-permute-done | bytes 81952 | tf_op jit(solution)/shard_map/ppermute | solution.py:149
  20.2 0.0 collective-permute-done.2.refs_1_
  20.2 0.4 %shard_map.88 = (f32[256,384]{1,0:T(8,128)S(1)}, f32[256,384]{1,0:T(8,128)S(1)}, bf16[512,256]{1,0:T(8,128)(2,1)S(1)}, bf16[16,512]{1,0:T(8,128)(2,1)S(1)}) custom-call(bf16[128,512]{1,0:T(8,128)(2,1)S(1)} %copy-done, bf16[80,512]{1,0:T(8,128)(2,1)S(1)} %collective-permute-done.far_ref, bf16[80,512]{1,0:T(8,128)(2,1)S(1)} %collective-permute-done.1.near_ref, ...), custom_call_target="tpu_custom_call" | custom-call | flops 134217728 | bytes 1048576 | tf_op jit(solution)/shard_map/pallas_call | solution.py:415
  20.6 0.0 collective-permute-done.4.refs_3_
  20.6 2.1 %shard_map.89 = (f32[2,64,128]{2,1,0:T(8,128)S(1)}, bf16[2,64,128]{2,1,0:T(8,128)(2,1)S(1)}, bf16[2,64,128]{2,1,0:T(8,128)(2,1)S(1)}, bf16[2,64,128]{2,1,0:T(8,1...) custom-call(bf16[128,512]{1,0:T(8,128)(2,1)S(1)} %copy-done, ...), custom_call_target="tpu_custom_call" | custom-call | flops 402653184 | bytes 2097152 | tf_op jit(solution)/shard_map/pallas_call | solution.py:430
  22.7 1.6 %collective-permute-start.5 = (bf16[2,64,128]{2,1,0:T(8,128)(2,1)S(1)}, bf16[2,64,128]{2,1,0:T(8,128)(2,1)S(1)}, u32[]{:S(2)}, u32[]{:S(2)}) collective-permute-start(bf16[2,64,128]{2,1,0:T(8,128)(2,1)S(1)} %get-tuple-element.31), channel_id=1, source_target_pairs={{0,4},{4,0},{8,12},{12,8},{16,20},{20,16},{24,28},{28,24},{1,5},{5... | collective-permute-start | bytes 98312 | tf_op jit(solution)/shard_map/ppermute | solution.py:149
  24.4 0.7 %collective-permute-start.6 = (bf16[2,64,128]{2,1,0:T(8,128)(2,1)S(1)}, bf16[2,64,128]{2,1,0:T(8,128)(2,1)S(1)}, u32[]{:S(2)}, u32[]{:S(2)}) collective-permute-start(bf16[2,64,128]{2,1,0:T(8,128)(2,1)S(1)} %get-tuple-element.32), channel_id=1, source_target_pairs={{0,8},{4,12},{8,0},{12,4},{16,24},{20,28},{24,16},{28,20},{1,9},{5... | collective-permute-start | bytes 98312 | tf_op jit(solution)/shard_map/ppermute | solution.py:149
  25.1 1.2 %collective-permute-start.7 = (bf16[2,64,128]{2,1,0:T(8,128)(2,1)S(1)}, bf16[2,64,128]{2,1,0:T(8,128)(2,1)S(1)}, u32[]{:S(2)}, u32[]{:S(2)}) collective-permute-start(bf16[2,64,128]{2,1,0:T(8,128)(2,1)S(1)} %get-tuple-element.33), channel_id=1, source_target_pairs={{0,12},{4,8},{8,4},{12,0},{16,28},{20,24},{24,20},{28,16},{1,13},{... | collective-permute-start | bytes 98312 | tf_op jit(solution)/shard_map/ppermute | solution.py:149
  26.3 0.8 %shard_map.85 = (f32[9,64,128]{2,1,0:T(8,128)}, f32[9,64,128]{2,1,0:T(8,128)}) custom-call(), custom_call_target="tpu_custom_call" | custom-call | tf_op jit(solution)/shard_map/pallas_call | solution.py:410
  27.1 0.3 %shard_map.90.input_grad_ref = bf16[128,512]{1,0:T(8,128)(2,1)S(1)} custom-call(f32[128,512]{1,0:T(8,128)S(1)} %get-tuple-element.28.grad_ref, bf16[128,512]{1,0:T(8,128)(2,1)S(1)} %get-tuple-element.29.grad_conv_ref, bf16[2,512,128]{2,1,0:T(8,128)(2,1)S(1)} %shard_map.87.refs_0_, bf16[2,512,128]{2,1,0:T(8,128)(2,1)S(1)} %collective-permute-done.2.refs_1_, ...), custom_call_target="tpu_custom_call" | custom-call | flops 67108864 | bytes 524288 | tf_op jit(solution)/shard_map/pallas_call | solution.py:453
  27.5 0.0 collective-permute-done.5.refs_0_
  27.5 0.8 %collective-permute-done.6.refs_1_ = bf16[2,64,128]{2,1,0:T(8,128)(2,1)S(1)} collective-permute-done((bf16[2,64,128]{2,1,0:T(8,128)(2,1)S(1)}, bf16[2,64,128]{2,1,0:T(8,128)(2,1)S(1)}, u32[]{:S(2)}, u32[]{:S(2)}) %collective-permute-start.6) | collective-permute-done | bytes 32800 | tf_op jit(solution)/shard_map/ppermute | solution.py:149
  28.3 1.6 %collective-permute-done.7.refs_2_ = bf16[2,64,128]{2,1,0:T(8,128)(2,1)S(1)} collective-permute-done((bf16[2,64,128]{2,1,0:T(8,128)(2,1)S(1)}, bf16[2,64,128]{2,1,0:T(8,128)(2,1)S(1)}, u32[]{:S(2)}, u32[]{:S(2)}) %collective-permute-start.7) | collective-permute-done | bytes 32800 | tf_op jit(solution)/shard_map/ppermute | solution.py:149
  29.9 0.7 %shard_map.91 = (f32[9,64,128]{2,1,0:T(8,128)}, f32[9,64,128]{2,1,0:T(8,128)}, bf16[128,512]{1,0:T(8,128)(2,1)}) custom-call(f32[9,64,128]{2,1,0:T(8,128)} %get-tuple-element.20.first_in_ref, f32[9,64,128]{2,1,0:T(8,128)} %get-tuple-element.21.second_in_ref, ...), custom_call_target="tpu_custom_call", output_to_operand_aliasing={{0}: (0, {}), {1}: (1, {})} | custom-call | tf_op jit(solution)/shard_map/pallas_call | solution.py:460
  (7 shorter events, 0.0 us)
Async XLA Ops:
  0.6 10.4 %copy-start.2 = (s32[16]{0:T(128)S(1)}, s32[16]{0:T(128)}, u32[]{:S(2)}) copy-start(s32[16]{0:T(128)} %param.8) | copy-start | bytes 196
  0.6 10.4 %copy-start.3 = (s32[128]{0:T(128)S(1)}, s32[128]{0:T(128)}, u32[]{:S(2)}) copy-start(s32[128]{0:T(128)} %param.7) | copy-start | bytes 1540
  0.7 10.4 %copy-start = (bf16[128,512]{1,0:T(8,128)(2,1)S(1)}, bf16[128,512]{1,0:T(8,128)(2,1)}, u32[]{:S(2)}) copy-start(bf16[128,512]{1,0:T(8,128)(2,1)} %own_ref.3) | copy-start | bytes 393220
  0.7 19.6 %copy-start.1 = (bf16[512,5]{0,1:T(8,128)(2,1)S(1)}, bf16[512,5]{0,1:T(8,128)(2,1)}, u32[]{:S(2)}) copy-start(bf16[512,5]{0,1:T(8,128)(2,1)} %param.11) | copy-start | bytes 15364
  1.7 9.3 %collective-permute-start.3 = (bf16[2,512,128]{2,1,0:T(8,128)(2,1)S(1)}, bf16[2,512,128]{2,1,0:T(8,128)(2,1)S(1)}, u32[]{:S(2)}, u32[]{:S(2)}) collective-permute-start(bf16[2,512,128]{2,1,0:T(8,128)(2,1)S(1)} %shard_map.87.refs_0_), channel_id=1, source_target_pairs={{0,2},{1,3},{2,0},{3,1},{4,6},{5,7},{6,4},{7,5},{8,10},{9,11},{10,... | collective-permute-start | bytes 786440 | tf_op jit(solution)/shard_map/ppermute | solution.py:149
  4.7 15.5 %collective-permute-start.2 = (bf16[2,512,128]{2,1,0:T(8,128)(2,1)S(1)}, bf16[2,512,128]{2,1,0:T(8,128)(2,1)S(1)}, u32[]{:S(2)}, u32[]{:S(2)}) collective-permute-start(bf16[2,512,128]{2,1,0:T(8,128)(2,1)S(1)} %shard_map.87.refs_0_), channel_id=1, source_target_pairs={{0,1},{1,0},{2,3},{3,2},{4,5},{5,4},{6,7},{7,6},{8,9},{9,8},{10,11... | collective-permute-start | bytes 786440 | tf_op jit(solution)/shard_map/ppermute | solution.py:149
  11.0 9.6 %collective-permute-start.4 = (bf16[2,512,128]{2,1,0:T(8,128)(2,1)S(1)}, bf16[2,512,128]{2,1,0:T(8,128)(2,1)S(1)}, u32[]{:S(2)}, u32[]{:S(2)}) collective-permute-start(bf16[2,512,128]{2,1,0:T(8,128)(2,1)S(1)} %collective-permute-done.3.refs_2_), channel_id=1, source_target_pairs={{0,1},{1,0},{2,3},{3,2},{4,5},{5,4},{6,7},{7,6},{8,9},{9,8},{10,11... | collective-permute-start | bytes 786440 | tf_op jit(solution)/shard_map/ppermute | solution.py:149
  11.2 7.7 %collective-permute-start = (bf16[80,512]{1,0:T(8,128)(2,1)S(1)}, bf16[80,512]{1,0:T(8,128)(2,1)S(1)}, u32[]{:S(2)}, u32[]{:S(2)}) collective-permute-start(bf16[80,512]{1,0:T(8,128)(2,1)S(1)} %get-tuple-element.22), channel_id=1, source_target_pairs={{0,16},{4,20},{8,24},{12,28},{16,0},{20,4},{24,8},{28,12},{1,17},{... | collective-permute-start | bytes 245768 | tf_op jit(solution)/shard_map/ppermute | solution.py:149
  18.9 1.3 %collective-permute-start.1 = (bf16[80,512]{1,0:T(8,128)(2,1)S(1)}, bf16[80,512]{1,0:T(8,128)(2,1)S(1)}, u32[]{:S(2)}, u32[]{:S(2)}) collective-permute-start(bf16[80,512]{1,0:T(8,128)(2,1)S(1)} %collective-permute-done.far_ref), channel_id=1, source_target_pairs={{0,1},{1,0},{2,3},{3,2},{4,5},{5,4},{6,7},{7,6},{8,9},{9,8},{10,11... | collective-permute-start | bytes 245768 | tf_op jit(solution)/shard_map/ppermute | solution.py:149
  22.7 4.7 %collective-permute-start.5 = (bf16[2,64,128]{2,1,0:T(8,128)(2,1)S(1)}, bf16[2,64,128]{2,1,0:T(8,128)(2,1)S(1)}, u32[]{:S(2)}, u32[]{:S(2)}) collective-permute-start(bf16[2,64,128]{2,1,0:T(8,128)(2,1)S(1)} %get-tuple-element.31), channel_id=1, source_target_pairs={{0,4},{4,0},{8,12},{12,8},{16,20},{20,16},{24,28},{28,24},{1,5},{5... | collective-permute-start | bytes 98312 | tf_op jit(solution)/shard_map/ppermute | solution.py:149
  24.4 3.9 %collective-permute-start.6 = (bf16[2,64,128]{2,1,0:T(8,128)(2,1)S(1)}, bf16[2,64,128]{2,1,0:T(8,128)(2,1)S(1)}, u32[]{:S(2)}, u32[]{:S(2)}) collective-permute-start(bf16[2,64,128]{2,1,0:T(8,128)(2,1)S(1)} %get-tuple-element.32), channel_id=1, source_target_pairs={{0,8},{4,12},{8,0},{12,4},{16,24},{20,28},{24,16},{28,20},{1,9},{5... | collective-permute-start | bytes 98312 | tf_op jit(solution)/shard_map/ppermute | solution.py:149
  25.1 4.8 %collective-permute-start.7 = (bf16[2,64,128]{2,1,0:T(8,128)(2,1)S(1)}, bf16[2,64,128]{2,1,0:T(8,128)(2,1)S(1)}, u32[]{:S(2)}, u32[]{:S(2)}) collective-permute-start(bf16[2,64,128]{2,1,0:T(8,128)(2,1)S(1)} %get-tuple-element.33), channel_id=1, source_target_pairs={{0,12},{4,8},{8,4},{12,0},{16,28},{20,24},{24,20},{28,16},{1,13},{... | collective-permute-start | bytes 98312 | tf_op jit(solution)/shard_map/ppermute | solution.py:149

commit v4 on v3

--- a/solution.py
+++ b/solution.py
@@ -175,7 +175,7 @@
         copy.wait()
 
 
-def prepare_body(mask_ref, ids_ref, source_ref, own_ref, sent_ref):
+def prepare_body(mask_ref, ids_ref, source_ref, own_ref, sent_targets_ref, sent_ref):
     rows = source_ref.shape[0]
     share = rows // 2
     entries = mask_ref.shape[1]
@@ -190,9 +190,8 @@
     targets = jnp.broadcast_to(targets, own_ref.shape)
     turned = pltpu.roll(targets, share, 1)
     own_ref[...] = targets.astype(jnp.bfloat16)
-    sent_ref[0:share, :] = source_ref[pl.ds(pl.multiple_of(part * share, share), share), :]
-    sent_ref[share:, :] = jnp.zeros((SIDE_ROWS, source_ref.shape[1]), jnp.bfloat16)
-    sent_ref[share:, 0:rows] = jnp.where(part == 1, turned, targets).astype(jnp.bfloat16)
+    sent_targets_ref[...] = jnp.where(part == 1, turned, targets).astype(jnp.bfloat16)
+    sent_ref[...] = source_ref[pl.ds(pl.multiple_of(part * share, share), share), :]
 
 
 def blank_body(first_ref, second_ref):
@@ -212,8 +211,7 @@
 
 
 def row_halves(own_ref, far_ref, near_ref):
-    share = own_ref.shape[0] // 2
-    return ((own_ref,), (far_ref.at[0:share], near_ref.at[0:share]))
+    return ((own_ref,), (far_ref, near_ref))
 
 
 def early_body(count, own_ref, far_ref, near_ref, head_ref, *refs):
@@ -232,7 +230,7 @@
     head_out_ref[0:classes, :] = own_order(me, (head_ref,), count)
 
 
-def main_body(count, blocks, classes, own_ref, far_ref, near_ref, own_targets_ref, activation_ref, slope_ref, source_flip_ref, head_ref, *refs):
+def main_body(count, blocks, classes, own_ref, far_ref, near_ref, own_targets_ref, peer_targets_ref, activation_ref, slope_ref, source_flip_ref, head_ref, *refs):
     turns = blocks // 2
     matrix_refs, refs = refs[:count], refs[count:]
     self_ref, sent_refs, refs = refs[0], refs[1:turns], refs[turns:]
@@ -242,7 +240,7 @@
     half = own_ref.shape[0]
     _, depth, width = self_ref.shape
     source_refs = row_halves(own_ref, far_ref, near_ref)
-    target_refs = (own_targets_ref, far_ref.at[half // 2 :, 0:half])
+    target_refs = (own_targets_ref, peer_targets_ref)
     late = columns_of(me, matrix_refs[-1:], 0, count)
     weights = columns_of(me, matrix_refs, 1, count)
     head = head_ref[...]
@@ -399,13 +397,12 @@
         bit //= 2
     blocks = [blocks[offset] for offset in range(mp_count)]
 
-    own_targets, sent_rows = call(
-        prepare_body,
-        [vmem] * 3,
-        (shape((SIDE_ROWS, rows)), shape((rows // 2 + SIDE_ROWS, channels))),
+    own_targets, sent_targets, sent_rows = call(
+        prepare_body, [vmem] * 3, (shape((SIDE_ROWS, rows)),) * 2 + (shape((rows // 2, channels)),)
     )(mask_index[None, :], base_ids[None, :], hidden_entry_states)
     far_rows = swap(sent_rows, "seq", seq_count // 2)
     near_rows = swap(far_rows, "mp", 1)
+    peer_targets = swap(sent_targets, "seq", seq_count // 2)
     whole = shape((tap_count, depth, width), jnp.float32)
     first_grad, second_grad = call(blank_body, [], (whole, whole))()
 
@@ -429,7 +426,7 @@
     part = (2, depth, width)
     outs = call(
         functools.partial(main_body, mp_count, seq_count, classes),
-        [vmem] * (8 + mp_count),
+        [vmem] * (9 + mp_count),
         (shape(part, jnp.float32),)
         + (shape(part),) * (turns - 1)
         + (shape((rows, channels), jnp.float32), shape((rows, channels))),
@@ -446,7 +443,7 @@
         ],
         flops=3 * product,
         moved=16 * pair_rows * channels,
-    )(hidden_entry_states, far_rows, near_rows, own_targets, activation, slope, source_flip, head, *blocks)
+    )(hidden_entry_states, far_rows, near_rows, own_targets, peer_targets, activation, slope, source_flip, head, *blocks)
     own_part, sent, (grad_one, grad_conv) = outs[0], outs[1:-2], outs[-2:]
 
     received = [swap(piece, "seq", turn) for turn, piece in enumerate(sent, 1)]

time: 30.7 us -> 33.4 us (1.088)
  starting transfers between devices: 9.43 us -> 10.8 us
  waiting for transfers between devices: 14.9 us -> 16.2 us
    ppermute x8 -> x9, starting transfers between devices: 9.43 us -> 10.8 us  [swap(): lax.ppermute(block, axis, [(i, i ^ offset) for i in range(lax.axis_size(a...]
    ppermute x8 -> x9, waiting for transfers between devices: 14.9 us -> 16.2 us  [swap(): lax.ppermute(block, axis, [(i, i ^ offset) for i in range(lax.axis_size(a...]
  transfers between devices with their start and end apart: 8 -> 9, of which waited for: 5 -> 5; matrix products, arithmetic and copies ran while one was open for 0% -> 0% of each run, Pallas kernels for 6% -> 5%
where the time goes in v4:
time: 33.4 us; the launch traced here: 33.2 us
  waiting for transfers between devices  16.2 us (49%)
  starting transfers between devices  10.8 us (32%)
  Pallas kernels  5.53 us (17%)
  between operations  0.72 us (2%)
    ppermute x9, waiting for transfers between devices, swap(): lax.ppermute(block, axis, [(i, i ^ offset) for i in range(lax.axis_size(a...  16.2 us
    ppermute x9, starting transfers between devices, swap(): lax.ppermute(block, axis, [(i, i ^ offset) for i in range(lax.axis_size(a...  10.8 us
    pallas_call x1, Pallas kernels, local_plan(): call(functools.partial(main_body, mp_count, seq_count, classes), [vmem] *...  2.12 us
    pallas_call x1, Pallas kernels, local_plan(): call(functools.partial(matrices_body, centre_tap), [hbm] * 2, (shape((2,...  1.03 us
    pallas_call x1, Pallas kernels, local_plan(): first_grad, second_grad = call(blank_body, [], (whole, whole))()  0.83 us
    pallas_call x1, Pallas kernels, local_plan(): call(functools.partial(total_body, centre_tap), [hbm, hbm] + [vmem] * (1...  0.69 us
  transfers between devices with their start and end apart: 9, of which 5 were waited for; matrix products, arithmetic and copies ran while one was open for 0% of the time, Pallas kernels for 5%

profile of v4, /device:TPU:0, one launch (start us, length us, event | category | flops | bytes accessed | tf_op | source)
XLA Modules:
  0.0 33.2 jit_solution(15791450952514576258)
XLA Ops:
  0.7 1.0 %shard_map.87.refs_0_ = bf16[2,512,128]{2,1,0:T(8,128)(2,1)S(1)} custom-call(bf16[9,512,128]{2,1,0:T(8,128)(2,1)} %first_ref.1, bf16[9,512,128]{2,1,0:T(8,128)(2,1)} %second_ref.1), custom_call_target="tpu_custom_call" | custom-call | tf_op jit(solution)/shard_map/pallas_call | solution.py:386
  1.7 3.0 %collective-permute-start.4 = (bf16[2,512,128]{2,1,0:T(8,128)(2,1)S(1)}, bf16[2,512,128]{2,1,0:T(8,128)(2,1)S(1)}, u32[]{:S(2)}, u32[]{:S(2)}) collective-permute-start(bf16[2,512,128]{2,1,0:T(8,128)(2,1)S(1)} %shard_map.87.refs_0_), channel_id=1, source_target_pairs={{0,2},{1,3},{2,0},{3,1},{4,6},{5,7},{6,4},{7,5},{8,10},{9,11},{10,... | collective-permute-start | bytes 786440 | tf_op jit(solution)/shard_map/ppermute | solution.py:149
  4.7 0.0 collective-permute-start.3
  4.7 6.3 %collective-permute-done.4.refs_2_ = bf16[2,512,128]{2,1,0:T(8,128)(2,1)S(1)} collective-permute-done((bf16[2,512,128]{2,1,0:T(8,128)(2,1)S(1)}, bf16[2,512,128]{2,1,0:T(8,128)(2,1)S(1)}, u32[]{:S(2)}, u32[]{:S(2)}) %collective-permute-start.4) | collective-permute-done | bytes 262176 | tf_op jit(solution)/shard_map/ppermute | solution.py:149
  11.0 0.0 collective-permute-start.5
  11.1 0.2 shard_map.86
  11.2 2.8 %collective-permute-start = (bf16[64,512]{1,0:T(8,128)(2,1)S(1)}, bf16[64,512]{1,0:T(8,128)(2,1)S(1)}, u32[]{:S(2)}, u32[]{:S(2)}) collective-permute-start(bf16[64,512]{1,0:T(8,128)(2,1)S(1)} %get-tuple-element.23), channel_id=1, source_target_pairs={{0,16},{4,20},{8,24},{12,28},{16,0},{20,4},{24,8},{28,12},{1,17},{... | collective-permute-start | bytes 196616 | tf_op jit(solution)/shard_map/ppermute | solution.py:149
  14.1 4.2 %collective-permute-done.far_ref = bf16[64,512]{1,0:T(8,128)(2,1)S(1)} collective-permute-done((bf16[64,512]{1,0:T(8,128)(2,1)S(1)}, bf16[64,512]{1,0:T(8,128)(2,1)S(1)}, u32[]{:S(2)}, u32[]{:S(2)}) %collective-permute-start) | collective-permute-done | bytes 65568 | tf_op jit(solution)/shard_map/ppermute | solution.py:149
  18.2 0.0 collective-permute-start.1
  18.2 1.3 %collective-permute-start.2 = (bf16[16,128]{1,0:T(8,128)(2,1)S(1)}, bf16[16,128]{1,0:T(8,128)(2,1)S(1)}, u32[]{:S(2)}, u32[]{:S(2)}) collective-permute-start(bf16[16,128]{1,0:T(8,128)(2,1)S(1)} %get-tuple-element.25), channel_id=1, source_target_pairs={{0,16},{4,20},{8,24},{12,28},{16,0},{20,4},{24,8},{28,12},{1,17},{... | collective-permute-start | bytes 12296 | tf_op jit(solution)/shard_map/ppermute | solution.py:149
  19.6 0.0 collective-permute-done.1.near_ref
  19.6 0.0 collective-permute-done.3.refs_1_
  19.6 0.4 %shard_map.88 = (f32[256,384]{1,0:T(8,128)S(1)}, f32[256,384]{1,0:T(8,128)S(1)}, bf16[512,256]{1,0:T(8,128)(2,1)S(1)}, bf16[16,512]{1,0:T(8,128)(2,1)S(1)}) custom-call(bf16[128,512]{1,0:T(8,128)(2,1)S(1)} %copy-done, bf16[64,512]{1,0:T(8,128)(2,1)S(1)} %collective-permute-done.far_ref, bf16[64,512]{1,0:T(8,128)(2,1)S(1)} %collective-permute-done.1.near_ref, ...), custom_call_target="tpu_custom_call" | custom-call | flops 134217728 | bytes 1048576 | tf_op jit(solution)/shard_map/pallas_call | solution.py:412
  20.0 2.8 %collective-permute-done.2.peer_targets_ref = bf16[16,128]{1,0:T(8,128)(2,1)S(1)} collective-permute-done((bf16[16,128]{1,0:T(8,128)(2,1)S(1)}, bf16[16,128]{1,0:T(8,128)(2,1)S(1)}, u32[]{:S(2)}, u32[]{:S(2)}) %collective-permute-start.2) | collective-permute-done | bytes 4128 | tf_op jit(solution)/shard_map/ppermute | solution.py:149
  22.7 2.1 %shard_map.89 = (f32[2,64,128]{2,1,0:T(8,128)S(1)}, bf16[2,64,128]{2,1,0:T(8,128)(2,1)S(1)}, bf16[2,64,128]{2,1,0:T(8,128)(2,1)S(1)}, bf16[2,64,128]{2,1,0:T(8,1...) custom-call(bf16[128,512]{1,0:T(8,128)(2,1)S(1)} %copy-done, ...), custom_call_target="tpu_custom_call" | custom-call | flops 402653184 | bytes 2097152 | tf_op jit(solution)/shard_map/pallas_call | solution.py:427
  24.9 1.6 %collective-permute-start.6 = (bf16[2,64,128]{2,1,0:T(8,128)(2,1)S(1)}, bf16[2,64,128]{2,1,0:T(8,128)(2,1)S(1)}, u32[]{:S(2)}, u32[]{:S(2)}) collective-permute-start(bf16[2,64,128]{2,1,0:T(8,128)(2,1)S(1)} %get-tuple-element.33), channel_id=1, source_target_pairs={{0,4},{4,0},{8,12},{12,8},{16,20},{20,16},{24,28},{28,24},{1,5},{5... | collective-permute-start | bytes 98312 | tf_op jit(solution)/shard_map/ppermute | solution.py:149
  26.5 1.2 %collective-permute-start.7 = (bf16[2,64,128]{2,1,0:T(8,128)(2,1)S(1)}, bf16[2,64,128]{2,1,0:T(8,128)(2,1)S(1)}, u32[]{:S(2)}, u32[]{:S(2)}) collective-permute-start(bf16[2,64,128]{2,1,0:T(8,128)(2,1)S(1)} %get-tuple-element.34), channel_id=1, source_target_pairs={{0,8},{4,12},{8,0},{12,4},{16,24},{20,28},{24,16},{28,20},{1,9},{5... | collective-permute-start | bytes 98312 | tf_op jit(solution)/shard_map/ppermute | solution.py:149
  27.7 0.7 %collective-permute-start.8 = (bf16[2,64,128]{2,1,0:T(8,128)(2,1)S(1)}, bf16[2,64,128]{2,1,0:T(8,128)(2,1)S(1)}, u32[]{:S(2)}, u32[]{:S(2)}) collective-permute-start(bf16[2,64,128]{2,1,0:T(8,128)(2,1)S(1)} %get-tuple-element.35), channel_id=1, source_target_pairs={{0,12},{4,8},{8,4},{12,0},{16,28},{20,24},{24,20},{28,16},{1,13},{... | collective-permute-start | bytes 98312 | tf_op jit(solution)/shard_map/ppermute | solution.py:149
  28.4 0.8 %shard_map.85 = (f32[9,64,128]{2,1,0:T(8,128)}, f32[9,64,128]{2,1,0:T(8,128)}) custom-call(), custom_call_target="tpu_custom_call" | custom-call | tf_op jit(solution)/shard_map/pallas_call | solution.py:407
  29.3 0.3 shard_map.90.input_grad_ref
  29.6 0.0 collective-permute-done.6.refs_0_
  29.6 0.8 %collective-permute-done.7.refs_1_ = bf16[2,64,128]{2,1,0:T(8,128)(2,1)S(1)} collective-permute-done((bf16[2,64,128]{2,1,0:T(8,128)(2,1)S(1)}, bf16[2,64,128]{2,1,0:T(8,128)(2,1)S(1)}, u32[]{:S(2)}, u32[]{:S(2)}) %collective-permute-start.7) | collective-permute-done | bytes 32800 | tf_op jit(solution)/shard_map/ppermute | solution.py:149
  30.4 2.1 %collective-permute-done.8.refs_2_ = bf16[2,64,128]{2,1,0:T(8,128)(2,1)S(1)} collective-permute-done((bf16[2,64,128]{2,1,0:T(8,128)(2,1)S(1)}, bf16[2,64,128]{2,1,0:T(8,128)(2,1)S(1)}, u32[]{:S(2)}, u32[]{:S(2)}) %collective-permute-start.8) | collective-permute-done | bytes 32800 | tf_op jit(solution)/shard_map/ppermute | solution.py:149
  32.5 0.7 %shard_map.91 = (f32[9,64,128]{2,1,0:T(8,128)}, f32[9,64,128]{2,1,0:T(8,128)}, bf16[128,512]{1,0:T(8,128)(2,1)}) custom-call(f32[9,64,128]{2,1,0:T(8,128)} %get-tuple-element.21.first_in_ref, f32[9,64,128]{2,1,0:T(8,128)} %get-tuple-element.22.second_in_ref, ...), custom_call_target="tpu_custom_call", output_to_operand_aliasing={{0}: (0, {}), {1}: (1, {})} | custom-call | tf_op jit(solution)/shard_map/pallas_call | solution.py:457
  (9 shorter events, 0.0 us)
Async XLA Ops:
  0.6 10.4 %copy-start.2 = (s32[16]{0:T(128)S(1)}, s32[16]{0:T(128)}, u32[]{:S(2)}) copy-start(s32[16]{0:T(128)} %param.8) | copy-start | bytes 196
  0.6 10.4 %copy-start.3 = (s32[128]{0:T(128)S(1)}, s32[128]{0:T(128)}, u32[]{:S(2)}) copy-start(s32[128]{0:T(128)} %param.7) | copy-start | bytes 1540
  0.7 10.4 %copy-start = (bf16[128,512]{1,0:T(8,128)(2,1)S(1)}, bf16[128,512]{1,0:T(8,128)(2,1)}, u32[]{:S(2)}) copy-start(bf16[128,512]{1,0:T(8,128)(2,1)} %own_ref.3) | copy-start | bytes 393220
  0.7 18.9 %copy-start.1 = (bf16[512,5]{0,1:T(8,128)(2,1)S(1)}, bf16[512,5]{0,1:T(8,128)(2,1)}, u32[]{:S(2)}) copy-start(bf16[512,5]{0,1:T(8,128)(2,1)} %param.11) | copy-start | bytes 15364
  1.7 9.3 %collective-permute-start.4 = (bf16[2,512,128]{2,1,0:T(8,128)(2,1)S(1)}, bf16[2,512,128]{2,1,0:T(8,128)(2,1)S(1)}, u32[]{:S(2)}, u32[]{:S(2)}) collective-permute-start(bf16[2,512,128]{2,1,0:T(8,128)(2,1)S(1)} %shard_map.87.refs_0_), channel_id=1, source_target_pairs={{0,2},{1,3},{2,0},{3,1},{4,6},{5,7},{6,4},{7,5},{8,10},{9,11},{10,... | collective-permute-start | bytes 786440 | tf_op jit(solution)/shard_map/ppermute | solution.py:149
  4.7 14.8 %collective-permute-start.3 = (bf16[2,512,128]{2,1,0:T(8,128)(2,1)S(1)}, bf16[2,512,128]{2,1,0:T(8,128)(2,1)S(1)}, u32[]{:S(2)}, u32[]{:S(2)}) collective-permute-start(bf16[2,512,128]{2,1,0:T(8,128)(2,1)S(1)} %shard_map.87.refs_0_), channel_id=1, source_target_pairs={{0,1},{1,0},{2,3},{3,2},{4,5},{5,4},{6,7},{7,6},{8,9},{9,8},{10,11... | collective-permute-start | bytes 786440 | tf_op jit(solution)/shard_map/ppermute | solution.py:149
  11.0 11.7 %collective-permute-start.5 = (bf16[2,512,128]{2,1,0:T(8,128)(2,1)S(1)}, bf16[2,512,128]{2,1,0:T(8,128)(2,1)S(1)}, u32[]{:S(2)}, u32[]{:S(2)}) collective-permute-start(bf16[2,512,128]{2,1,0:T(8,128)(2,1)S(1)} %collective-permute-done.4.refs_2_), channel_id=1, source_target_pairs={{0,1},{1,0},{2,3},{3,2},{4,5},{5,4},{6,7},{7,6},{8,9},{9,8},{10,11... | collective-permute-start | bytes 786440 | tf_op jit(solution)/shard_map/ppermute | solution.py:149
  11.2 7.0 %collective-permute-start = (bf16[64,512]{1,0:T(8,128)(2,1)S(1)}, bf16[64,512]{1,0:T(8,128)(2,1)S(1)}, u32[]{:S(2)}, u32[]{:S(2)}) collective-permute-start(bf16[64,512]{1,0:T(8,128)(2,1)S(1)} %get-tuple-element.23), channel_id=1, source_target_pairs={{0,16},{4,20},{8,24},{12,28},{16,0},{20,4},{24,8},{28,12},{1,17},{... | collective-permute-start | bytes 196616 | tf_op jit(solution)/shard_map/ppermute | solution.py:149
  18.2 1.3 %collective-permute-start.1 = (bf16[64,512]{1,0:T(8,128)(2,1)S(1)}, bf16[64,512]{1,0:T(8,128)(2,1)S(1)}, u32[]{:S(2)}, u32[]{:S(2)}) collective-permute-start(bf16[64,512]{1,0:T(8,128)(2,1)S(1)} %collective-permute-done.far_ref), channel_id=1, source_target_pairs={{0,1},{1,0},{2,3},{3,2},{4,5},{5,4},{6,7},{7,6},{8,9},{9,8},{10,11... | collective-permute-start | bytes 196616 | tf_op jit(solution)/shard_map/ppermute | solution.py:149
  18.2 4.5 %collective-permute-start.2 = (bf16[16,128]{1,0:T(8,128)(2,1)S(1)}, bf16[16,128]{1,0:T(8,128)(2,1)S(1)}, u32[]{:S(2)}, u32[]{:S(2)}) collective-permute-start(bf16[16,128]{1,0:T(8,128)(2,1)S(1)} %get-tuple-element.25), channel_id=1, source_target_pairs={{0,16},{4,20},{8,24},{12,28},{16,0},{20,4},{24,8},{28,12},{1,17},{... | collective-permute-start | bytes 12296 | tf_op jit(solution)/shard_map/ppermute | solution.py:149
  24.9 4.7 %collective-permute-start.6 = (bf16[2,64,128]{2,1,0:T(8,128)(2,1)S(1)}, bf16[2,64,128]{2,1,0:T(8,128)(2,1)S(1)}, u32[]{:S(2)}, u32[]{:S(2)}) collective-permute-start(bf16[2,64,128]{2,1,0:T(8,128)(2,1)S(1)} %get-tuple-element.33), channel_id=1, source_target_pairs={{0,4},{4,0},{8,12},{12,8},{16,20},{20,16},{24,28},{28,24},{1,5},{5... | collective-permute-start | bytes 98312 | tf_op jit(solution)/shard_map/ppermute | solution.py:149
  26.5 3.9 %collective-permute-start.7 = (bf16[2,64,128]{2,1,0:T(8,128)(2,1)S(1)}, bf16[2,64,128]{2,1,0:T(8,128)(2,1)S(1)}, u32[]{:S(2)}, u32[]{:S(2)}) collective-permute-start(bf16[2,64,128]{2,1,0:T(8,128)(2,1)S(1)} %get-tuple-element.34), channel_id=1, source_target_pairs={{0,8},{4,12},{8,0},{12,4},{16,24},{20,28},{24,16},{28,20},{1,9},{5... | collective-permute-start | bytes 98312 | tf_op jit(solution)/shard_map/ppermute | solution.py:149
  27.7 4.8 %collective-permute-start.8 = (bf16[2,64,128]{2,1,0:T(8,128)(2,1)S(1)}, bf16[2,64,128]{2,1,0:T(8,128)(2,1)S(1)}, u32[]{:S(2)}, u32[]{:S(2)}) collective-permute-start(bf16[2,64,128]{2,1,0:T(8,128)(2,1)S(1)} %get-tuple-element.35), channel_id=1, source_target_pairs={{0,12},{4,8},{8,4},{12,0},{16,28},{20,24},{24,20},{28,16},{1,13},{... | collective-permute-start | bytes 98312 | tf_op jit(solution)/shard_map/ppermute | solution.py:149

commit v5 on v4

--- a/solution.py
+++ b/solution.py
@@ -164,10 +164,11 @@
     )
 
 
-def matrices_body(centre_tap, first_ref, second_ref, both_ref, sems):
+def matrices_body(centre_tap, first_ref, second_ref, own_first_ref, own_second_ref, both_ref, sems):
+    targets = (own_first_ref, own_second_ref, both_ref.at[0], both_ref.at[1])
     copies = [
-        pltpu.make_async_copy(ref.at[centre_tap], both_ref.at[slot], sems.at[slot])
-        for slot, ref in enumerate((first_ref, second_ref))
+        pltpu.make_async_copy(source.at[centre_tap], target, sems.at[n])
+        for n, (source, target) in enumerate(zip((first_ref, second_ref) * 2, targets))
     ]
     for copy in copies:
         copy.start()
@@ -199,13 +200,11 @@
     second_ref[...] = jnp.zeros_like(second_ref)
 
 
-def columns_of(me, matrix_refs, slot, count):
-    width = matrix_refs[0].shape[2]
+def square(me, matrix_refs):
+    width = matrix_refs[0].shape[1]
+    count = len(matrix_refs)
     return stacked(
-        [
-            stacked([ref[slot, block_at(me, o, width), :] for o in range(count)], 0)
-            for ref in matrix_refs
-        ],
+        [stacked([ref[block_at(me, o, width), :] for o in range(count)], 0) for ref in matrix_refs],
         1,
     )
 
@@ -214,45 +213,43 @@
     return ((own_ref,), (far_ref, near_ref))
 
 
-def early_body(count, own_ref, far_ref, near_ref, head_ref, *refs):
-    matrix_refs = refs[:-4]
-    activation_ref, slope_ref, flip_ref, head_out_ref = refs[-4:]
+def first_block_body(count, own_ref, far_ref, near_ref, head_ref, *refs):
+    matrix_refs = refs[:count]
+    hidden_ref, normed_ref, scale_ref, hidden_flip_ref, source_flip_ref, head_out_ref = refs[count:]
     me = lax.axis_index("mp")
     half = own_ref.shape[0]
-    weights = columns_of(me, matrix_refs, 0, count)
+    width = matrix_refs[0].shape[1]
+    weights = square(me, matrix_refs)
     for part, source_refs in enumerate(row_halves(own_ref, far_ref, near_ref)):
         rows = pl.ds(part * half, half)
-        conv_out = dot(own_order(me, source_refs, count), weights)
-        activation_ref[rows, :], slope_ref[rows, :] = gelu_and_slope(conv_out)
-        flip_ref[:, rows] = stacked([ref[...] for ref in source_refs], 0).T
+        source = own_order(me, source_refs, count)
+        activation, gelu_slope = gelu_and_slope(dot(source, weights))
+        normed, inverse = norm_parts(activation)
+        scale_ref[rows, :] = gelu_slope * inverse
+        normed_ref[rows, :] = normed
+        hidden = (source.astype(jnp.float32) + normed).astype(jnp.bfloat16)
+        hidden_ref[rows, :] = hidden
+        source_flip_ref[:, rows] = stacked([ref[...] for ref in source_refs], 0).T
+        for offset in range(count):
+            flipped = hidden[:, offset * width : (offset + 1) * width].T
+            hidden_flip_ref[block_at(me, offset, width), rows] = flipped
     head_out_ref[...] = jnp.zeros_like(head_out_ref)
     classes = head_ref.shape[0]
     head_out_ref[0:classes, :] = own_order(me, (head_ref,), count)
 
 
-def main_body(count, blocks, classes, own_ref, far_ref, near_ref, own_targets_ref, peer_targets_ref, activation_ref, slope_ref, source_flip_ref, head_ref, *refs):
+def main_body(count, blocks, classes, own_targets_ref, peer_targets_ref, hidden_one_ref, normed_one_ref, scale_one_ref, hidden_flip_ref, source_flip_ref, head_ref, *refs):
     turns = blocks // 2
     matrix_refs, refs = refs[:count], refs[count:]
     self_ref, sent_refs, refs = refs[0], refs[1:turns], refs[turns:]
     grad_out_ref, grad_conv_out_ref = refs[:2]
-    hidden_one_ref, normed_one_ref, scale_one_ref, hidden_flip_ref, normed_two_ref, scale_two_ref, hidden_two_ref, grad_ref, grad_conv_ref = refs[2:]
+    normed_two_ref, scale_two_ref, hidden_two_ref, grad_ref, grad_conv_ref = refs[2:]
     me, block = lax.axis_index("mp"), lax.axis_index("seq")
-    half = own_ref.shape[0]
+    half = own_targets_ref.shape[1]
     _, depth, width = self_ref.shape
-    source_refs = row_halves(own_ref, far_ref, near_ref)
     target_refs = (own_targets_ref, peer_targets_ref)
-    late = columns_of(me, matrix_refs[-1:], 0, count)
-    weights = columns_of(me, matrix_refs, 1, count)
+    weights = square(me, matrix_refs)
     head = head_ref[...]
-
-    def first_block(part):
-        rows = pl.ds(part * half, half)
-        source = own_order(me, source_refs[part], count)
-        activation, gelu_slope = gelu_and_slope(dot(source, late))
-        normed, inverse = norm_parts(jnp.concatenate([activation_ref[rows, :], activation], axis=1))
-        scale_one_ref[rows, :] = jnp.concatenate([slope_ref[rows, :], gelu_slope], axis=1) * inverse
-        normed_one_ref[rows, :] = normed
-        hidden_one_ref[rows, :] = (source.astype(jnp.float32) + normed).astype(jnp.bfloat16)
 
     def second_block(part):
         rows = pl.ds(part * half, half)
@@ -262,12 +259,6 @@
         scale_two_ref[rows, :] = gelu_slope * inverse
         normed_two_ref[rows, :] = normed
         hidden_two_ref[rows, :] = (source.astype(jnp.float32) + normed).astype(jnp.bfloat16)
-
-    def flip_hidden(part):
-        rows = pl.ds(part * half, half)
-        for offset in range(count):
-            flipped = hidden_one_ref[rows, pl.ds(offset * width, width)].T
-            hidden_flip_ref[block_at(me, offset, width), rows] = flipped
 
     def loss_backward(part):
         rows = pl.ds(part * half, half)
@@ -309,8 +300,6 @@
         for turn, ref in enumerate(sent_refs, 1):
             ref[slot] = part[turn * depth : (turn + 1) * depth].astype(jnp.bfloat16)
 
-    first_block(0)
-    first_block(1)
     second_block(0)
     second_block(1)
     loss_backward(0)
@@ -319,8 +308,6 @@
     norm_backward(1, normed_two_ref, scale_two_ref)
     input_backward(0)
     input_backward(1)
-    flip_hidden(0)
-    flip_hidden(1)
     kernel_parts(hidden_flip_ref, 1)
     norm_backward(0, normed_one_ref, scale_one_ref)
     norm_backward(1, normed_one_ref, scale_one_ref)
@@ -332,8 +319,8 @@
 def input_grad_body(count, grad_ref, grad_conv_ref, *refs):
     matrix_refs, input_grad_ref = refs[:count], refs[count]
     me = lax.axis_index("mp")
-    width = matrix_refs[0].shape[2]
-    total = grad_ref[...] + dot(grad_conv_ref[...], columns_of(me, matrix_refs, 0, count), NT)
+    width = matrix_refs[0].shape[1]
+    total = grad_ref[...] + dot(grad_conv_ref[...], square(me, matrix_refs), NT)
     for offset in range(count):
         input_grad_ref[:, block_at(me, offset, width)] = total[
             :, offset * width : (offset + 1) * width
@@ -383,19 +370,26 @@
             cost_estimate=pl.CostEstimate(flops=flops, bytes_accessed=moved, transcendentals=0),
         )
 
-    (own,) = call(
+    matrix = shape((channels, width))
+    own_first, own_second, own_both = call(
         functools.partial(matrices_body, centre_tap),
         [hbm] * 2,
-        (shape((2, channels, width)),),
-        scratch=[pltpu.SemaphoreType.DMA((2,))],
+        (matrix, matrix, shape((2, channels, width))),
+        scratch=[pltpu.SemaphoreType.DMA((4,))],
     )(in_hbm(first_kernel), in_hbm(second_kernel))
-    blocks = {0: own}
-    bit = mp_count // 2
+    first, second = {0: own_first}, {0: own_second}
+    bit = far = mp_count // 2
     while bit:
-        for offset in list(blocks):
-            blocks[offset ^ bit] = swap(blocks[offset], "mp", bit)
+        for offset in list(first):
+            if offset == 0 and bit != far:
+                both = swap(own_both, "mp", bit)
+                first[bit], second[bit] = both[0], both[1]
+            else:
+                first[offset ^ bit] = swap(first[offset], "mp", bit)
+                second[offset ^ bit] = swap(second[offset], "mp", bit)
         bit //= 2
-    blocks = [blocks[offset] for offset in range(mp_count)]
+    first = [first[offset] for offset in range(mp_count)]
+    second = [second[offset] for offset in range(mp_count)]
 
     own_targets, sent_targets, sent_rows = call(
         prepare_body, [vmem] * 3, (shape((SIDE_ROWS, rows)),) * 2 + (shape((rows // 2, channels)),)
@@ -407,34 +401,26 @@
     first_grad, second_grad = call(blank_body, [], (whole, whole))()
 
     pair_rows = 2 * rows
-    early = channels - width
+    wide = shape((pair_rows, channels), jnp.float32)
+    flip = shape((channels, pair_rows))
     product = 2 * pair_rows * channels * channels
-    activation, slope, source_flip, head = call(
-        functools.partial(early_body, mp_count),
-        [vmem] * (3 + mp_count),
-        (
-            shape((pair_rows, early), jnp.float32),
-            shape((pair_rows, early), jnp.float32),
-            shape((channels, pair_rows)),
-            shape((SIDE_ROWS, channels)),
-        ),
+    hidden_one, normed_one, scale_one, hidden_flip, source_flip, head = call(
+        functools.partial(first_block_body, mp_count),
+        [vmem] * (4 + mp_count),
+        (shape((pair_rows, channels)), wide, wide, flip, flip, shape((SIDE_ROWS, channels))),
         flops=product,
         moved=8 * pair_rows * channels,
-    )(hidden_entry_states, far_rows, near_rows, head_weight.T, *blocks[:-1])
+    )(hidden_entry_states, far_rows, near_rows, head_weight.T, *first)
 
     turns = seq_count // 2
     part = (2, depth, width)
     outs = call(
         functools.partial(main_body, mp_count, seq_count, classes),
-        [vmem] * (9 + mp_count),
+        [vmem] * (8 + mp_count),
         (shape(part, jnp.float32),)
         + (shape(part),) * (turns - 1)
         + (shape((rows, channels), jnp.float32), shape((rows, channels))),
         scratch=[
-            pltpu.VMEM((pair_rows, channels), jnp.bfloat16),
-            pltpu.VMEM((pair_rows, channels), jnp.float32),
-            pltpu.VMEM((pair_rows, channels), jnp.float32),
-            pltpu.VMEM((channels, pair_rows), jnp.bfloat16),
             pltpu.VMEM((pair_rows, channels), jnp.float32),
             pltpu.VMEM((pair_rows, channels), jnp.float32),
             pltpu.VMEM((pair_rows, channels), jnp.bfloat16),
@@ -443,7 +429,7 @@
         ],
         flops=3 * product,
         moved=16 * pair_rows * channels,
-    )(hidden_entry_states, far_rows, near_rows, own_targets, peer_targets, activation, slope, source_flip, head, *blocks)
+    )(own_targets, peer_targets, hidden_one, normed_one, scale_one, hidden_flip, source_flip, head, *second)
     own_part, sent, (grad_one, grad_conv) = outs[0], outs[1:-2], outs[-2:]
 
     received = [swap(piece, "seq", turn) for turn, piece in enumerate(sent, 1)]
@@ -453,7 +439,7 @@
         (shape((rows, channels)),),
         flops=product // 2,
         moved=8 * rows * channels,
-    )(grad_one, grad_conv, *blocks)
+    )(grad_one, grad_conv, *first)
     first_grad, second_grad, input_grad = call(
         functools.partial(total_body, centre_tap),
         [hbm, hbm] + [vmem] * (1 + turns),

time: 33.4 us -> 23.1 us (0.69)
  waiting for transfers between devices: 16.2 us -> 6.05 us
  starting transfers between devices: 10.8 us -> 10.4 us
    ppermute x9 -> x11, waiting for transfers between devices: 16.2 us -> 6.05 us  [swap(): lax.ppermute(block, axis, [(i, i ^ offset) for i in range(lax.axis_size(a...]
    pallas_call x2, Pallas kernels: 1.4 us -> 1.91 us  [the longest x1 1.17 us: local_plan(): call(functools.partial(matrices_body, centre_tap), [hbm] * 2, (matrix, ma...]
    pallas_call x1, Pallas kernels: 2.12 us -> 1.74 us  [local_plan(): call(functools.partial(main_body, mp_count, seq_count, classes), [vmem] *...]
    ppermute x9 -> x11, starting transfers between devices: 10.8 us -> 10.4 us  [swap(): lax.ppermute(block, axis, [(i, i ^ offset) for i in range(lax.axis_size(a...]
  transfers between devices with their start and end apart: 9 -> 11, of which waited for: 5 -> 6; matrix products, arithmetic and copies ran while one was open for 0% -> 0% of each run, Pallas kernels for 5% -> 9%
where the time goes in v5:
time: 23.1 us; the launch traced here: 22.9 us
  starting transfers between devices  10.4 us (45%)
  waiting for transfers between devices  6.05 us (26%)
  Pallas kernels  5.67 us (25%)
  between operations  0.72 us (3%)
    ppermute x11, starting transfers between devices, swap(): lax.ppermute(block, axis, [(i, i ^ offset) for i in range(lax.axis_size(a...  10.4 us
    ppermute x11, waiting for transfers between devices, swap(): lax.ppermute(block, axis, [(i, i ^ offset) for i in range(lax.axis_size(a...  6.05 us
    pallas_call x1, Pallas kernels, local_plan(): call(functools.partial(main_body, mp_count, seq_count, classes), [vmem] *...  1.74 us
    pallas_call x1, Pallas kernels, local_plan(): call(functools.partial(matrices_body, centre_tap), [hbm] * 2, (matrix, ma...  1.17 us
    pallas_call x1, Pallas kernels, local_plan(): first_grad, second_grad = call(blank_body, [], (whole, whole))()  0.83 us
    pallas_call x1, Pallas kernels, local_plan(): call(functools.partial(first_block_body, mp_count), [vmem] * (4 + mp_coun...  0.74 us
    pallas_call x1, Pallas kernels, local_plan(): call(functools.partial(total_body, centre_tap), [hbm, hbm] + [vmem] * (1...  0.69 us
  transfers between devices with their start and end apart: 11, of which 6 were waited for; matrix products, arithmetic and copies ran while one was open for 0% of the time, Pallas kernels for 9%

profile of v5, /device:TPU:0, one launch (start us, length us, event | category | flops | bytes accessed | tf_op | source)
XLA Modules:
  0.0 22.9 jit_solution(14435020673992089775)
XLA Ops:
  0.7 1.2 %shard_map.87 = (bf16[512,128]{1,0:T(8,128)(2,1)S(1)}, bf16[512,128]{1,0:T(8,128)(2,1)S(1)}, bf16[2,512,128]{2,1,0:T(8,128)(2,1)S(1)}) custom-call(bf16[9,512,128]{2,1,0:T(8,128)(2,1)} %first_ref.1, bf16[9,512,128]{2,1,0:T(8,128)(2,1)} %second_ref.1), custom_call_target="tpu_custom_call" | custom-call | tf_op jit(solution)/shard_map/pallas_call | solution.py:374
  1.9 0.6 %collective-permute-start.3 = (bf16[2,512,128]{2,1,0:T(8,128)(2,1)S(1)}, bf16[2,512,128]{2,1,0:T(8,128)(2,1)S(1)}, u32[]{:S(2)}, u32[]{:S(2)}) collective-permute-start(bf16[2,512,128]{2,1,0:T(8,128)(2,1)S(1)} %get-tuple-element.32), channel_id=1, source_target_pairs={{0,1},{1,0},{2,3},{3,2},{4,5},{5,4},{6,7},{7,6},{8,9},{9,8},{10,11... | collective-permute-start | bytes 786440 | tf_op jit(solution)/shard_map/ppermute | solution.py:149
  2.4 2.6 %collective-permute-start.4 = (bf16[512,128]{1,0:T(8,128)(2,1)S(1)}, bf16[512,128]{1,0:T(8,128)(2,1)S(1)}, u32[]{:S(2)}, u32[]{:S(2)}) collective-permute-start(bf16[512,128]{1,0:T(8,128)(2,1)S(1)} %get-tuple-element.31.refs_0_), channel_id=1, source_target_pairs={{0,2},{1,3},{2,0},{3,1},{4,6},{5,7},{6,4},{7,5},{8,10},{9,11},{10,... | collective-permute-start | bytes 393224 | tf_op jit(solution)/shard_map/ppermute | solution.py:149
  5.0 0.1 collective-permute-start.6
  5.0 0.2 shard_map.86
  5.2 3.0 %collective-permute-start.1 = (bf16[64,512]{1,0:T(8,128)(2,1)S(1)}, bf16[64,512]{1,0:T(8,128)(2,1)S(1)}, u32[]{:S(2)}, u32[]{:S(2)}) collective-permute-start(bf16[64,512]{1,0:T(8,128)(2,1)S(1)} %get-tuple-element.30), channel_id=1, source_target_pairs={{0,16},{4,20},{8,24},{12,28},{16,0},{20,4},{24,8},{28,12},{1,17},{... | collective-permute-start | bytes 196616 | tf_op jit(solution)/shard_map/ppermute | solution.py:149
  8.3 0.1 collective-permute-start
  8.3 3.6 %collective-permute-done.1.far_ref = bf16[64,512]{1,0:T(8,128)(2,1)S(1)} collective-permute-done((bf16[64,512]{1,0:T(8,128)(2,1)S(1)}, bf16[64,512]{1,0:T(8,128)(2,1)S(1)}, u32[]{:S(2)}, u32[]{:S(2)}) %collective-permute-start.1) | collective-permute-done | bytes 65568 | tf_op jit(solution)/shard_map/ppermute | solution.py:149
  12.0 0.0 collective-permute-start.2
  12.0 0.5 %collective-permute-start.5 = (bf16[512,128]{1,0:T(8,128)(2,1)S(1)}, bf16[512,128]{1,0:T(8,128)(2,1)S(1)}, u32[]{:S(2)}, u32[]{:S(2)}) collective-permute-start(bf16[512,128]{1,0:T(8,128)(2,1)S(1)} %collective-permute-done.4.refs_2_), channel_id=1, source_target_pairs={{0,1},{1,0},{2,3},{3,2},{4,5},{5,4},{6,7},{7,6},{8,9},{9,8},{10,11... | collective-permute-start | bytes 393224 | tf_op jit(solution)/shard_map/ppermute | solution.py:149
  12.5 0.1 collective-permute-start.7
  12.6 0.6 %collective-permute-done.2.near_ref = bf16[64,512]{1,0:T(8,128)(2,1)S(1)} collective-permute-done((bf16[64,512]{1,0:T(8,128)(2,1)S(1)}, bf16[64,512]{1,0:T(8,128)(2,1)S(1)}, u32[]{:S(2)}, u32[]{:S(2)}) %collective-permute-start.2) | collective-permute-done | bytes 65568 | tf_op jit(solution)/shard_map/ppermute | solution.py:149
  13.2 0.2 %collective-permute-done.5.refs_3_ = bf16[512,128]{1,0:T(8,128)(2,1)S(1)} collective-permute-done((bf16[512,128]{1,0:T(8,128)(2,1)S(1)}, bf16[512,128]{1,0:T(8,128)(2,1)S(1)}, u32[]{:S(2)}, u32[]{:S(2)}) %collective-permute-start.5) | collective-permute-done | bytes 131104 | tf_op jit(solution)/shard_map/ppermute | solution.py:149
  13.5 0.7 %shard_map.88 = (bf16[256,512]{1,0:T(8,128)(2,1)S(1)}, f32[256,512]{1,0:T(8,128)S(1)}, f32[256,512]{1,0:T(8,128)S(1)}, bf16[512,256]{1,0:T(8,128)(2,1)S(1)}, bf1...) custom-call(bf16[128,512]{1,0:T(8,128)(2,1)S(1)} %copy-done, bf16[64,512]{1,0:T(8,128)(2,1)S(1)} %collective-permute-done.1.far_ref, ...), custom_call_target="tpu_custom_call" | custom-call | flops 134217728 | bytes 1048576 | tf_op jit(solution)/shard_map/pallas_call | solution.py:407
  14.2 1.7 %shard_map.89 = (f32[2,64,128]{2,1,0:T(8,128)S(1)}, bf16[2,64,128]{2,1,0:T(8,128)(2,1)S(1)}, bf16[2,64,128]{2,1,0:T(8,128)(2,1)S(1)}, bf16[2,64,128]{2,1,0:T(8,1...) custom-call(bf16[16,128]{1,0:T(8,128)(2,1)S(1)} %get-tuple-element.28.own_targets_ref, ...), custom_call_target="tpu_custom_call" | custom-call | flops 402653184 | bytes 2097152 | tf_op jit(solution)/shard_map/pallas_call | solution.py:417
  16.0 1.8 %collective-permute-start.10 = (bf16[2,64,128]{2,1,0:T(8,128)(2,1)S(1)}, bf16[2,64,128]{2,1,0:T(8,128)(2,1)S(1)}, u32[]{:S(2)}, u32[]{:S(2)}) collective-permute-start(bf16[2,64,128]{2,1,0:T(8,128)(2,1)S(1)} %get-tuple-element.45), channel_id=1, source_target_pairs={{0,12},{4,8},{8,4},{12,0},{16,28},{20,24},{24,20},{28,16},{1,13},{... | collective-permute-start | bytes 98312 | tf_op jit(solution)/shard_map/ppermute | solution.py:149
  17.8 0.5 %collective-permute-start.8 = (bf16[2,64,128]{2,1,0:T(8,128)(2,1)S(1)}, bf16[2,64,128]{2,1,0:T(8,128)(2,1)S(1)}, u32[]{:S(2)}, u32[]{:S(2)}) collective-permute-start(bf16[2,64,128]{2,1,0:T(8,128)(2,1)S(1)} %get-tuple-element.43), channel_id=1, source_target_pairs={{0,4},{4,0},{8,12},{12,8},{16,20},{20,16},{24,28},{28,24},{1,5},{5... | collective-permute-start | bytes 98312 | tf_op jit(solution)/shard_map/ppermute | solution.py:149
  18.3 1.2 %collective-permute-start.9 = (bf16[2,64,128]{2,1,0:T(8,128)(2,1)S(1)}, bf16[2,64,128]{2,1,0:T(8,128)(2,1)S(1)}, u32[]{:S(2)}, u32[]{:S(2)}) collective-permute-start(bf16[2,64,128]{2,1,0:T(8,128)(2,1)S(1)} %get-tuple-element.44), channel_id=1, source_target_pairs={{0,8},{4,12},{8,0},{12,4},{16,24},{20,28},{24,16},{28,20},{1,9},{5... | collective-permute-start | bytes 98312 | tf_op jit(solution)/shard_map/ppermute | solution.py:149
  19.5 0.8 %shard_map.85 = (f32[9,64,128]{2,1,0:T(8,128)}, f32[9,64,128]{2,1,0:T(8,128)}) custom-call(), custom_call_target="tpu_custom_call" | custom-call | tf_op jit(solution)/shard_map/pallas_call | solution.py:401
  20.4 0.3 %shard_map.90.input_grad_ref = bf16[128,512]{1,0:T(8,128)(2,1)S(1)} custom-call(f32[128,512]{1,0:T(8,128)S(1)} %get-tuple-element.40.grad_ref, bf16[128,512]{1,0:T(8,128)(2,1)S(1)} %get-tuple-element.41.grad_conv_ref, bf16[512,128]{1,0:T(8,128)(2,1)S(1)} %get-tuple-element.31.refs_0_, bf16[512,128]{1,0:T(8,128)(2,1)S(1)} %get-tuple-element.50.refs_1_, ...), custom_call_target="tpu_custom_call" | custom-call | flops 67108864 | bytes 524288 | tf_op jit(solution)/shard_map/pallas_call | solution.py:436
  20.7 0.3 %collective-permute-done.10.refs_2_ = bf16[2,64,128]{2,1,0:T(8,128)(2,1)S(1)} collective-permute-done((bf16[2,64,128]{2,1,0:T(8,128)(2,1)S(1)}, bf16[2,64,128]{2,1,0:T(8,128)(2,1)S(1)}, u32[]{:S(2)}, u32[]{:S(2)}) %collective-permute-start.10) | collective-permute-done | bytes 32800 | tf_op jit(solution)/shard_map/ppermute | solution.py:149
  21.0 0.8 %collective-permute-done.8.refs_0_ = bf16[2,64,128]{2,1,0:T(8,128)(2,1)S(1)} collective-permute-done((bf16[2,64,128]{2,1,0:T(8,128)(2,1)S(1)}, bf16[2,64,128]{2,1,0:T(8,128)(2,1)S(1)}, u32[]{:S(2)}, u32[]{:S(2)}) %collective-permute-start.8) | collective-permute-done | bytes 32800 | tf_op jit(solution)/shard_map/ppermute | solution.py:149
  21.7 0.5 %collective-permute-done.9.refs_1_ = bf16[2,64,128]{2,1,0:T(8,128)(2,1)S(1)} collective-permute-done((bf16[2,64,128]{2,1,0:T(8,128)(2,1)S(1)}, bf16[2,64,128]{2,1,0:T(8,128)(2,1)S(1)}, u32[]{:S(2)}, u32[]{:S(2)}) %collective-permute-start.9) | collective-permute-done | bytes 32800 | tf_op jit(solution)/shard_map/ppermute | solution.py:149
  22.2 0.7 %shard_map.91 = (f32[9,64,128]{2,1,0:T(8,128)}, f32[9,64,128]{2,1,0:T(8,128)}, bf16[128,512]{1,0:T(8,128)(2,1)}) custom-call(f32[9,64,128]{2,1,0:T(8,128)} %get-tuple-element.26.first_in_ref, f32[9,64,128]{2,1,0:T(8,128)} %get-tuple-element.27.second_in_ref, ...), custom_call_target="tpu_custom_call", output_to_operand_aliasing={{0}: (0, {}), {1}: (1, {})} | custom-call | tf_op jit(solution)/shard_map/pallas_call | solution.py:443
  (14 shorter events, 0.0 us)
Async XLA Ops:
  0.6 4.4 %copy-start.2 = (s32[16]{0:T(128)S(1)}, s32[16]{0:T(128)}, u32[]{:S(2)}) copy-start(s32[16]{0:T(128)} %param.8) | copy-start | bytes 196
  0.6 4.4 %copy-start.3 = (s32[128]{0:T(128)S(1)}, s32[128]{0:T(128)}, u32[]{:S(2)}) copy-start(s32[128]{0:T(128)} %param.7) | copy-start | bytes 1540
  0.7 4.4 %copy-start = (bf16[128,512]{1,0:T(8,128)(2,1)S(1)}, bf16[128,512]{1,0:T(8,128)(2,1)}, u32[]{:S(2)}) copy-start(bf16[128,512]{1,0:T(8,128)(2,1)} %own_ref.1) | copy-start | bytes 393220
  0.7 12.8 %copy-start.1 = (bf16[512,5]{0,1:T(8,128)(2,1)S(1)}, bf16[512,5]{0,1:T(8,128)(2,1)}, u32[]{:S(2)}) copy-start(bf16[512,5]{0,1:T(8,128)(2,1)} %param.11) | copy-start | bytes 15364
  1.9 10.7 %collective-permute-start.3 = (bf16[2,512,128]{2,1,0:T(8,128)(2,1)S(1)}, bf16[2,512,128]{2,1,0:T(8,128)(2,1)S(1)}, u32[]{:S(2)}, u32[]{:S(2)}) collective-permute-start(bf16[2,512,128]{2,1,0:T(8,128)(2,1)S(1)} %get-tuple-element.32), channel_id=1, source_target_pairs={{0,1},{1,0},{2,3},{3,2},{4,5},{5,4},{6,7},{7,6},{8,9},{9,8},{10,11... | collective-permute-start | bytes 786440 | tf_op jit(solution)/shard_map/ppermute | solution.py:149
  2.4 9.6 %collective-permute-start.4 = (bf16[512,128]{1,0:T(8,128)(2,1)S(1)}, bf16[512,128]{1,0:T(8,128)(2,1)S(1)}, u32[]{:S(2)}, u32[]{:S(2)}) collective-permute-start(bf16[512,128]{1,0:T(8,128)(2,1)S(1)} %get-tuple-element.31.refs_0_), channel_id=1, source_target_pairs={{0,2},{1,3},{2,0},{3,1},{4,6},{5,7},{6,4},{7,5},{8,10},{9,11},{10,... | collective-permute-start | bytes 393224 | tf_op jit(solution)/shard_map/ppermute | solution.py:149
  5.0 7.5 %collective-permute-start.6 = (bf16[512,128]{1,0:T(8,128)(2,1)S(1)}, bf16[512,128]{1,0:T(8,128)(2,1)S(1)}, u32[]{:S(2)}, u32[]{:S(2)}) collective-permute-start(bf16[512,128]{1,0:T(8,128)(2,1)S(1)} %get-tuple-element.39.refs_0_), channel_id=1, source_target_pairs={{0,2},{1,3},{2,0},{3,1},{4,6},{5,7},{6,4},{7,5},{8,10},{9,11},{10,... | collective-permute-start | bytes 393224 | tf_op jit(solution)/shard_map/ppermute | solution.py:149
  5.2 6.7 %collective-permute-start.1 = (bf16[64,512]{1,0:T(8,128)(2,1)S(1)}, bf16[64,512]{1,0:T(8,128)(2,1)S(1)}, u32[]{:S(2)}, u32[]{:S(2)}) collective-permute-start(bf16[64,512]{1,0:T(8,128)(2,1)S(1)} %get-tuple-element.30), channel_id=1, source_target_pairs={{0,16},{4,20},{8,24},{12,28},{16,0},{20,4},{24,8},{28,12},{1,17},{... | collective-permute-start | bytes 196616 | tf_op jit(solution)/shard_map/ppermute | solution.py:149
  8.3 5.9 %collective-permute-start = (bf16[16,128]{1,0:T(8,128)(2,1)S(1)}, bf16[16,128]{1,0:T(8,128)(2,1)S(1)}, u32[]{:S(2)}, u32[]{:S(2)}) collective-permute-start(bf16[16,128]{1,0:T(8,128)(2,1)S(1)} %get-tuple-element.29), channel_id=1, source_target_pairs={{0,16},{4,20},{8,24},{12,28},{16,0},{20,4},{24,8},{28,12},{1,17},{... | collective-permute-start | bytes 12296 | tf_op jit(solution)/shard_map/ppermute | solution.py:149
  12.0 1.3 %collective-permute-start.2 = (bf16[64,512]{1,0:T(8,128)(2,1)S(1)}, bf16[64,512]{1,0:T(8,128)(2,1)S(1)}, u32[]{:S(2)}, u32[]{:S(2)}) collective-permute-start(bf16[64,512]{1,0:T(8,128)(2,1)S(1)} %collective-permute-done.1.far_ref), channel_id=1, source_target_pairs={{0,1},{1,0},{2,3},{3,2},{4,5},{5,4},{6,7},{7,6},{8,9},{9,8},{10,11... | collective-permute-start | bytes 196616 | tf_op jit(solution)/shard_map/ppermute | solution.py:149
  12.0 1.5 %collective-permute-start.5 = (bf16[512,128]{1,0:T(8,128)(2,1)S(1)}, bf16[512,128]{1,0:T(8,128)(2,1)S(1)}, u32[]{:S(2)}, u32[]{:S(2)}) collective-permute-start(bf16[512,128]{1,0:T(8,128)(2,1)S(1)} %collective-permute-done.4.refs_2_), channel_id=1, source_target_pairs={{0,1},{1,0},{2,3},{3,2},{4,5},{5,4},{6,7},{7,6},{8,9},{9,8},{10,11... | collective-permute-start | bytes 393224 | tf_op jit(solution)/shard_map/ppermute | solution.py:149
  12.5 1.7 %collective-permute-start.7 = (bf16[512,128]{1,0:T(8,128)(2,1)S(1)}, bf16[512,128]{1,0:T(8,128)(2,1)S(1)}, u32[]{:S(2)}, u32[]{:S(2)}) collective-permute-start(bf16[512,128]{1,0:T(8,128)(2,1)S(1)} %collective-permute-done.6.refs_2_), channel_id=1, source_target_pairs={{0,1},{1,0},{2,3},{3,2},{4,5},{5,4},{6,7},{7,6},{8,9},{9,8},{10,11... | collective-permute-start | bytes 393224 | tf_op jit(solution)/shard_map/ppermute | solution.py:149
  16.0 5.0 %collective-permute-start.10 = (bf16[2,64,128]{2,1,0:T(8,128)(2,1)S(1)}, bf16[2,64,128]{2,1,0:T(8,128)(2,1)S(1)}, u32[]{:S(2)}, u32[]{:S(2)}) collective-permute-start(bf16[2,64,128]{2,1,0:T(8,128)(2,1)S(1)} %get-tuple-element.45), channel_id=1, source_target_pairs={{0,12},{4,8},{8,4},{12,0},{16,28},{20,24},{24,20},{28,16},{1,13},{... | collective-permute-start | bytes 98312 | tf_op jit(solution)/shard_map/ppermute | solution.py:149
  17.8 3.9 %collective-permute-start.8 = (bf16[2,64,128]{2,1,0:T(8,128)(2,1)S(1)}, bf16[2,64,128]{2,1,0:T(8,128)(2,1)S(1)}, u32[]{:S(2)}, u32[]{:S(2)}) collective-permute-start(bf16[2,64,128]{2,1,0:T(8,128)(2,1)S(1)} %get-tuple-element.43), channel_id=1, source_target_pairs={{0,4},{4,0},{8,12},{12,8},{16,20},{20,16},{24,28},{28,24},{1,5},{5... | collective-permute-start | bytes 98312 | tf_op jit(solution)/shard_map/ppermute | solution.py:149
  18.3 3.9 %collective-permute-start.9 = (bf16[2,64,128]{2,1,0:T(8,128)(2,1)S(1)}, bf16[2,64,128]{2,1,0:T(8,128)(2,1)S(1)}, u32[]{:S(2)}, u32[]{:S(2)}) collective-permute-start(bf16[2,64,128]{2,1,0:T(8,128)(2,1)S(1)} %get-tuple-element.44), channel_id=1, source_target_pairs={{0,8},{4,12},{8,0},{12,4},{16,24},{20,28},{24,16},{28,20},{1,9},{5... | collective-permute-start | bytes 98312 | tf_op jit(solution)/shard_map/ppermute | solution.py:149

commit v6 on v5

--- a/solution.py
+++ b/solution.py
@@ -164,11 +164,10 @@
     )
 
 
-def matrices_body(centre_tap, first_ref, second_ref, own_first_ref, own_second_ref, both_ref, sems):
-    targets = (own_first_ref, own_second_ref, both_ref.at[0], both_ref.at[1])
+def matrices_body(centre_tap, first_ref, second_ref, own_first_ref, own_second_ref, sems):
     copies = [
-        pltpu.make_async_copy(source.at[centre_tap], target, sems.at[n])
-        for n, (source, target) in enumerate(zip((first_ref, second_ref) * 2, targets))
+        pltpu.make_async_copy(first_ref.at[centre_tap], own_first_ref, sems.at[0]),
+        pltpu.make_async_copy(second_ref.at[centre_tap], own_second_ref, sems.at[1]),
     ]
     for copy in copies:
         copy.start()
@@ -176,7 +175,7 @@
         copy.wait()
 
 
-def prepare_body(mask_ref, ids_ref, source_ref, own_ref, sent_targets_ref, sent_ref):
+def prepare_body(mask_ref, ids_ref, source_ref, own_first_ref, own_second_ref, own_ref, sent_targets_ref, sent_ref, both_ref):
     rows = source_ref.shape[0]
     share = rows // 2
     entries = mask_ref.shape[1]
@@ -192,6 +191,8 @@
     turned = pltpu.roll(targets, share, 1)
     own_ref[...] = targets.astype(jnp.bfloat16)
     sent_targets_ref[...] = jnp.where(part == 1, turned, targets).astype(jnp.bfloat16)
+    both_ref[0] = own_first_ref[...]
+    both_ref[1] = own_second_ref[...]
     sent_ref[...] = source_ref[pl.ds(pl.multiple_of(part * share, share), share), :]
 
 
@@ -371,12 +372,17 @@
         )
 
     matrix = shape((channels, width))
-    own_first, own_second, own_both = call(
+    own_first, own_second = call(
         functools.partial(matrices_body, centre_tap),
         [hbm] * 2,
-        (matrix, matrix, shape((2, channels, width))),
-        scratch=[pltpu.SemaphoreType.DMA((4,))],
+        (matrix, matrix),
+        scratch=[pltpu.SemaphoreType.DMA((2,))],
     )(in_hbm(first_kernel), in_hbm(second_kernel))
+    own_targets, sent_targets, sent_rows, own_both = call(
+        prepare_body,
+        [vmem] * 5,
+        (shape((SIDE_ROWS, rows)),) * 2 + (shape((rows // 2, channels)), shape((2, channels, width))),
+    )(mask_index[None, :], base_ids[None, :], hidden_entry_states, own_first, own_second)
     first, second = {0: own_first}, {0: own_second}
     bit = far = mp_count // 2
     while bit:
@@ -391,9 +397,6 @@
     first = [first[offset] for offset in range(mp_count)]
     second = [second[offset] for offset in range(mp_count)]
 
-    own_targets, sent_targets, sent_rows = call(
-        prepare_body, [vmem] * 3, (shape((SIDE_ROWS, rows)),) * 2 + (shape((rows // 2, channels)),)
-    )(mask_index[None, :], base_ids[None, :], hidden_entry_states)
     far_rows = swap(sent_rows, "seq", seq_count // 2)
     near_rows = swap(far_rows, "mp", 1)
     peer_targets = swap(sent_targets, "seq", seq_count // 2)

time: 23.1 us -> 23.1 us (level)
    ppermute x11, waiting for transfers between devices: 6.05 us -> 6.28 us  [swap(): lax.ppermute(block, axis, [(i, i ^ offset) for i in range(lax.axis_size(a...]
  transfers between devices with their start and end apart: 11 -> 11, of which waited for: 6 -> 6; matrix products, arithmetic and copies ran while one was open for 0% -> 0% of each run, Pallas kernels for 9% -> 8%
where the time goes in v6:
time: 23.1 us; the launch traced here: 22.9 us
  starting transfers between devices  10.3 us (45%)
  waiting for transfers between devices  6.28 us (27%)
  Pallas kernels  5.52 us (24%)
  between operations  0.75 us (3%)
    ppermute x11, starting transfers between devices, swap(): lax.ppermute(block, axis, [(i, i ^ offset) for i in range(lax.axis_size(a...  10.3 us
    ppermute x11, waiting for transfers between devices, swap(): lax.ppermute(block, axis, [(i, i ^ offset) for i in range(lax.axis_size(a...  6.28 us
    pallas_call x1, Pallas kernels, local_plan(): call(functools.partial(main_body, mp_count, seq_count, classes), [vmem] *...  1.74 us
    pallas_call x1, Pallas kernels, local_plan(): call(functools.partial(matrices_body, centre_tap), [hbm] * 2, (matrix, ma...  1.03 us
    pallas_call x1, Pallas kernels, local_plan(): first_grad, second_grad = call(blank_body, [], (whole, whole))()  0.83 us
    pallas_call x1, Pallas kernels, local_plan(): call(functools.partial(first_block_body, mp_count), [vmem] * (4 + mp_coun...  0.74 us
    pallas_call x1, Pallas kernels, local_plan(): call(functools.partial(total_body, centre_tap), [hbm, hbm] + [vmem] * (1...  0.69 us
  transfers between devices with their start and end apart: 11, of which 6 were waited for; matrix products, arithmetic and copies ran while one was open for 0% of the time, Pallas kernels for 8%

profile of v6, /device:TPU:0, one launch (start us, length us, event | category | flops | bytes accessed | tf_op | source)
XLA Modules:
  0.0 22.9 jit_solution(2571070490526353759)
XLA Ops:
  0.7 1.0 %shard_map.86 = (bf16[512,128]{1,0:T(8,128)(2,1)S(1)}, bf16[512,128]{1,0:T(8,128)(2,1)S(1)}) custom-call(bf16[9,512,128]{2,1,0:T(8,128)(2,1)} %first_ref.1, bf16[9,512,128]{2,1,0:T(8,128)(2,1)} %second_ref.1), custom_call_target="tpu_custom_call" | custom-call | tf_op jit(solution)/shard_map/pallas_call | solution.py:375
  1.7 0.2 shard_map.87
  1.9 0.5 %collective-permute-start.3 = (bf16[2,512,128]{2,1,0:T(8,128)(2,1)S(1)}, bf16[2,512,128]{2,1,0:T(8,128)(2,1)S(1)}, u32[]{:S(2)}, u32[]{:S(2)}) collective-permute-start(bf16[2,512,128]{2,1,0:T(8,128)(2,1)S(1)} %get-tuple-element.33), channel_id=1, source_target_pairs={{0,1},{1,0},{2,3},{3,2},{4,5},{5,4},{6,7},{7,6},{8,9},{9,8},{10,11... | collective-permute-start | bytes 786440 | tf_op jit(solution)/shard_map/ppermute | solution.py:149
  2.4 2.6 %collective-permute-start.4 = (bf16[512,128]{1,0:T(8,128)(2,1)S(1)}, bf16[512,128]{1,0:T(8,128)(2,1)S(1)}, u32[]{:S(2)}, u32[]{:S(2)}) collective-permute-start(bf16[512,128]{1,0:T(8,128)(2,1)S(1)} %get-tuple-element.28.own_first_ref.refs_0_), channel_id=1, source_target_pairs={{0,2},{1,3},{2,0},{3,1},{4,6},{5,7},{6,4},{7,5},{8,10},{9,11},{10,... | collective-permute-start | bytes 393224 | tf_op jit(solution)/shard_map/ppermute | solution.py:149
  5.0 0.1 collective-permute-start.6
  5.0 3.0 %collective-permute-start.1 = (bf16[64,512]{1,0:T(8,128)(2,1)S(1)}, bf16[64,512]{1,0:T(8,128)(2,1)S(1)}, u32[]{:S(2)}, u32[]{:S(2)}) collective-permute-start(bf16[64,512]{1,0:T(8,128)(2,1)S(1)} %get-tuple-element.32), channel_id=1, source_target_pairs={{0,16},{4,20},{8,24},{12,28},{16,0},{20,4},{24,8},{28,12},{1,17},{... | collective-permute-start | bytes 196616 | tf_op jit(solution)/shard_map/ppermute | solution.py:149
  8.1 0.0 collective-permute-start
  8.1 3.7 %collective-permute-done.1.far_ref = bf16[64,512]{1,0:T(8,128)(2,1)S(1)} collective-permute-done((bf16[64,512]{1,0:T(8,128)(2,1)S(1)}, bf16[64,512]{1,0:T(8,128)(2,1)S(1)}, u32[]{:S(2)}, u32[]{:S(2)}) %collective-permute-start.1) | collective-permute-done | bytes 65568 | tf_op jit(solution)/shard_map/ppermute | solution.py:149
  11.8 0.5 %collective-permute-start.5 = (bf16[512,128]{1,0:T(8,128)(2,1)S(1)}, bf16[512,128]{1,0:T(8,128)(2,1)S(1)}, u32[]{:S(2)}, u32[]{:S(2)}) collective-permute-start(bf16[512,128]{1,0:T(8,128)(2,1)S(1)} %collective-permute-done.4.refs_2_), channel_id=1, source_target_pairs={{0,1},{1,0},{2,3},{3,2},{4,5},{5,4},{6,7},{7,6},{8,9},{9,8},{10,11... | collective-permute-start | bytes 393224 | tf_op jit(solution)/shard_map/ppermute | solution.py:149
  12.3 0.1 collective-permute-start.7
  12.4 0.6 %collective-permute-done.2.near_ref = bf16[64,512]{1,0:T(8,128)(2,1)S(1)} collective-permute-done((bf16[64,512]{1,0:T(8,128)(2,1)S(1)}, bf16[64,512]{1,0:T(8,128)(2,1)S(1)}, u32[]{:S(2)}, u32[]{:S(2)}) %collective-permute-start.2) | collective-permute-done | bytes 65568 | tf_op jit(solution)/shard_map/ppermute | solution.py:149
  13.0 0.2 %collective-permute-done.5.refs_3_ = bf16[512,128]{1,0:T(8,128)(2,1)S(1)} collective-permute-done((bf16[512,128]{1,0:T(8,128)(2,1)S(1)}, bf16[512,128]{1,0:T(8,128)(2,1)S(1)}, u32[]{:S(2)}, u32[]{:S(2)}) %collective-permute-start.5) | collective-permute-done | bytes 131104 | tf_op jit(solution)/shard_map/ppermute | solution.py:149
  13.3 0.7 %shard_map.88 = (bf16[256,512]{1,0:T(8,128)(2,1)S(1)}, f32[256,512]{1,0:T(8,128)S(1)}, f32[256,512]{1,0:T(8,128)S(1)}, bf16[512,256]{1,0:T(8,128)(2,1)S(1)}, bf1...) custom-call(bf16[128,512]{1,0:T(8,128)(2,1)S(1)} %copy-done, bf16[64,512]{1,0:T(8,128)(2,1)S(1)} %collective-permute-done.1.far_ref, ...), custom_call_target="tpu_custom_call" | custom-call | flops 134217728 | bytes 1048576 | tf_op jit(solution)/shard_map/pallas_call | solution.py:410
  14.0 0.0 collective-permute-done.peer_targets_ref
  14.0 1.7 %shard_map.89 = (f32[2,64,128]{2,1,0:T(8,128)S(1)}, bf16[2,64,128]{2,1,0:T(8,128)(2,1)S(1)}, bf16[2,64,128]{2,1,0:T(8,128)(2,1)S(1)}, bf16[2,64,128]{2,1,0:T(8,1...) custom-call(bf16[16,128]{1,0:T(8,128)(2,1)S(1)} %get-tuple-element.30.own_targets_ref, ...), custom_call_target="tpu_custom_call" | custom-call | flops 402653184 | bytes 2097152 | tf_op jit(solution)/shard_map/pallas_call | solution.py:420
  15.8 2.0 %collective-permute-start.10 = (bf16[2,64,128]{2,1,0:T(8,128)(2,1)S(1)}, bf16[2,64,128]{2,1,0:T(8,128)(2,1)S(1)}, u32[]{:S(2)}, u32[]{:S(2)}) collective-permute-start(bf16[2,64,128]{2,1,0:T(8,128)(2,1)S(1)} %get-tuple-element.45), channel_id=1, source_target_pairs={{0,12},{4,8},{8,4},{12,0},{16,28},{20,24},{24,20},{28,16},{1,13},{... | collective-permute-start | bytes 98312 | tf_op jit(solution)/shard_map/ppermute | solution.py:149
  17.8 0.5 %collective-permute-start.8 = (bf16[2,64,128]{2,1,0:T(8,128)(2,1)S(1)}, bf16[2,64,128]{2,1,0:T(8,128)(2,1)S(1)}, u32[]{:S(2)}, u32[]{:S(2)}) collective-permute-start(bf16[2,64,128]{2,1,0:T(8,128)(2,1)S(1)} %get-tuple-element.43), channel_id=1, source_target_pairs={{0,4},{4,0},{8,12},{12,8},{16,20},{20,16},{24,28},{28,24},{1,5},{5... | collective-permute-start | bytes 98312 | tf_op jit(solution)/shard_map/ppermute | solution.py:149
  18.3 1.0 %collective-permute-start.9 = (bf16[2,64,128]{2,1,0:T(8,128)(2,1)S(1)}, bf16[2,64,128]{2,1,0:T(8,128)(2,1)S(1)}, u32[]{:S(2)}, u32[]{:S(2)}) collective-permute-start(bf16[2,64,128]{2,1,0:T(8,128)(2,1)S(1)} %get-tuple-element.44), channel_id=1, source_target_pairs={{0,8},{4,12},{8,0},{12,4},{16,24},{20,28},{24,16},{28,20},{1,9},{5... | collective-permute-start | bytes 98312 | tf_op jit(solution)/shard_map/ppermute | solution.py:149
  19.3 0.8 %shard_map.85 = (f32[9,64,128]{2,1,0:T(8,128)}, f32[9,64,128]{2,1,0:T(8,128)}) custom-call(), custom_call_target="tpu_custom_call" | custom-call | tf_op jit(solution)/shard_map/pallas_call | solution.py:404
  20.2 0.3 %shard_map.90.input_grad_ref = bf16[128,512]{1,0:T(8,128)(2,1)S(1)} custom-call(f32[128,512]{1,0:T(8,128)S(1)} %get-tuple-element.40.grad_ref, bf16[128,512]{1,0:T(8,128)(2,1)S(1)} %get-tuple-element.41.grad_conv_ref, bf16[512,128]{1,0:T(8,128)(2,1)S(1)} %get-tuple-element.28.own_first_ref.refs_0_, bf16[512,128]{1,0:T(8,128)(2,1)S(1)} %get-tuple-element.50.refs_1_, ...), custom_call_target="tpu_custom_call" | custom-call | flops 67108864 | bytes 524288 | tf_op jit(solution)/shard_map/pallas_call | solution.py:439
  20.5 0.3 %collective-permute-done.10.refs_2_ = bf16[2,64,128]{2,1,0:T(8,128)(2,1)S(1)} collective-permute-done((bf16[2,64,128]{2,1,0:T(8,128)(2,1)S(1)}, bf16[2,64,128]{2,1,0:T(8,128)(2,1)S(1)}, u32[]{:S(2)}, u32[]{:S(2)}) %collective-permute-start.10) | collective-permute-done | bytes 32800 | tf_op jit(solution)/shard_map/ppermute | solution.py:149
  20.8 0.9 %collective-permute-done.8.refs_0_ = bf16[2,64,128]{2,1,0:T(8,128)(2,1)S(1)} collective-permute-done((bf16[2,64,128]{2,1,0:T(8,128)(2,1)S(1)}, bf16[2,64,128]{2,1,0:T(8,128)(2,1)S(1)}, u32[]{:S(2)}, u32[]{:S(2)}) %collective-permute-start.8) | collective-permute-done | bytes 32800 | tf_op jit(solution)/shard_map/ppermute | solution.py:149
  21.7 0.5 %collective-permute-done.9.refs_1_ = bf16[2,64,128]{2,1,0:T(8,128)(2,1)S(1)} collective-permute-done((bf16[2,64,128]{2,1,0:T(8,128)(2,1)S(1)}, bf16[2,64,128]{2,1,0:T(8,128)(2,1)S(1)}, u32[]{:S(2)}, u32[]{:S(2)}) %collective-permute-start.9) | collective-permute-done | bytes 32800 | tf_op jit(solution)/shard_map/ppermute | solution.py:149
  22.2 0.7 %shard_map.91 = (f32[9,64,128]{2,1,0:T(8,128)}, f32[9,64,128]{2,1,0:T(8,128)}, bf16[128,512]{1,0:T(8,128)(2,1)}) custom-call(f32[9,64,128]{2,1,0:T(8,128)} %get-tuple-element.26.first_in_ref, f32[9,64,128]{2,1,0:T(8,128)} %get-tuple-element.27.second_in_ref, ...), custom_call_target="tpu_custom_call", output_to_operand_aliasing={{0}: (0, {}), {1}: (1, {})} | custom-call | tf_op jit(solution)/shard_map/pallas_call | solution.py:446
  (14 shorter events, 0.0 us)
Async XLA Ops:
  0.6 1.1 %copy-start.2 = (s32[16]{0:T(128)S(1)}, s32[16]{0:T(128)}, u32[]{:S(2)}) copy-start(s32[16]{0:T(128)} %param.8) | copy-start | bytes 196
  0.6 1.1 %copy-start.3 = (s32[128]{0:T(128)S(1)}, s32[128]{0:T(128)}, u32[]{:S(2)}) copy-start(s32[128]{0:T(128)} %param.7) | copy-start | bytes 1540
  0.7 1.1 %copy-start = (bf16[128,512]{1,0:T(8,128)(2,1)S(1)}, bf16[128,512]{1,0:T(8,128)(2,1)}, u32[]{:S(2)}) copy-start(bf16[128,512]{1,0:T(8,128)(2,1)} %own_ref.1) | copy-start | bytes 393220
  0.7 12.6 %copy-start.1 = (bf16[512,5]{0,1:T(8,128)(2,1)S(1)}, bf16[512,5]{0,1:T(8,128)(2,1)}, u32[]{:S(2)}) copy-start(bf16[512,5]{0,1:T(8,128)(2,1)} %param.11) | copy-start | bytes 15364
  1.9 10.5 %collective-permute-start.3 = (bf16[2,512,128]{2,1,0:T(8,128)(2,1)S(1)}, bf16[2,512,128]{2,1,0:T(8,128)(2,1)S(1)}, u32[]{:S(2)}, u32[]{:S(2)}) collective-permute-start(bf16[2,512,128]{2,1,0:T(8,128)(2,1)S(1)} %get-tuple-element.33), channel_id=1, source_target_pairs={{0,1},{1,0},{2,3},{3,2},{4,5},{5,4},{6,7},{7,6},{8,9},{9,8},{10,11... | collective-permute-start | bytes 786440 | tf_op jit(solution)/shard_map/ppermute | solution.py:149
  2.4 9.4 %collective-permute-start.4 = (bf16[512,128]{1,0:T(8,128)(2,1)S(1)}, bf16[512,128]{1,0:T(8,128)(2,1)S(1)}, u32[]{:S(2)}, u32[]{:S(2)}) collective-permute-start(bf16[512,128]{1,0:T(8,128)(2,1)S(1)} %get-tuple-element.28.own_first_ref.refs_0_), channel_id=1, source_target_pairs={{0,2},{1,3},{2,0},{3,1},{4,6},{5,7},{6,4},{7,5},{8,10},{9,11},{10,... | collective-permute-start | bytes 393224 | tf_op jit(solution)/shard_map/ppermute | solution.py:149
  5.0 7.3 %collective-permute-start.6 = (bf16[512,128]{1,0:T(8,128)(2,1)S(1)}, bf16[512,128]{1,0:T(8,128)(2,1)S(1)}, u32[]{:S(2)}, u32[]{:S(2)}) collective-permute-start(bf16[512,128]{1,0:T(8,128)(2,1)S(1)} %get-tuple-element.29.own_second_ref.refs_0_), channel_id=1, source_target_pairs={{0,2},{1,3},{2,0},{3,1},{4,6},{5,7},{6,4},{7,5},{8,10},{9,11},{10,... | collective-permute-start | bytes 393224 | tf_op jit(solution)/shard_map/ppermute | solution.py:149
  5.0 6.7 %collective-permute-start.1 = (bf16[64,512]{1,0:T(8,128)(2,1)S(1)}, bf16[64,512]{1,0:T(8,128)(2,1)S(1)}, u32[]{:S(2)}, u32[]{:S(2)}) collective-permute-start(bf16[64,512]{1,0:T(8,128)(2,1)S(1)} %get-tuple-element.32), channel_id=1, source_target_pairs={{0,16},{4,20},{8,24},{12,28},{16,0},{20,4},{24,8},{28,12},{1,17},{... | collective-permute-start | bytes 196616 | tf_op jit(solution)/shard_map/ppermute | solution.py:149
  8.1 5.9 %collective-permute-start = (bf16[16,128]{1,0:T(8,128)(2,1)S(1)}, bf16[16,128]{1,0:T(8,128)(2,1)S(1)}, u32[]{:S(2)}, u32[]{:S(2)}) collective-permute-start(bf16[16,128]{1,0:T(8,128)(2,1)S(1)} %get-tuple-element.31), channel_id=1, source_target_pairs={{0,16},{4,20},{8,24},{12,28},{16,0},{20,4},{24,8},{28,12},{1,17},{... | collective-permute-start | bytes 12296 | tf_op jit(solution)/shard_map/ppermute | solution.py:149
  11.8 1.3 %collective-permute-start.2 = (bf16[64,512]{1,0:T(8,128)(2,1)S(1)}, bf16[64,512]{1,0:T(8,128)(2,1)S(1)}, u32[]{:S(2)}, u32[]{:S(2)}) collective-permute-start(bf16[64,512]{1,0:T(8,128)(2,1)S(1)} %collective-permute-done.1.far_ref), channel_id=1, source_target_pairs={{0,1},{1,0},{2,3},{3,2},{4,5},{5,4},{6,7},{7,6},{8,9},{9,8},{10,11... | collective-permute-start | bytes 196616 | tf_op jit(solution)/shard_map/ppermute | solution.py:149
  11.8 1.5 %collective-permute-start.5 = (bf16[512,128]{1,0:T(8,128)(2,1)S(1)}, bf16[512,128]{1,0:T(8,128)(2,1)S(1)}, u32[]{:S(2)}, u32[]{:S(2)}) collective-permute-start(bf16[512,128]{1,0:T(8,128)(2,1)S(1)} %collective-permute-done.4.refs_2_), channel_id=1, source_target_pairs={{0,1},{1,0},{2,3},{3,2},{4,5},{5,4},{6,7},{7,6},{8,9},{9,8},{10,11... | collective-permute-start | bytes 393224 | tf_op jit(solution)/shard_map/ppermute | solution.py:149
  12.3 1.7 %collective-permute-start.7 = (bf16[512,128]{1,0:T(8,128)(2,1)S(1)}, bf16[512,128]{1,0:T(8,128)(2,1)S(1)}, u32[]{:S(2)}, u32[]{:S(2)}) collective-permute-start(bf16[512,128]{1,0:T(8,128)(2,1)S(1)} %collective-permute-done.6.refs_2_), channel_id=1, source_target_pairs={{0,1},{1,0},{2,3},{3,2},{4,5},{5,4},{6,7},{7,6},{8,9},{9,8},{10,11... | collective-permute-start | bytes 393224 | tf_op jit(solution)/shard_map/ppermute | solution.py:149
  15.8 5.0 %collective-permute-start.10 = (bf16[2,64,128]{2,1,0:T(8,128)(2,1)S(1)}, bf16[2,64,128]{2,1,0:T(8,128)(2,1)S(1)}, u32[]{:S(2)}, u32[]{:S(2)}) collective-permute-start(bf16[2,64,128]{2,1,0:T(8,128)(2,1)S(1)} %get-tuple-element.45), channel_id=1, source_target_pairs={{0,12},{4,8},{8,4},{12,0},{16,28},{20,24},{24,20},{28,16},{1,13},{... | collective-permute-start | bytes 98312 | tf_op jit(solution)/shard_map/ppermute | solution.py:149
  17.8 3.9 %collective-permute-start.8 = (bf16[2,64,128]{2,1,0:T(8,128)(2,1)S(1)}, bf16[2,64,128]{2,1,0:T(8,128)(2,1)S(1)}, u32[]{:S(2)}, u32[]{:S(2)}) collective-permute-start(bf16[2,64,128]{2,1,0:T(8,128)(2,1)S(1)} %get-tuple-element.43), channel_id=1, source_target_pairs={{0,4},{4,0},{8,12},{12,8},{16,20},{20,16},{24,28},{28,24},{1,5},{5... | collective-permute-start | bytes 98312 | tf_op jit(solution)/shard_map/ppermute | solution.py:149
  18.3 3.9 %collective-permute-start.9 = (bf16[2,64,128]{2,1,0:T(8,128)(2,1)S(1)}, bf16[2,64,128]{2,1,0:T(8,128)(2,1)S(1)}, u32[]{:S(2)}, u32[]{:S(2)}) collective-permute-start(bf16[2,64,128]{2,1,0:T(8,128)(2,1)S(1)} %get-tuple-element.44), channel_id=1, source_target_pairs={{0,8},{4,12},{8,0},{12,4},{16,24},{20,28},{24,16},{28,20},{1,9},{5... | collective-permute-start | bytes 98312 | tf_op jit(solution)/shard_map/ppermute | solution.py:149
